TPU v7x, 256 devices: a whole 4x4x8 slice. The times are simulated.
256 devices in a mesh: segment: 8 (over z_lo, core), dp: 32 (over x, y, z_hi).
Axes of the slice: x: 4, y: 4, z: 8 (z_hi: 2, z_lo: 4; z = z_hi * 4 + z_lo), core: 2. Of those that a mesh axis runs over, the one named last changes fastest.
Arguments:
- layer_inputs: bfloat16 [8, 8192, 6144], P('segment', 'dp'), may hold values from -6 to 6
- resid_grad: bfloat16 [8, 8192, 6144], P('segment', 'dp'), may hold values from -3 to 3
- key_grad: bfloat16 [8, 8192, 512], P('segment', 'dp'), may hold values from -4 to 4
- key_weight: bfloat16 [8, 6144, 512], P('segment', 'dp'), may hold values from -0.125 to 0.125
- fim_bounds: int32 [8, 2], P('segment'), may hold values from 1 to 4095
- slot_block: int32 [8, 32], P('segment'), may hold values from 0 to 31, each once within a row
- inv_input: float32 [8, 32, 192, 192], P('segment', 'dp'), may hold values from -1.5 to 10.8, as said below
- inv_head: float32 [8, 4, 128, 128], P('segment'), may hold values from -1.5 to 10.8, as said below
Outputs:
- passed: bfloat16 [8, 8192, 6144], P('segment', 'dp')
- precond: float32 [8, 32, 192, 512], P('segment', 'dp')
- input_grams: float32 [8, 32, 192, 192], P('segment', 'dp')
- head_grams: float32 [8, 4, 128, 128], P('segment')
Inputs may be any that keep to these rules, and one draw needn't show every extreme that they name: `slot_block`: each section's row names every block once. `inv_input`: symmetric. `inv_head`: symmetric.
All inputs are finite; a program needn't handle non-finite values.
Results may differ from a plain program's by a relative error of at most 0.0039.
Values may be sent and summed in bfloat16 or wider, within the bound.
No kernel may reach another device: no remote copies, remote signals or barrier semaphores. Data moves between devices by JAX's collectives and lax.ppermute only.
A program may use at most 128 MiB of HBM per device.

v0:
```python
import jax
import jax.numpy as jnp
from jax import lax
from jax.sharding import PartitionSpec as P

rope_base = 100000.0


def passed_along(block, axis, distance):
    devices = range(lax.axis_size(axis))
    route = [(i - distance, i) for i in devices if i - distance in devices]
    return lax.ppermute(block, axis, route)


def fim_positions(token_index, bounds, total):
    prefix_len = bounds[0]
    suffix_len = bounds[1]
    middle_len = total - prefix_len - suffix_len
    return jnp.where(
        token_index < prefix_len,
        token_index,
        jnp.where(
            token_index < prefix_len + suffix_len,
            token_index + middle_len,
            token_index - suffix_len,
        ),
    )


def rope_back(grad_rot, token_pos, head_count, head_dim):
    half_dim = head_dim // 2
    frequency = jnp.power(
        jnp.float32(rope_base), -2.0 * jnp.arange(half_dim, dtype=jnp.float32) / head_dim
    )
    angle = token_pos.astype(jnp.float32)[:, None] * frequency[None, :]
    cosines = jnp.cos(angle)[:, None, :]
    sine_part = jnp.sin(angle)[:, None, :]
    heads = grad_rot.astype(jnp.float32).reshape(grad_rot.shape[0], head_count, head_dim)
    first_half = heads[..., :half_dim]
    second_half = heads[..., half_dim:]
    joined = jnp.concatenate(
        [
            first_half * cosines + second_half * sine_part,
            second_half * cosines - first_half * sine_part,
        ],
        axis=-1,
    )
    return joined.reshape(grad_rot.shape[0], head_count * head_dim)


def body(
    layer_inputs, resid_grad, key_grad, key_weight, fim_bounds, slot_block, inv_input, inv_head
):
    inputs_local = layer_inputs[0]
    row_count = inputs_local.shape[0]
    total = row_count * lax.axis_size("dp")
    head_count = inv_head.shape[1]
    head_dim = inv_head.shape[2]
    token_index = lax.axis_index("dp") * row_count + jnp.arange(row_count, dtype=jnp.int32)
    token_pos = fim_positions(token_index, fim_bounds[0], total)
    key_pre = rope_back(key_grad[0], token_pos, head_count, head_dim).astype(jnp.bfloat16)
    key_out = key_pre.shape[1]
    branch = lax.dot_general(
        key_pre,
        lax.all_gather(key_weight[0], "dp", axis=0, tiled=True),
        (((1,), (1,)), ((), ())),
        preferred_element_type=jnp.float32,
    )
    sent = (resid_grad[0].astype(jnp.float32) + branch).astype(jnp.bfloat16)
    passed = passed_along(sent, "segment", -1)
    key_heads = key_pre.reshape(row_count, head_count, head_dim)
    head_term = jnp.einsum("rhd,rhe->hde", key_heads, key_heads, preferred_element_type=jnp.float32)
    head_grams = lax.psum(head_term, "dp") / total
    owned = inv_input.shape[1]
    block_width = inv_input.shape[2]
    block_total = inputs_local.shape[1] // block_width
    blocked = inputs_local.reshape(row_count, block_total, block_width)
    slot_ids = slot_block[0]

    def slot_columns():
        return jnp.take(blocked, slot_ids, axis=1)

    chosen = slot_columns()
    weight_grad = (
        lax.psum_scatter(
            jnp.einsum("rcb,rk->cbk", chosen, key_pre, preferred_element_type=jnp.float32),
            "dp",
            scatter_dimension=0,
            tiled=True,
        )
        / total
    )
    chosen = slot_columns()
    input_grams = (
        lax.psum_scatter(
            jnp.einsum("rcb,rce->cbe", chosen, chosen, preferred_element_type=jnp.float32),
            "dp",
            scatter_dimension=0,
            tiled=True,
        )
        / total
    )
    left_side = jnp.einsum(
        "cab,cbk->cak", inv_input[0], weight_grad, precision=lax.Precision.HIGHEST
    )
    both_sides = jnp.einsum(
        "cahd,hde->cahe",
        left_side.reshape(owned, block_width, head_count, head_dim),
        inv_head[0],
        precision=lax.Precision.HIGHEST,
    )
    precond = both_sides.reshape(owned, block_width, key_out)
    return (passed[None], precond[None], input_grams[None], head_grams[None])


def solution(mesh):
    return jax.shard_map(
        body,
        mesh=mesh,
        in_specs=(
            P("segment", "dp", None),
            P("segment", "dp", None),
            P("segment", "dp", None),
            P("segment", "dp", None),
            P("segment", None),
            P("segment", None),
            P("segment", "dp", None, None),
            P("segment", None, None, None),
        ),
        out_specs=(
            P("segment", "dp", None),
            P("segment", "dp", None, None),
            P("segment", "dp", None, None),
            P("segment", None, None, None),
        ),
        check_vma=False,
    )
```

profile of v0, /device:TPU:96, one launch (start us, length us, event | category | flops | bytes accessed | tf_op | source)
XLA Modules:
  0.0 1162.4 jit_solution(15779966716798476548)
XLA Ops:
  7.2 0.0 copy-start
  7.2 0.0 all-gather.3.cloned.1.call-start
  7.2 0.7 all-gather.3.cloned.1.call-update
  7.9 0.0 all-reduce.2.cloned.1.call-start
  8.0 1.4 fusion.16
  11.9 1.8 copy.14
  13.7 1.9 fusion.15
  15.6 1.9 copy.24
  17.6 1.9 copy.25
  19.5 1.3 fusion.12
  20.8 0.5 multiply_cosine_fusion
  21.4 1.3 multiply_add_fusion
  22.7 0.0 copy-start.4
  22.7 0.0 copy-start.5
  22.8 0.7 copy-done.4
  23.4 0.1 maximum_convert_fusion
  23.6 0.0 copy-done.5
  23.6 0.0 copy-start.1
  23.6 0.7 copy-done.1
  24.3 1.0 fusion.17
  25.3 0.0 all-reduce.2.cloned.1.call-update
  25.3 0.0 reduce-scatter.5.cloned.1.call-start
  25.4 0.0 copy-done.6
  25.4 0.0 copy-done.2
  25.4 2.8 copy.18
  28.2 2.6 gather_fusion
  30.8 3.7 fusion.2
  34.5 0.0 reduce-scatter.5.cloned.1.call-update
  34.6 0.0 reduce-scatter.3.cloned.1.call-start
  34.6 1.9 copy.17
  36.5 1.8 reshape.124
  38.2 7.3 fusion.4
  45.6 0.0 reduce-scatter.3.cloned.1.call-update
  45.6 94.7 %all-gather.3.cloned.1.call-done = bf16[1,6144,512]{2,1,0:T(8,128)(2,1)} async-done(((bf16[1,192,512]{2,1,0:T(8,128)(2,1)}), bf16[1,6144,512]{2,1,0:T(8,128)(2,1)}) %all-gather.3.cloned.1.call-update) | async-done | bytes 6291472 | tf_op jit(solution)/shard_map/all_gather | solution.py:65
  140.2 0.0 copy-done.3
  140.2 6.5 fusion
  146.7 3.8 collective-permute-start
  150.5 414.5 %all-reduce.2.cloned.1.call-done = f32[4,128,128]{2,1,0:T(8,128)} async-done(((f32[4,128,128]{2,1,0:T(8,128)}), f32[4,128,128]{2,1,0:T(8,128)}) %all-reduce.2.cloned.1.call-update) | async-done | bytes 262160 | tf_op jit(solution)/shard_map/psum | solution.py:73
  565.0 1.7 multiply_bitcast_fusion.1
  566.7 272.8 %reduce-scatter.5.cloned.1.call-done = f32[1,192,192]{2,1,0:T(8,128)} async-done(((f32[32,192,192]{2,1,0:T(8,128)}), f32[1,192,192]{2,1,0:T(8,128)}) %reduce-scatter.5.cloned.1.call-update) | async-done | bytes 147472 | tf_op jit(solution)/shard_map/reduce_scatter | solution.py:95
  839.5 1.6 multiply_bitcast_fusion.2
  841.1 0.0 collective-permute-done
  841.1 310.0 %reduce-scatter.3.cloned.1.call-done = f32[1,192,512]{2,1,0:T(8,128)} async-done(((f32[32,192,512]{2,1,0:T(8,128)}), f32[1,192,512]{2,1,0:T(8,128)}) %reduce-scatter.3.cloned.1.call-update) | async-done | bytes 393232 | tf_op jit(solution)/shard_map/reduce_scatter | solution.py:85
  1151.1 1.6 convolution_bitcast_fusion.1
  1152.7 0.5 convolution_bitcast_fusion
  1153.2 0.3 copy.19
  1153.5 0.8 copy.21
  1154.2 1.7 copy.38
  (8 shorter events, 0.0 us)
Async XLA Ops:
  7.2 1145.5 %copy-start = (f32[1,4,128,128]{3,2,1,0:T(8,128)S(1)}, f32[1,4,128,128]{3,2,1,0:T(8,128)}, u32[]{:S(2)}) copy-start(f32[1,4,128,128]{3,2,1,0:T(8,128)} %param.17) | copy-start | bytes 786436
  7.2 133.1 %all-gather.3.cloned.1.call-start = ((), (), s32[]{:S(2)}) async-start(), calls=%async_computation.5 | async-start | bytes 6488064 | tf_op jit(solution)/shard_map/all_gather | solution.py:65
  7.9 557.1 %all-reduce.2.cloned.1.call-start = ((), (), s32[]{:S(2)}) async-start(), calls=%async_computation.4 | async-start | bytes 524288 | tf_op jit(solution)/shard_map/psum | solution.py:73
  13.7 11.7 %copy-start.6 = (s32[1,32]{1,0:T(1,128)S(1)}, s32[1,32]{1,0:T(1,128)}, u32[]{:S(2)}) copy-start(s32[1,32]{1,0:T(1,128)} %param.15) | copy-start | bytes 388
  13.7 11.7 %copy-start.2 = (bf16[1,256,6144]{2,1,0:T(8,128)(2,1)S(1)}, bf16[1,256,6144]{2,1,0:T(8,128)(2,1)}, u32[]{:S(2)}) copy-start(bf16[1,256,6144]{2,1,0:T(8,128)(2,1)} %param.10) | copy-start | bytes 9437188
  22.7 0.7 copy-start.4
  22.7 0.8 copy-start.5
  23.6 0.7 copy-start.1
  25.3 814.1 %reduce-scatter.5.cloned.1.call-start = ((), (), s32[]{:S(2)}) async-start(), calls=%async_computation.3 | async-start | bytes 6488064 | tf_op jit(solution)/shard_map/reduce_scatter | solution.py:95
  34.6 1116.5 %reduce-scatter.3.cloned.1.call-start = ((), (), s32[]{:S(2)}) async-start(), calls=%async_computation.2 | async-start | bytes 12976128 | tf_op jit(solution)/shard_map/reduce_scatter | solution.py:85
  45.6 94.7 %copy-start.3 = (bf16[1,256,6144]{2,1,0:T(8,128)(2,1)S(1)}, bf16[1,256,6144]{2,1,0:T(8,128)(2,1)}, u32[]{:S(2)}) copy-start(bf16[1,256,6144]{2,1,0:T(8,128)(2,1)} %param.11) | copy-start | bytes 9437188
  146.7 694.3 %collective-permute-start = (bf16[256,6144]{1,0:T(8,128)(2,1)}, bf16[256,6144]{1,0:T(8,128)(2,1)S(1)}, u32[]{:S(2)}, u32[]{:S(2)}) collective-permute-start(bf16[256,6144]{1,0:T(8,128)(2,1)} %fusion), channel_id=1, source_target_pairs={{32,0},{64,32},{96,64},{128,96},{160,128},{192,160},{224,192},{33,... | collective-permute-start | bytes 9437192 | tf_op jit(solution)/shard_map/ppermute | solution.py:12
Sparse Core Ops, SparseCore 0:
  11.4 128.7 all-gather.2
  142.8 422.1 all-reduce.1
  571.5 267.9 reduce-scatter.4
  846.0 305.0 reduce-scatter.2
where the time goes:
time: 1170 us; the launch traced here: 1160 us
  waiting for transfers between devices  1090 us (93%)
  local copies, waits for them, and re-layouts  22.1 us (2%)
  matrix products  20.6 us (2%)
  between operations  16.5 us (1%)
    psum x1, waiting for transfers between devices, body(): head_grams = lax.psum(head_term, 'dp') / total  414 us
    reduce_scatter x1, waiting for transfers between devices, body(): lax.psum_scatter(jnp.einsum('rcb,rk->cbk', chosen, key_pre, preferred_ele...  310 us
    reduce_scatter x1, waiting for transfers between devices, body(): lax.psum_scatter(jnp.einsum('rcb,rce->cbe', chosen, chosen, preferred_ele...  273 us
    all_gather x1, waiting for transfers between devices, body(): lax.all_gather(key_weight[0], 'dp', axis=0, tiled=True)  94.7 us
  transfers between devices with their start and end apart: 5, of which 4 were waited for; matrix products, arithmetic and copies ran while one was open for 4% of the time, Pallas kernels for 0%

commit v1 on v0

v1 whole, which is shorter than its diff:
```python
import jax
import jax.numpy as jnp
from jax import lax
from jax.experimental import pallas as pl
from jax.experimental.pallas import tpu as pltpu
from jax.sharding import PartitionSpec as P

rope_base = 100000.0
AXES = ("segment", "dp")
SECTIONS = 8
NX, NY, NZ = 4, 4, 2
DP = NX * NY * NZ
BLK = 192
HALF = BLK // 2
PAIR = 2 * BLK
KO = 512
HD = 128
KVH = 4
PACK = KO + 128

Z, YA, YB, XA, XB = 0, 1, 2, 3, 4
ORDERS = (
    ((XA, XB, YA, YB), (XB, XA, YB, YA)),
    ((YA, YB, XA, XB), (YB, YA, XB, XA)),
)


def gray(i):
    return i ^ (i >> 1)


def place_bits(dp):
    return (gray(dp >> 3) << 3) | (gray((dp >> 1) & 3) << 1) | (dp & 1)


def flipped(dp, dim):
    x, y, z = dp >> 3, (dp >> 1) & 3, dp & 1
    if dim == XA:
        x ^= 1
    elif dim == XB:
        x = 3 - x
    elif dim == YA:
        y ^= 1
    elif dim == YB:
        y = 3 - y
    else:
        z ^= 1
    return (x * NY + y) * NZ + z


def swap_route(stream, step):
    route = []
    for seg in range(SECTIONS):
        dim = Z if step == 4 else ORDERS[seg % 2][stream][step]
        for dp in range(DP):
            route.append((seg * DP + dp, seg * DP + flipped(dp, dim)))
    return route


def back_route(cross):
    route = []
    for seg in range(1, SECTIONS):
        for dp in range(DP):
            target = flipped(dp, Z) if cross else dp
            route.append((seg * DP + dp, (seg - 1) * DP + target))
    return route


def bit(v, i):
    return (v >> i) & 1


def stream_place(rel, core, stream, weights):
    even, odd = ORDERS[0][stream], ORDERS[1][stream]
    on_even = sum(bit(rel, d) * w for d, w in zip(even, weights))
    on_odd = sum(bit(rel, d) * w for d, w in zip(odd, weights))
    return jnp.where(core == 0, on_even, on_odd)


def fim_positions(token_index, bounds, total):
    prefix_len = bounds[0]
    suffix_len = bounds[1]
    middle_len = total - prefix_len - suffix_len
    return jnp.where(
        token_index < prefix_len,
        token_index,
        jnp.where(
            token_index < prefix_len + suffix_len,
            token_index + middle_len,
            token_index - suffix_len,
        ),
    )


def rope_back(grad_rot, token_pos, head_count, head_dim):
    half_dim = head_dim // 2
    frequency = jnp.power(
        jnp.float32(rope_base), -2.0 * jnp.arange(half_dim, dtype=jnp.float32) / head_dim
    )
    angle = token_pos.astype(jnp.float32)[:, None] * frequency[None, :]
    cosines = jnp.cos(angle)
    sines = jnp.sin(angle)
    cos_wide = jnp.tile(cosines, (1, 2 * head_count))
    sin_wide = jnp.tile(jnp.concatenate([sines, -sines], axis=1), (1, head_count))
    grad = grad_rot.astype(jnp.float32)
    rows = grad.shape[0]
    heads = grad.reshape(rows, head_count, 2, half_dim)
    swapped = jnp.concatenate([heads[:, :, 1:], heads[:, :, :1]], axis=2).reshape(grad.shape)
    return grad * cos_wide + swapped * sin_wide


def dot_rows(a, b):
    return lax.dot_general(a, b, (((0,), (0,)), ((), ())), preferred_element_type=jnp.float32)


def products_kernel(slot_ref, x_ref, k_ref, send_a, keep_a, send_b, keep_b, head_ref, place):
    core = lax.axis_index("segment") & 1
    me = place_bits(lax.axis_index("dp"))
    for j in range(DP):
        rel = me ^ place_bits(j)
        block = slot_ref[j]
        for stream in range(2):
            place[stream, block] = stream_place(rel, core, stream, (16, 8, 4, 2)) + bit(rel, Z)
    keys = k_ref[...]
    for h in range(KVH):
        head = keys[:, h * HD : (h + 1) * HD]
        head_ref[h] = dot_rows(head, head)
    half = DP // 2

    def put(stream, send, keep, block, wide, narrow):
        at = place[stream, block]

        @pl.when(at >= half)
        def _():
            send[at - half, :, :KO] = wide.astype(jnp.bfloat16)
            send[at - half, :, KO:] = narrow.astype(jnp.bfloat16)

        @pl.when(at < half)
        def _():
            keep[at, :, :KO] = wide
            keep[at, :, KO:] = narrow

    def pair(q, _):
        cols = x_ref[:, pl.ds(pl.multiple_of(q * PAIR, 128), PAIR)]
        for e in range(2):
            own = cols[:, e * BLK : (e + 1) * BLK]
            wide = dot_rows(own, keys)
            gram = dot_rows(own, own)
            top = jnp.concatenate([gram[:64, :64], gram[128:, 128:]], axis=1)
            narrow = jnp.concatenate([top, gram[64:, :128]], axis=0)
            put(0, send_a, keep_a, 2 * q + e, wide[:HALF], narrow[:HALF])
            put(1, send_b, keep_b, 2 * q + e, wide[HALF:], narrow[HALF:])
        return 0

    lax.fori_loop(0, DP // 2, pair, 0)


def section_products(slots, inputs_local, key_pre):
    half = DP // 2
    send = jax.ShapeDtypeStruct((half, HALF, PACK), jnp.bfloat16)
    keep = jax.ShapeDtypeStruct((half, HALF, PACK), jnp.float32)
    vmem = pl.BlockSpec(memory_space=pltpu.VMEM)
    return pl.pallas_call(
        products_kernel,
        out_shape=(send, keep, send, keep, jax.ShapeDtypeStruct((KVH, HD, HD), jnp.float32)),
        in_specs=[pl.BlockSpec(memory_space=pltpu.SMEM), vmem, vmem],
        out_specs=(vmem,) * 5,
        scratch_shapes=[pltpu.SMEM((2, DP), jnp.int32)],
        compiler_params=pltpu.CompilerParams(vmem_limit_bytes=40 * 2**20),
        cost_estimate=pl.CostEstimate(
            flops=2 * 256 * 6144 * 704, bytes_accessed=20 * 2**20, transcendentals=0
        ),
        name="section_products",
    )(slots, inputs_local, key_pre)


def finish_kernel(total, keep_a, got_a, keep_b, got_b, inv_in, inv_out, precond_ref, gram_ref, left):
    scale = jnp.float32(1.0 / total)
    sum_a = (keep_a[0] + got_a[0].astype(jnp.float32)) * scale
    sum_b = (keep_b[0] + got_b[0].astype(jnp.float32)) * scale
    left[...] = jnp.concatenate([sum_a[:, :KO], sum_b[:, :KO]], axis=0)
    packed = jnp.concatenate([sum_a[:, KO:], sum_b[:, KO:]], axis=0)
    low = packed[64:]
    turned = low.T
    gram_ref[:64] = jnp.concatenate([packed[:64, :64], turned[:64]], axis=1)
    gram_ref[64:128] = jnp.concatenate([low[:64], turned[64:, 64:]], axis=1)
    gram_ref[128:] = jnp.concatenate([low[64:], packed[:64, 64:]], axis=1)
    left[...] = jnp.dot(
        inv_in[0],
        left[...],
        precision=lax.Precision.HIGHEST,
        preferred_element_type=jnp.float32,
    )
    for h in range(KVH):
        cols = slice(h * HD, (h + 1) * HD)
        precond_ref[0, :, cols] = jnp.dot(
            left[:, cols],
            inv_out[h],
            precision=lax.Precision.HIGHEST,
            preferred_element_type=jnp.float32,
        )


def finished(total, keep_a, got_a, keep_b, got_b, inv_in, inv_out):
    vmem = pl.BlockSpec(memory_space=pltpu.VMEM)

    def kernel(*refs):
        finish_kernel(total, *refs)

    return pl.pallas_call(
        kernel,
        out_shape=(
            jax.ShapeDtypeStruct((1, BLK, KO), jnp.float32),
            jax.ShapeDtypeStruct((BLK, BLK), jnp.float32),
        ),
        in_specs=[vmem] * 6,
        out_specs=(vmem, vmem),
        scratch_shapes=[pltpu.VMEM((BLK, KO), jnp.float32)],
        compiler_params=pltpu.CompilerParams(vmem_limit_bytes=16 * 2**20),
        name="finish",
    )(keep_a, got_a, keep_b, got_b, inv_in, inv_out)


def passed_kernel(held_a, got_a, held_b, got_b, k_ref, resid_ref, out_ref, partial):
    core = lax.axis_index("segment") & 1
    me = place_bits(lax.axis_index("dp"))
    lower = len(ORDERS[0][0])
    inv_gray = gray

    def column(stream, h):
        even, odd = ORDERS[0][stream], ORDERS[1][stream]
        on_even = sum(bit(h, i) << even[i] for i in range(lower))
        on_odd = sum(bit(h, i) << odd[i] for i in range(lower))
        owner = me ^ jnp.where(core == 0, on_even, on_odd)
        x = inv_gray(owner >> 3)
        y = inv_gray((owner >> 1) & 3)
        return pl.ds(pl.multiple_of((x * NY + y) * PAIR, 128), PAIR)

    def times(keys, rows):
        return lax.dot_general(
            keys, rows, (((1,), (1,)), ((), ())), preferred_element_type=jnp.float32
        )

    keys = k_ref[:, : KO // 2]
    for ref, base in ((held_a, 0), (got_a, 8)):

        def first(h, _, ref=ref, base=base):
            partial[:, column(0, h + base)] = times(keys, ref[h])
            return 0

        lax.fori_loop(0, 8, first, 0)
    more_keys = k_ref[:, KO // 2 :]
    for ref, base in ((held_b, 0), (got_b, 8)):

        def second(h, _, ref=ref, base=base):
            cols = column(1, h + base)
            branch = partial[:, cols] + times(more_keys, ref[h])
            out_ref[:, cols] = (resid_ref[:, cols].astype(jnp.float32) + branch).astype(
                jnp.bfloat16
            )
            return 0

        lax.fori_loop(0, 8, second, 0)


def passed_grad(held_a, got_a, held_b, got_b, key_pre, resid):
    vmem = pl.BlockSpec(memory_space=pltpu.VMEM)
    return pl.pallas_call(
        passed_kernel,
        out_shape=jax.ShapeDtypeStruct(resid.shape, jnp.bfloat16),
        in_specs=[vmem] * 6,
        out_specs=vmem,
        scratch_shapes=[pltpu.VMEM(resid.shape, jnp.float32)],
        compiler_params=pltpu.CompilerParams(vmem_limit_bytes=40 * 2**20),
        cost_estimate=pl.CostEstimate(
            flops=2 * 256 * 6144 * 512, bytes_accessed=12 * 2**20, transcendentals=0
        ),
        name="passed_grad",
    )(held_a, got_a, held_b, got_b, key_pre, resid)


def hop(block, route):
    return lax.ppermute(block, AXES, route)


def body(
    layer_inputs, resid_grad, key_grad, key_weight, fim_bounds, slot_block, inv_input, inv_head
):
    inputs_local = layer_inputs[0]
    row_count = inputs_local.shape[0]
    total = row_count * lax.axis_size("dp")
    dp = lax.axis_index("dp")

    straight = hop(key_weight[0], back_route(False))
    crossed = hop(key_weight[0], back_route(True))

    token_index = dp * row_count + jnp.arange(row_count, dtype=jnp.int32)
    token_pos = fim_positions(token_index, fim_bounds[0], total)
    key_pre = rope_back(key_grad[0], token_pos, KVH, HD).astype(jnp.bfloat16)

    send_a, keep_a, send_b, keep_b, head_sum = section_products(
        slot_block[0], inputs_local, key_pre
    )

    even = (dp & 1) == 0
    pair = jnp.concatenate(
        [jnp.where(even, straight, crossed), jnp.where(even, crossed, straight)], axis=0
    )
    held = [pair[None, :, : KO // 2], pair[None, :, KO // 2 :]]

    resid_in, key_in, pair = lax.optimization_barrier((resid_grad[0], key_pre, pair))
    resid = hop(resid_in, back_route(False))
    key_next = hop(key_in, back_route(False))

    sends, keeps = [send_a, send_b], [keep_a, keep_b]
    got = [None, None]
    came = [None, None]
    for step in range(5):
        rounded = lax.reduce_precision(head_sum, 8, 7)
        other = hop(rounded.astype(jnp.bfloat16), swap_route(0, (step + 4) % 5))
        head_sum = rounded + other.astype(jnp.float32)
        for s in range(2):
            if step < 4:
                came[s] = hop(held[s], swap_route(s, step))
                if step < 3:
                    held[s] = jnp.concatenate([held[s], came[s]], axis=0)
        for s in range(2):
            got[s] = hop(sends[s], swap_route(s, step))
            if step < 4:
                summed = keeps[s] + got[s].astype(jnp.float32)
                left = summed.shape[0] // 2
                keeps[s] = summed[:left]
                sends[s] = summed[left:].astype(jnp.bfloat16)

    passed = passed_grad(held[0], came[0], held[1], came[1], key_next, resid)
    precond, gram = finished(
        total, keeps[0], got[0], keeps[1], got[1], inv_input[0], inv_head[0]
    )
    head_grams = head_sum / total
    return (passed[None], precond[None], gram[None, None], head_grams[None])


def solution(mesh):
    return jax.shard_map(
        body,
        mesh=mesh,
        in_specs=(
            P("segment", "dp", None),
            P("segment", "dp", None),
            P("segment", "dp", None),
            P("segment", "dp", None),
            P("segment", None),
            P("segment", None),
            P("segment", "dp", None, None),
            P("segment", None, None, None),
        ),
        out_specs=(
            P("segment", "dp", None),
            P("segment", "dp", None, None),
            P("segment", "dp", None, None),
            P("segment", None, None, None),
        ),
        check_vma=False,
    )
```

time: 1170 us -> 168 us (0.14)
  waiting for transfers between devices: 1090 us -> 73.7 us
  starting transfers between devices: 3.94 us -> 44 us
  Pallas kernels: 0 us -> 29.4 us
  matrix products: 20.6 us -> 0 us
  local copies, waits for them, and re-layouts: 22.1 us -> 6.72 us
  between operations: 16.5 us -> 3.69 us
    reduce_scatter x2 -> x0, waiting for transfers between devices: 583 us -> none  [the longest x1 310 us: body(): lax.psum_scatter(jnp.einsum('rcb,rk->cbk', chosen, key_pre, preferred_ele...]
    psum x1 -> x0, waiting for transfers between devices: 414 us -> none  [body(): head_grams = lax.psum(head_term, 'dp') / total]
    all_gather x1 -> x0, waiting for transfers between devices: 94.7 us -> none  [body(): lax.all_gather(key_weight[0], 'dp', axis=0, tiled=True)]
    ppermute x1 -> x27, waiting for transfers between devices: 0.01 us -> 73.7 us  [hop(): return lax.ppermute(block, AXES, route)]
    ppermute x1 -> x27, starting transfers between devices: 3.78 us -> 44 us  [hop(): return lax.ppermute(block, AXES, route)]
    pallas_call x0 -> x3, Pallas kernels: none -> 29.4 us  [the longest x1 17.7 us: section_products(): pl.pallas_call(products_kernel, out_shape=(send, keep, send, keep, jax.Sh...]
    dot_general x6 -> x0, matrix products: 20.6 us -> none  [the longest x1 7.32 us: body(): jnp.einsum('rcb,rk->cbk', chosen, key_pre, preferred_element_type=jnp.flo...]
  transfers between devices with their start and end apart: 5 -> 27, of which waited for: 4 -> 11; matrix products, arithmetic and copies ran while one was open for 4% -> 4% of each run, Pallas kernels for 0% -> 6%
where the time goes in v1:
time: 168 us; the launch traced here: 166 us
  waiting for transfers between devices  73.7 us (44%)
  starting transfers between devices  44 us (26%)
  Pallas kernels  29.4 us (18%)
  other arithmetic  8.44 us (5%)
  local copies, waits for them, and re-layouts  6.72 us (4%)
  between operations  3.69 us (2%)
    ppermute x27, waiting for transfers between devices, hop(): return lax.ppermute(block, AXES, route)  73.7 us
    ppermute x27, starting transfers between devices, hop(): return lax.ppermute(block, AXES, route)  44 us
    pallas_call x1, Pallas kernels, section_products(): pl.pallas_call(products_kernel, out_shape=(send, keep, send, keep, jax.Sh...  17.7 us
    pallas_call x1, Pallas kernels, passed_grad(): pl.pallas_call(passed_kernel, out_shape=jax.ShapeDtypeStruct(resid.shape,...  9.9 us
    add x8, other arithmetic, body(): summed = keeps[s] + got[s].astype(jnp.float32)  4.96 us
    unnamed x18, local copies, waits for them, and re-layouts  4.17 us
  transfers between devices with their start and end apart: 27, of which 11 were waited for; matrix products, arithmetic and copies ran while one was open for 4% of the time, Pallas kernels for 6%

profile of v1, /device:TPU:96, one launch (start us, length us, event | category | flops | bytes accessed | tf_op | source)
XLA Modules:
  0.0 165.9 jit_solution(3763381140581468978)
XLA Ops:
  0.7 1.3 fusion.13
  4.6 1.3 fusion.10
  5.9 0.3 multiply_cosine_fusion
  6.3 0.2 copy.12
  7.5 1.9 %copy-done.4 = bf16[1,256,6144]{2,1,0:T(8,128)(2,1)S(1)} copy-done((bf16[1,256,6144]{2,1,0:T(8,128)(2,1)S(1)}, bf16[1,256,6144]{2,1,0:T(8,128)(2,1)}, u32[]{:S(2)}) %copy-start.4) | copy-done | bytes 3145752
  9.3 17.7 %section_products.1 = (bf16[16,96,640]{2,1,0:T(8,128)(2,1)S(1)}, f32[16,96,640]{2,1,0:T(8,128)S(1)}, bf16[16,96,640]{2,1,0:T(8,128)(2,1)}, f32[16,96,640]{2,1,0:T(8,128)}, f32[4,128,128]{2,1,0:T(8,128)S(1)}) custom-call(s32[32]{0:T(128)S(1)} %bitcast.34, bf16[256,6144]{1,0:T(8,128)(2,1)S(1)} %bitcast.33, bf16[256,512]{1,0:T(8,128)(2,1)S(1)} %fusion.1.k_ref), custom_call_target="tpu_custom_call" | custom-call | flops 2214592512 | bytes 20971520 | tf_op jit(solution)/shard_map/section_products/pallas_call | solution.py:163
  27.1 1.9 %copy-done = f32[16,96,640]{2,1,0:T(8,128)} copy-done((f32[16,96,640]{2,1,0:T(8,128)}, f32[16,96,640]{2,1,0:T(8,128)S(1)}, u32[]{:S(2)}) %copy-start) | copy-done | bytes 3932184
  29.0 2.8 %collective-permute-start.17 = (bf16[16,96,640]{2,1,0:T(8,128)(2,1)}, bf16[16,96,640]{2,1,0:T(8,128)(2,1)}, u32[]{:S(2)}, u32[]{:S(2)}) collective-permute-start(bf16[16,96,640]{2,1,0:T(8,128)(2,1)} %get-tuple-element.18), channel_id=1, source_target_pairs={{0,24},{1,25},{2,26},{3,27},{4,28},{5,29},{6,30},{7,31},{8,16},{9,... | collective-permute-start | bytes 5898248 | tf_op jit(solution)/shard_map/ppermute | solution.py:283
  31.7 1.9 %collective-permute-start = (bf16[192,512]{1,0:T(8,128)(2,1)S(1)}, bf16[192,512]{1,0:T(8,128)(2,1)S(1)}, u32[]{:S(2)}, u32[]{:S(2)}) collective-permute-start(bf16[192,512]{1,0:T(8,128)(2,1)S(1)} %bitcast.41), channel_id=1, source_target_pairs={{32,0},{33,1},{34,2},{35,3},{36,4},{37,5},{38,6},{39,7},{40,8},{41... | collective-permute-start | bytes 589832 | tf_op jit(solution)/shard_map/ppermute | solution.py:283
  33.6 6.0 %collective-permute-start.1 = (bf16[192,512]{1,0:T(8,128)(2,1)S(1)}, bf16[192,512]{1,0:T(8,128)(2,1)S(1)}, u32[]{:S(2)}, u32[]{:S(2)}) collective-permute-start(bf16[192,512]{1,0:T(8,128)(2,1)S(1)} %bitcast.42), channel_id=1, source_target_pairs={{32,1},{33,0},{34,3},{35,2},{36,5},{37,4},{38,7},{39,6},{40,9},{41... | collective-permute-start | bytes 589832 | tf_op jit(solution)/shard_map/ppermute | solution.py:283
  39.7 0.9 collective-permute-start.22
  40.6 1.5 collective-permute-start.12
  42.1 14.8 %collective-permute-done.1 = bf16[192,512]{1,0:T(8,128)(2,1)S(1)} collective-permute-done((bf16[192,512]{1,0:T(8,128)(2,1)S(1)}, bf16[192,512]{1,0:T(8,128)(2,1)S(1)}, u32[]{:S(2)}, u32[]{:S(2)}) %collective-permute-start.1) | collective-permute-done | bytes 196640 | tf_op jit(solution)/shard_map/ppermute | solution.py:283
  57.0 1.0 collective-permute-start.6
  58.1 0.4 collective-permute-start.23
  58.4 1.7 %collective-permute-start.2 = (bf16[1,384,256]{2,1,0:T(8,128)(2,1)S(1)}, bf16[1,384,256]{2,1,0:T(8,128)(2,1)S(1)}, u32[]{:S(2)}, u32[]{:S(2)}) collective-permute-start(bf16[1,384,256]{2,1,0:T(8,128)(2,1)S(1)} %get-tuple-element.27), channel_id=1, source_target_pairs={{0,8},{1,9},{2,10},{3,11},{4,12},{5,13},{6,14},{7,15},{8,0},{9,1},... | collective-permute-start | bytes 589832 | tf_op jit(solution)/shard_map/ppermute | solution.py:283
  60.2 3.8 %collective-permute-done.6 = bf16[1,384,256]{2,1,0:T(8,128)(2,1)S(1)} collective-permute-done((bf16[1,384,256]{2,1,0:T(8,128)(2,1)S(1)}, bf16[1,384,256]{2,1,0:T(8,128)(2,1)S(1)}, u32[]{:S(2)}, u32[]{:S(2)}) %collective-permute-start.6) | collective-permute-done | bytes 196640 | tf_op jit(solution)/shard_map/ppermute | solution.py:283
  64.1 2.5 %collective-permute-done.23 = bf16[4,128,128]{2,1,0:T(8,128)(2,1)S(1)} collective-permute-done((bf16[4,128,128]{2,1,0:T(8,128)(2,1)S(1)}, bf16[4,128,128]{2,1,0:T(8,128)(2,1)S(1)}, u32[]{:S(2)}, u32[]{:S(2)}) %collective-permute-start.23) | collective-permute-done | bytes 131104 | tf_op jit(solution)/shard_map/ppermute | solution.py:283
  66.7 2.8 %collective-permute-start.24 = (bf16[4,128,128]{2,1,0:T(8,128)(2,1)S(1)}, bf16[4,128,128]{2,1,0:T(8,128)(2,1)S(1)}, u32[]{:S(2)}, u32[]{:S(2)}) collective-permute-start(bf16[4,128,128]{2,1,0:T(8,128)(2,1)S(1)} %fusion.6), channel_id=1, source_target_pairs={{0,24},{1,25},{2,26},{3,27},{4,28},{5,29},{6,30},{7,31},{8,16},{9,... | collective-permute-start | bytes 393224 | tf_op jit(solution)/shard_map/ppermute | solution.py:283
  69.6 2.0 %collective-permute-start.3 = (bf16[2,384,256]{2,1,0:T(8,128)(2,1)S(1)}, bf16[2,384,256]{2,1,0:T(8,128)(2,1)S(1)}, u32[]{:S(2)}, u32[]{:S(2)}) collective-permute-start(bf16[2,384,256]{2,1,0:T(8,128)(2,1)S(1)} %pad_maximum_fusion.6), channel_id=1, source_target_pairs={{0,24},{1,25},{2,26},{3,27},{4,28},{5,29},{6,30},{7,31},{8,16},{9,... | collective-permute-start | bytes 1179656 | tf_op jit(solution)/shard_map/ppermute | solution.py:283
  71.6 1.3 collective-permute-done.24
  73.0 1.9 %collective-permute-start.11 = (bf16[256,6144]{1,0:T(8,128)(2,1)}, bf16[256,6144]{1,0:T(8,128)(2,1)S(1)}, u32[]{:S(2)}, u32[]{:S(2)}) collective-permute-start(bf16[256,6144]{1,0:T(8,128)(2,1)} %bitcast.3), channel_id=1, source_target_pairs={{32,0},{33,1},{34,2},{35,3},{36,4},{37,5},{38,6},{39,7},{40,8},{41... | collective-permute-start | bytes 9437192 | tf_op jit(solution)/shard_map/ppermute | solution.py:283
  75.0 1.4 collective-permute-start.25
  76.5 2.2 %collective-permute-done.3 = bf16[2,384,256]{2,1,0:T(8,128)(2,1)S(1)} collective-permute-done((bf16[2,384,256]{2,1,0:T(8,128)(2,1)S(1)}, bf16[2,384,256]{2,1,0:T(8,128)(2,1)S(1)}, u32[]{:S(2)}, u32[]{:S(2)}) %collective-permute-start.3) | collective-permute-done | bytes 393248 | tf_op jit(solution)/shard_map/ppermute | solution.py:283
  78.7 2.0 %collective-permute-start.8 = (bf16[4,384,256]{2,1,0:T(8,128)(2,1)S(1)}, bf16[4,384,256]{2,1,0:T(8,128)(2,1)S(1)}, u32[]{:S(2)}, u32[]{:S(2)}) collective-permute-start(bf16[4,384,256]{2,1,0:T(8,128)(2,1)S(1)} %pad_maximum_fusion.3), channel_id=1, source_target_pairs={{0,6},{1,7},{2,4},{3,5},{4,2},{5,3},{6,0},{7,1},{8,14},{9,15},{10,... | collective-permute-start | bytes 2359304 | tf_op jit(solution)/shard_map/ppermute | solution.py:283
  80.7 0.2 collective-permute-start.4
  80.9 2.2 %convert_add_fusion = f32[16,96,640]{2,1,0:T(8,128)S(1)} fusion(f32[16,96,640]{2,1,0:T(8,128)S(1)} %copy-done.6, bf16[16,96,640]{2,1,0:T(8,128)(2,1)} %collective-permute-done.17), kind=kLoop, calls=%fused_computation | loop fusion | flops 1966080 | bytes 9830400 | tf_op jit(solution)/shard_map/add | solution.py:330
  83.4 0.2 copy-done.1
  83.6 2.1 %convert_add_fusion.1 = f32[16,96,640]{2,1,0:T(8,128)S(1)} fusion(f32[16,96,640]{2,1,0:T(8,128)S(1)} %copy-done.1, bf16[16,96,640]{2,1,0:T(8,128)(2,1)} %collective-permute-done.12), kind=kLoop, calls=%fused_computation.1 | loop fusion | flops 1966080 | bytes 9830400 | tf_op jit(solution)/shard_map/add | solution.py:330
  85.9 1.4 collective-permute-start.13
  87.3 8.1 %collective-permute-done.8 = bf16[4,384,256]{2,1,0:T(8,128)(2,1)S(1)} collective-permute-done((bf16[4,384,256]{2,1,0:T(8,128)(2,1)S(1)}, bf16[4,384,256]{2,1,0:T(8,128)(2,1)S(1)}, u32[]{:S(2)}, u32[]{:S(2)}) %collective-permute-start.8) | collective-permute-done | bytes 786464 | tf_op jit(solution)/shard_map/ppermute | solution.py:283
  95.4 2.8 %collective-permute-start.26 = (bf16[4,128,128]{2,1,0:T(8,128)(2,1)S(1)}, bf16[4,128,128]{2,1,0:T(8,128)(2,1)S(1)}, u32[]{:S(2)}, u32[]{:S(2)}) collective-permute-start(bf16[4,128,128]{2,1,0:T(8,128)(2,1)S(1)} %fusion.7), channel_id=1, source_target_pairs={{0,6},{1,7},{2,4},{3,5},{4,2},{5,3},{6,0},{7,1},{8,14},{9,15},{10,... | collective-permute-start | bytes 393224 | tf_op jit(solution)/shard_map/ppermute | solution.py:283
  98.3 2.7 %collective-permute-done.4 = bf16[4,384,256]{2,1,0:T(8,128)(2,1)S(1)} collective-permute-done((bf16[4,384,256]{2,1,0:T(8,128)(2,1)S(1)}, bf16[4,384,256]{2,1,0:T(8,128)(2,1)S(1)}, u32[]{:S(2)}, u32[]{:S(2)}) %collective-permute-start.4) | collective-permute-done | bytes 786464 | tf_op jit(solution)/shard_map/ppermute | solution.py:283
  101.2 4.1 %collective-permute-done.18 = bf16[8,96,640]{2,1,0:T(8,128)(2,1)S(1)} collective-permute-done((bf16[8,96,640]{2,1,0:T(8,128)(2,1)S(1)}, bf16[8,96,640]{2,1,0:T(8,128)(2,1)S(1)}, u32[]{:S(2)}, u32[]{:S(2)}) %collective-permute-start.18) | collective-permute-done | bytes 983072 | tf_op jit(solution)/shard_map/ppermute | solution.py:283
  105.3 1.2 collective-permute-start.5
  106.7 2.2 %collective-permute-start.19 = (bf16[4,96,640]{2,1,0:T(8,128)(2,1)S(1)}, bf16[4,96,640]{2,1,0:T(8,128)(2,1)S(1)}, u32[]{:S(2)}, u32[]{:S(2)}) collective-permute-start(bf16[4,96,640]{2,1,0:T(8,128)(2,1)S(1)} %slice.152), channel_id=1, source_target_pairs={{0,6},{1,7},{2,4},{3,5},{4,2},{5,3},{6,0},{7,1},{8,14},{9,15},{10,... | collective-permute-start | bytes 1474568 | tf_op jit(solution)/shard_map/ppermute | solution.py:283
  109.1 0.3 collective-permute-start.14
  109.4 0.8 multiply_bitcast_fusion
  110.2 22.0 %collective-permute-done.19 = bf16[4,96,640]{2,1,0:T(8,128)(2,1)S(1)} collective-permute-done((bf16[4,96,640]{2,1,0:T(8,128)(2,1)S(1)}, bf16[4,96,640]{2,1,0:T(8,128)(2,1)S(1)}, u32[]{:S(2)}, u32[]{:S(2)}) %collective-permute-start.19) | collective-permute-done | bytes 491552 | tf_op jit(solution)/shard_map/ppermute | solution.py:283
  132.2 1.9 %collective-permute-start.10 = (bf16[256,512]{1,0:T(8,128)(2,1)S(1)}, bf16[256,512]{1,0:T(8,128)(2,1)S(1)}, u32[]{:S(2)}, u32[]{:S(2)}) collective-permute-start(bf16[256,512]{1,0:T(8,128)(2,1)S(1)} %fusion.1.k_ref), channel_id=1, source_target_pairs={{32,0},{33,1},{34,2},{35,3},{36,4},{37,5},{38,6},{39,7},{40,8},{41... | collective-permute-start | bytes 786440 | tf_op jit(solution)/shard_map/ppermute | solution.py:283
  134.3 0.3 collective-permute-start.20
  134.7 5.9 %collective-permute-done.20 = bf16[2,96,640]{2,1,0:T(8,128)(2,1)S(1)} collective-permute-done((bf16[2,96,640]{2,1,0:T(8,128)(2,1)S(1)}, bf16[2,96,640]{2,1,0:T(8,128)(2,1)S(1)}, u32[]{:S(2)}, u32[]{:S(2)}) %collective-permute-start.20) | collective-permute-done | bytes 245792 | tf_op jit(solution)/shard_map/ppermute | solution.py:283
  140.6 1.2 collective-permute-start.15
  141.8 6.2 %collective-permute-done.15 = bf16[2,96,640]{2,1,0:T(8,128)(2,1)S(1)} collective-permute-done((bf16[2,96,640]{2,1,0:T(8,128)(2,1)S(1)}, bf16[2,96,640]{2,1,0:T(8,128)(2,1)S(1)}, u32[]{:S(2)}, u32[]{:S(2)}) %collective-permute-start.15) | collective-permute-done | bytes 245792 | tf_op jit(solution)/shard_map/ppermute | solution.py:283
  148.0 5.4 %collective-permute-start.21 = (bf16[1,96,640]{2,1,0:T(8,128)(2,1)S(1)}, bf16[1,96,640]{2,1,0:T(8,128)(2,1)S(1)}, u32[]{:S(2)}, u32[]{:S(2)}) collective-permute-start(bf16[1,96,640]{2,1,0:T(8,128)(2,1)S(1)} %slice.156), channel_id=1, source_target_pairs={{0,1},{1,0},{2,3},{3,2},{4,5},{5,4},{6,7},{7,6},{8,9},{9,8},{10,11... | collective-permute-start | bytes 368648 | tf_op jit(solution)/shard_map/ppermute | solution.py:283
  153.5 0.6 collective-permute-start.16
  154.1 9.9 %passed_grad.1 = bf16[256,6144]{1,0:T(8,128)(2,1)} custom-call(bf16[8,384,256]{2,1,0:T(8,128)(2,1)S(1)} %pad_maximum_fusion.held_a, bf16[8,384,256]{2,1,0:T(8,128)(2,1)S(1)} %collective-permute-done.5.got_a, bf16[8,384,256]{2,1,0:T(8,128)(2,1)S(1)} %pad_maximum_fusion.1.held_b, bf16[8,384,256]{2,1,0:T(8,128)(2,1)S(1)} %collective-permute-done.9.got_b, ...), custom_call_target="tpu_custom_call" | custom-call | flops 1610612736 | bytes 12582912 | tf_op jit(solution)/shard_map/passed_grad/pallas_call | solution.py:268
  164.1 1.8 %finish.1 = (f32[1,192,512]{2,1,0:T(8,128)}, f32[192,192]{1,0:T(8,128)}) custom-call(f32[1,96,640]{2,1,0:T(8,128)S(1)} %slice.110.refs_0_, bf16[1,96,640]{2,1,0:T(8,128)(2,1)S(1)} %collective-permute-done.16.refs_1_, f32[1,96,640]{2,1,0:T(8,128)S(1)} %slice.118.refs_2_, bf16[1,96,640]{2,1,0:T(8,128)(2,1)S(1)} %collective-permute-done.21.refs_3_, ...), custom_call_target="tpu_custom_call" | custom-call | tf_op jit(solution)/shard_map/finish/pallas_call | solution.py:210
  (73 shorter events, 3.2 us)
Async XLA Ops:
  0.6 5.9 %copy-start.7 = (bf16[1,256,512]{2,1,0:T(8,128)(2,1)S(1)}, bf16[1,256,512]{2,1,0:T(8,128)(2,1)}, u32[]{:S(2)}) copy-start(bf16[1,256,512]{2,1,0:T(8,128)(2,1)} %param.10) | copy-start | bytes 786436
  6.8 0.7 copy-start.5
  7.5 1.9 %copy-start.4 = (bf16[1,256,6144]{2,1,0:T(8,128)(2,1)S(1)}, bf16[1,256,6144]{2,1,0:T(8,128)(2,1)}, u32[]{:S(2)}) copy-start(bf16[1,256,6144]{2,1,0:T(8,128)(2,1)} %param.8) | copy-start | bytes 9437188
  9.3 22.4 %copy-start.8 = (bf16[1,192,512]{2,1,0:T(8,128)(2,1)S(1)}, bf16[1,192,512]{2,1,0:T(8,128)(2,1)}, u32[]{:S(2)}) copy-start(bf16[1,192,512]{2,1,0:T(8,128)(2,1)} %param.11) | copy-start | bytes 589828
  27.1 1.9 %copy-start = (f32[16,96,640]{2,1,0:T(8,128)}, f32[16,96,640]{2,1,0:T(8,128)S(1)}, u32[]{:S(2)}) copy-start(f32[16,96,640]{2,1,0:T(8,128)S(1)} %get-tuple-element.15) | copy-start | bytes 11796484
  29.0 51.7 %collective-permute-start.17 = (bf16[16,96,640]{2,1,0:T(8,128)(2,1)}, bf16[16,96,640]{2,1,0:T(8,128)(2,1)}, u32[]{:S(2)}, u32[]{:S(2)}) collective-permute-start(bf16[16,96,640]{2,1,0:T(8,128)(2,1)} %get-tuple-element.18), channel_id=1, source_target_pairs={{0,24},{1,25},{2,26},{3,27},{4,28},{5,29},{6,30},{7,31},{8,16},{9,... | collective-permute-start | bytes 5898248 | tf_op jit(solution)/shard_map/ppermute | solution.py:283
  31.7 10.4 %collective-permute-start = (bf16[192,512]{1,0:T(8,128)(2,1)S(1)}, bf16[192,512]{1,0:T(8,128)(2,1)S(1)}, u32[]{:S(2)}, u32[]{:S(2)}) collective-permute-start(bf16[192,512]{1,0:T(8,128)(2,1)S(1)} %bitcast.41), channel_id=1, source_target_pairs={{32,0},{33,1},{34,2},{35,3},{36,4},{37,5},{38,6},{39,7},{40,8},{41... | collective-permute-start | bytes 589832 | tf_op jit(solution)/shard_map/ppermute | solution.py:283
  33.6 23.3 %collective-permute-start.1 = (bf16[192,512]{1,0:T(8,128)(2,1)S(1)}, bf16[192,512]{1,0:T(8,128)(2,1)S(1)}, u32[]{:S(2)}, u32[]{:S(2)}) collective-permute-start(bf16[192,512]{1,0:T(8,128)(2,1)S(1)} %bitcast.42), channel_id=1, source_target_pairs={{32,1},{33,0},{34,3},{35,2},{36,5},{37,4},{38,7},{39,6},{40,9},{41... | collective-permute-start | bytes 589832 | tf_op jit(solution)/shard_map/ppermute | solution.py:283
  39.7 18.3 %collective-permute-start.22 = (bf16[4,128,128]{2,1,0:T(8,128)(2,1)S(1)}, bf16[4,128,128]{2,1,0:T(8,128)(2,1)S(1)}, u32[]{:S(2)}, u32[]{:S(2)}) collective-permute-start(bf16[4,128,128]{2,1,0:T(8,128)(2,1)S(1)} %reduce-precision_convert_fusion), channel_id=1, source_target_pairs={{0,1},{1,0},{2,3},{3,2},{4,5},{5,4},{6,7},{7,6},{8,9},{9,8},{10,11... | collective-permute-start | bytes 393224 | tf_op jit(solution)/shard_map/ppermute | solution.py:283
  40.6 42.7 %collective-permute-start.12 = (bf16[16,96,640]{2,1,0:T(8,128)(2,1)S(1)}, bf16[16,96,640]{2,1,0:T(8,128)(2,1)}, u32[]{:S(2)}, u32[]{:S(2)}) collective-permute-start(bf16[16,96,640]{2,1,0:T(8,128)(2,1)S(1)} %get-tuple-element.16), channel_id=1, source_target_pairs={{0,8},{1,9},{2,10},{3,11},{4,12},{5,13},{6,14},{7,15},{8,0},{9,1},... | collective-permute-start | bytes 5898248 | tf_op jit(solution)/shard_map/ppermute | solution.py:283
  57.0 7.0 %collective-permute-start.6 = (bf16[1,384,256]{2,1,0:T(8,128)(2,1)S(1)}, bf16[1,384,256]{2,1,0:T(8,128)(2,1)S(1)}, u32[]{:S(2)}, u32[]{:S(2)}) collective-permute-start(bf16[1,384,256]{2,1,0:T(8,128)(2,1)S(1)} %get-tuple-element.26), channel_id=1, source_target_pairs={{0,24},{1,25},{2,26},{3,27},{4,28},{5,29},{6,30},{7,31},{8,16},{9,... | collective-permute-start | bytes 589832 | tf_op jit(solution)/shard_map/ppermute | solution.py:283
  58.1 8.6 %collective-permute-start.23 = (bf16[4,128,128]{2,1,0:T(8,128)(2,1)S(1)}, bf16[4,128,128]{2,1,0:T(8,128)(2,1)S(1)}, u32[]{:S(2)}, u32[]{:S(2)}) collective-permute-start(bf16[4,128,128]{2,1,0:T(8,128)(2,1)S(1)} %fusion.8), channel_id=1, source_target_pairs={{0,8},{1,9},{2,10},{3,11},{4,12},{5,13},{6,14},{7,15},{8,0},{9,1},... | collective-permute-start | bytes 393224 | tf_op jit(solution)/shard_map/ppermute | solution.py:283
  58.4 11.1 %collective-permute-start.2 = (bf16[1,384,256]{2,1,0:T(8,128)(2,1)S(1)}, bf16[1,384,256]{2,1,0:T(8,128)(2,1)S(1)}, u32[]{:S(2)}, u32[]{:S(2)}) collective-permute-start(bf16[1,384,256]{2,1,0:T(8,128)(2,1)S(1)} %get-tuple-element.27), channel_id=1, source_target_pairs={{0,8},{1,9},{2,10},{3,11},{4,12},{5,13},{6,14},{7,15},{8,0},{9,1},... | collective-permute-start | bytes 589832 | tf_op jit(solution)/shard_map/ppermute | solution.py:283
  64.0 11.0 %collective-permute-start.7 = (bf16[2,384,256]{2,1,0:T(8,128)(2,1)S(1)}, bf16[2,384,256]{2,1,0:T(8,128)(2,1)S(1)}, u32[]{:S(2)}, u32[]{:S(2)}) collective-permute-start(bf16[2,384,256]{2,1,0:T(8,128)(2,1)S(1)} %pad_maximum_fusion.7), channel_id=1, source_target_pairs={{0,8},{1,9},{2,10},{3,11},{4,12},{5,13},{6,14},{7,15},{8,0},{9,1},... | collective-permute-start | bytes 1179656 | tf_op jit(solution)/shard_map/ppermute | solution.py:283
  66.7 6.3 %collective-permute-start.24 = (bf16[4,128,128]{2,1,0:T(8,128)(2,1)S(1)}, bf16[4,128,128]{2,1,0:T(8,128)(2,1)S(1)}, u32[]{:S(2)}, u32[]{:S(2)}) collective-permute-start(bf16[4,128,128]{2,1,0:T(8,128)(2,1)S(1)} %fusion.6), channel_id=1, source_target_pairs={{0,24},{1,25},{2,26},{3,27},{4,28},{5,29},{6,30},{7,31},{8,16},{9,... | collective-permute-start | bytes 393224 | tf_op jit(solution)/shard_map/ppermute | solution.py:283
  69.6 9.1 %collective-permute-start.3 = (bf16[2,384,256]{2,1,0:T(8,128)(2,1)S(1)}, bf16[2,384,256]{2,1,0:T(8,128)(2,1)S(1)}, u32[]{:S(2)}, u32[]{:S(2)}) collective-permute-start(bf16[2,384,256]{2,1,0:T(8,128)(2,1)S(1)} %pad_maximum_fusion.6), channel_id=1, source_target_pairs={{0,24},{1,25},{2,26},{3,27},{4,28},{5,29},{6,30},{7,31},{8,16},{9,... | collective-permute-start | bytes 1179656 | tf_op jit(solution)/shard_map/ppermute | solution.py:283
  71.6 9.3 %copy-start.6 = (f32[16,96,640]{2,1,0:T(8,128)S(1)}, f32[16,96,640]{2,1,0:T(8,128)}, u32[]{:S(2)}) copy-start(f32[16,96,640]{2,1,0:T(8,128)} %get-tuple-element.17) | copy-start | bytes 11796484
  73.0 81.2 %collective-permute-start.11 = (bf16[256,6144]{1,0:T(8,128)(2,1)}, bf16[256,6144]{1,0:T(8,128)(2,1)S(1)}, u32[]{:S(2)}, u32[]{:S(2)}) collective-permute-start(bf16[256,6144]{1,0:T(8,128)(2,1)} %bitcast.3), channel_id=1, source_target_pairs={{32,0},{33,1},{34,2},{35,3},{36,4},{37,5},{38,6},{39,7},{40,8},{41... | collective-permute-start | bytes 9437192 | tf_op jit(solution)/shard_map/ppermute | solution.py:283
  75.0 10.9 %collective-permute-start.25 = (bf16[4,128,128]{2,1,0:T(8,128)(2,1)S(1)}, bf16[4,128,128]{2,1,0:T(8,128)(2,1)S(1)}, u32[]{:S(2)}, u32[]{:S(2)}) collective-permute-start(bf16[4,128,128]{2,1,0:T(8,128)(2,1)S(1)} %get-tuple-element.22), channel_id=1, source_target_pairs={{0,2},{1,3},{2,0},{3,1},{4,6},{5,7},{6,4},{7,5},{8,10},{9,11},{10,... | collective-permute-start | bytes 393224 | tf_op jit(solution)/shard_map/ppermute | solution.py:283
  78.7 16.7 %collective-permute-start.8 = (bf16[4,384,256]{2,1,0:T(8,128)(2,1)S(1)}, bf16[4,384,256]{2,1,0:T(8,128)(2,1)S(1)}, u32[]{:S(2)}, u32[]{:S(2)}) collective-permute-start(bf16[4,384,256]{2,1,0:T(8,128)(2,1)S(1)} %pad_maximum_fusion.3), channel_id=1, source_target_pairs={{0,6},{1,7},{2,4},{3,5},{4,2},{5,3},{6,0},{7,1},{8,14},{9,15},{10,... | collective-permute-start | bytes 2359304 | tf_op jit(solution)/shard_map/ppermute | solution.py:283
  80.7 20.3 %collective-permute-start.4 = (bf16[4,384,256]{2,1,0:T(8,128)(2,1)S(1)}, bf16[4,384,256]{2,1,0:T(8,128)(2,1)S(1)}, u32[]{:S(2)}, u32[]{:S(2)}) collective-permute-start(bf16[4,384,256]{2,1,0:T(8,128)(2,1)S(1)} %pad_maximum_fusion.2), channel_id=1, source_target_pairs={{0,2},{1,3},{2,0},{3,1},{4,6},{5,7},{6,4},{7,5},{8,10},{9,11},{10,... | collective-permute-start | bytes 2359304 | tf_op jit(solution)/shard_map/ppermute | solution.py:283
  80.9 2.7 %copy-start.1 = (f32[16,96,640]{2,1,0:T(8,128)S(1)}, f32[16,96,640]{2,1,0:T(8,128)}, u32[]{:S(2)}) copy-start(f32[16,96,640]{2,1,0:T(8,128)} %copy-done) | copy-start | bytes 11796484
  83.3 22.0 %collective-permute-start.18 = (bf16[8,96,640]{2,1,0:T(8,128)(2,1)S(1)}, bf16[8,96,640]{2,1,0:T(8,128)(2,1)S(1)}, u32[]{:S(2)}, u32[]{:S(2)}) collective-permute-start(bf16[8,96,640]{2,1,0:T(8,128)(2,1)S(1)} %slice.150), channel_id=1, source_target_pairs={{0,8},{1,9},{2,10},{3,11},{4,12},{5,13},{6,14},{7,15},{8,0},{9,1},... | collective-permute-start | bytes 2949128 | tf_op jit(solution)/shard_map/ppermute | solution.py:283
  85.9 20.9 %collective-permute-start.13 = (bf16[8,96,640]{2,1,0:T(8,128)(2,1)S(1)}, bf16[8,96,640]{2,1,0:T(8,128)(2,1)S(1)}, u32[]{:S(2)}, u32[]{:S(2)}) collective-permute-start(bf16[8,96,640]{2,1,0:T(8,128)(2,1)S(1)} %slice.151), channel_id=1, source_target_pairs={{0,24},{1,25},{2,26},{3,27},{4,28},{5,29},{6,30},{7,31},{8,16},{9,... | collective-permute-start | bytes 2949128 | tf_op jit(solution)/shard_map/ppermute | solution.py:283
  95.4 13.8 %collective-permute-start.26 = (bf16[4,128,128]{2,1,0:T(8,128)(2,1)S(1)}, bf16[4,128,128]{2,1,0:T(8,128)(2,1)S(1)}, u32[]{:S(2)}, u32[]{:S(2)}) collective-permute-start(bf16[4,128,128]{2,1,0:T(8,128)(2,1)S(1)} %fusion.7), channel_id=1, source_target_pairs={{0,6},{1,7},{2,4},{3,5},{4,2},{5,3},{6,0},{7,1},{8,14},{9,15},{10,... | collective-permute-start | bytes 393224 | tf_op jit(solution)/shard_map/ppermute | solution.py:283
  101.1 53.0 %collective-permute-start.9 = (bf16[8,384,256]{2,1,0:T(8,128)(2,1)S(1)}, bf16[8,384,256]{2,1,0:T(8,128)(2,1)S(1)}, u32[]{:S(2)}, u32[]{:S(2)}) collective-permute-start(bf16[8,384,256]{2,1,0:T(8,128)(2,1)S(1)} %pad_maximum_fusion.1.held_b), channel_id=1, source_target_pairs={{0,2},{1,3},{2,0},{3,1},{4,6},{5,7},{6,4},{7,5},{8,10},{9,11},{10,... | collective-permute-start | bytes 4718600 | tf_op jit(solution)/shard_map/ppermute | solution.py:283
  105.3 48.8 %collective-permute-start.5 = (bf16[8,384,256]{2,1,0:T(8,128)(2,1)S(1)}, bf16[8,384,256]{2,1,0:T(8,128)(2,1)S(1)}, u32[]{:S(2)}, u32[]{:S(2)}) collective-permute-start(bf16[8,384,256]{2,1,0:T(8,128)(2,1)S(1)} %pad_maximum_fusion.held_a), channel_id=1, source_target_pairs={{0,6},{1,7},{2,4},{3,5},{4,2},{5,3},{6,0},{7,1},{8,14},{9,15},{10,... | collective-permute-start | bytes 4718600 | tf_op jit(solution)/shard_map/ppermute | solution.py:283
  106.7 25.5 %collective-permute-start.19 = (bf16[4,96,640]{2,1,0:T(8,128)(2,1)S(1)}, bf16[4,96,640]{2,1,0:T(8,128)(2,1)S(1)}, u32[]{:S(2)}, u32[]{:S(2)}) collective-permute-start(bf16[4,96,640]{2,1,0:T(8,128)(2,1)S(1)} %slice.152), channel_id=1, source_target_pairs={{0,6},{1,7},{2,4},{3,5},{4,2},{5,3},{6,0},{7,1},{8,14},{9,15},{10,... | collective-permute-start | bytes 1474568 | tf_op jit(solution)/shard_map/ppermute | solution.py:283
  109.1 25.1 %collective-permute-start.14 = (bf16[4,96,640]{2,1,0:T(8,128)(2,1)S(1)}, bf16[4,96,640]{2,1,0:T(8,128)(2,1)S(1)}, u32[]{:S(2)}, u32[]{:S(2)}) collective-permute-start(bf16[4,96,640]{2,1,0:T(8,128)(2,1)S(1)} %slice.153), channel_id=1, source_target_pairs={{0,2},{1,3},{2,0},{3,1},{4,6},{5,7},{6,4},{7,5},{8,10},{9,11},{10,... | collective-permute-start | bytes 1474568 | tf_op jit(solution)/shard_map/ppermute | solution.py:283
  132.2 21.3 %collective-permute-start.10 = (bf16[256,512]{1,0:T(8,128)(2,1)S(1)}, bf16[256,512]{1,0:T(8,128)(2,1)S(1)}, u32[]{:S(2)}, u32[]{:S(2)}) collective-permute-start(bf16[256,512]{1,0:T(8,128)(2,1)S(1)} %fusion.1.k_ref), channel_id=1, source_target_pairs={{32,0},{33,1},{34,2},{35,3},{36,4},{37,5},{38,6},{39,7},{40,8},{41... | collective-permute-start | bytes 786440 | tf_op jit(solution)/shard_map/ppermute | solution.py:283
  134.3 6.3 %collective-permute-start.20 = (bf16[2,96,640]{2,1,0:T(8,128)(2,1)S(1)}, bf16[2,96,640]{2,1,0:T(8,128)(2,1)S(1)}, u32[]{:S(2)}, u32[]{:S(2)}) collective-permute-start(bf16[2,96,640]{2,1,0:T(8,128)(2,1)S(1)} %slice.154), channel_id=1, source_target_pairs={{0,2},{1,3},{2,0},{3,1},{4,6},{5,7},{6,4},{7,5},{8,10},{9,11},{10,... | collective-permute-start | bytes 737288 | tf_op jit(solution)/shard_map/ppermute | solution.py:283
  140.6 7.4 %collective-permute-start.15 = (bf16[2,96,640]{2,1,0:T(8,128)(2,1)S(1)}, bf16[2,96,640]{2,1,0:T(8,128)(2,1)S(1)}, u32[]{:S(2)}, u32[]{:S(2)}) collective-permute-start(bf16[2,96,640]{2,1,0:T(8,128)(2,1)S(1)} %slice.155), channel_id=1, source_target_pairs={{0,6},{1,7},{2,4},{3,5},{4,2},{5,3},{6,0},{7,1},{8,14},{9,15},{10,... | collective-permute-start | bytes 737288 | tf_op jit(solution)/shard_map/ppermute | solution.py:283
  148.0 16.1 %collective-permute-start.21 = (bf16[1,96,640]{2,1,0:T(8,128)(2,1)S(1)}, bf16[1,96,640]{2,1,0:T(8,128)(2,1)S(1)}, u32[]{:S(2)}, u32[]{:S(2)}) collective-permute-start(bf16[1,96,640]{2,1,0:T(8,128)(2,1)S(1)} %slice.156), channel_id=1, source_target_pairs={{0,1},{1,0},{2,3},{3,2},{4,5},{5,4},{6,7},{7,6},{8,9},{9,8},{10,11... | collective-permute-start | bytes 368648 | tf_op jit(solution)/shard_map/ppermute | solution.py:283
  153.4 10.6 %copy-start.2 = (f32[1,4,128,128]{3,2,1,0:T(8,128)S(1)}, f32[1,4,128,128]{3,2,1,0:T(8,128)}, u32[]{:S(2)}) copy-start(f32[1,4,128,128]{3,2,1,0:T(8,128)} %param.15) | copy-start | bytes 786436
  153.4 10.6 %copy-start.3 = (f32[1,1,192,192]{3,2,1,0:T(8,128)S(1)}, f32[1,1,192,192]{3,2,1,0:T(8,128)}, u32[]{:S(2)}) copy-start(f32[1,1,192,192]{3,2,1,0:T(8,128)} %param.14) | copy-start | bytes 442372
  153.5 10.6 %collective-permute-start.16 = (bf16[1,96,640]{2,1,0:T(8,128)(2,1)S(1)}, bf16[1,96,640]{2,1,0:T(8,128)(2,1)S(1)}, u32[]{:S(2)}, u32[]{:S(2)}) collective-permute-start(bf16[1,96,640]{2,1,0:T(8,128)(2,1)S(1)} %slice.157), channel_id=1, source_target_pairs={{0,1},{1,0},{2,3},{3,2},{4,5},{5,4},{6,7},{7,6},{8,9},{9,8},{10,11... | collective-permute-start | bytes 368648 | tf_op jit(solution)/shard_map/ppermute | solution.py:283

commit v2 on v0

v2 whole, which is shorter than its diff:
```python
import jax
import jax.numpy as jnp
from jax import lax
from jax.experimental import pallas as pl
from jax.experimental.pallas import tpu as pltpu
from jax.sharding import PartitionSpec as P

rope_base = 100000.0
AXES = ("segment", "dp")
SECTIONS = 8
NX, NY, NZ = 4, 4, 2
DP = NX * NY * NZ
BLK = 192
PAIR = 2 * BLK
KO = 512
HD = 128
KVH = 4
CUT = 120
FOLD = 48

Z, YA, YB, XA, XB = 0, 1, 2, 3, 4
SUMS = (
    ((XA, XB, YA, YB, Z), (XB, XA, YA, YB, Z)),
    ((YA, YB, XA, XB, Z), (YB, YA, XA, XB, Z)),
)
WEIGHTS = (
    ((XA, XB, YA, YB), (XA, XB, YB, YA)),
    ((YA, YB, XA, XB), (YA, YB, XB, XA)),
)
RINGS = (((XA, XB), (YA, YB)), ((YA, YB), (XA, XB)))


def gray(i):
    return i ^ (i >> 1)


def place_bits(dp):
    return (gray(dp >> 3) << 3) | (gray((dp >> 1) & 3) << 1) | (dp & 1)


def flipped(dp, dim):
    x, y, z = dp >> 3, (dp >> 1) & 3, dp & 1
    if dim == XA:
        x ^= 1
    elif dim == XB:
        x = 3 - x
    elif dim == YA:
        y ^= 1
    elif dim == YB:
        y = 3 - y
    else:
        z ^= 1
    return (x * NY + y) * NZ + z


def flip_route(dims_of_core, sections=SECTIONS):
    route = []
    for seg in range(sections):
        for dp in range(DP):
            target = dp
            for dim in dims_of_core[seg % 2]:
                target = flipped(target, dim)
            route.append((seg * DP + dp, seg * DP + target))
    return route


def step_route(orders, stream, step):
    sections = SECTIONS - 1 if orders is WEIGHTS else SECTIONS
    return flip_route([(orders[core][stream][step],) for core in range(2)], sections)


def ring_route(ring, which):
    dims = [RINGS[core][ring] for core in range(2)]
    return flip_route([[d for i, d in enumerate(pair) if bit(which, i)] for pair in dims])


def back_route(cross):
    route = []
    for seg in range(1, SECTIONS):
        for dp in range(DP):
            target = flipped(dp, Z) if cross else dp
            route.append((seg * DP + dp, (seg - 1) * DP + target))
    return route


def bit(v, i):
    return (v >> i) & 1


def dot_rows(a, b):
    return lax.dot_general(a, b, (((0,), (0,)), ((), ())), preferred_element_type=jnp.float32)


def dot_cols(a, b):
    return lax.dot_general(a, b, (((1,), (1,)), ((), ())), preferred_element_type=jnp.float32)


def dot(a, b):
    return jnp.dot(a, b, preferred_element_type=jnp.float32)


def my_place():
    return lax.axis_index("segment") & 1, place_bits(lax.axis_index("dp"))


def block_order(slot_ref, order_ref):
    core, me = my_place()
    for stream in range(2):
        for r in range(DP):
            rels = [
                sum(bit(r, 4 - k) << d for k, d in enumerate(SUMS[c][stream])) for c in range(2)
            ]
            owner = me ^ jnp.where(core == 0, rels[0], rels[1])
            x, y, z = gray(owner >> 3), gray((owner >> 1) & 3), owner & 1
            order_ref[stream, r] = slot_ref[0, (x * NY + y) * NZ + z]


def frequencies():
    lane = lax.broadcasted_iota(jnp.int32, (1, HD), 1) & (HD // 2 - 1)
    row = jnp.full((1, HD), 1.0, jnp.float32)
    for i in range(1, HD // 2):
        row = jnp.where(lane == i, jnp.float32(rope_base ** (-2.0 * i / HD)), row)
    return row


def rope_back(grad_ref, bounds_ref, key_ref, total):
    rows = grad_ref.shape[1]
    index = lax.axis_index("dp") * rows + lax.broadcasted_iota(jnp.int32, (rows, HD), 0)
    prefix_len, suffix_len = bounds_ref[0, 0], bounds_ref[0, 1]
    position = jnp.where(
        index < prefix_len,
        index,
        jnp.where(
            index < prefix_len + suffix_len,
            index + (total - prefix_len - suffix_len),
            index - suffix_len,
        ),
    )
    angle = position.astype(jnp.float32) * frequencies()
    cosines = jnp.cos(angle)
    sines = jnp.sin(angle)
    lane = lax.broadcasted_iota(jnp.int32, (rows, HD), 1)
    sines = jnp.where(lane < HD // 2, sines, -sines)
    for h in range(KVH):
        cols = slice(h * HD, (h + 1) * HD)
        grad = grad_ref[0, :, cols].astype(jnp.float32)
        swapped = pltpu.roll(grad, HD // 2, 1)
        key_ref[:, cols] = (grad * cosines + swapped * sines).astype(jnp.bfloat16)


def keys_kernel(
    total, slot_ref, bounds_ref, grad_ref, weight_ref, key_ref, head_ref, order_ref, both_ref
):
    block_order(slot_ref, order_ref)
    rope_back(grad_ref, bounds_ref, key_ref, total)
    for h in range(KVH):
        head = key_ref[:, h * HD : (h + 1) * HD]
        head_ref[h * HD : (h + 1) * HD] = dot_rows(head, head).astype(jnp.bfloat16)
    both_ref[:BLK] = weight_ref[0]
    both_ref[BLK:] = key_ref[...]


def keys_and_order(total, slots, bounds, key_grad, key_weight):
    rows = key_grad.shape[1]
    smem = pl.BlockSpec(memory_space=pltpu.SMEM)
    vmem = pl.BlockSpec(memory_space=pltpu.VMEM)

    def kernel(*refs):
        keys_kernel(total, *refs)

    return pl.pallas_call(
        kernel,
        out_shape=(
            jax.ShapeDtypeStruct((rows, KO), jnp.bfloat16),
            jax.ShapeDtypeStruct((KVH * HD, HD), jnp.bfloat16),
            jax.ShapeDtypeStruct((2, DP), jnp.int32),
            jax.ShapeDtypeStruct((BLK + rows, KO), jnp.bfloat16),
        ),
        in_specs=[smem, smem, vmem, vmem],
        out_specs=(vmem, vmem, smem, vmem),
        compiler_params=pltpu.CompilerParams(vmem_limit_bytes=8 * 2**20),
        name="keys",
    )(slots, bounds, key_grad, key_weight)


def products_loop(order_ref, x_ref, key_ref, turned, out_a, out_b, base):
    lane = lax.broadcasted_iota(jnp.int32, (64, 128), 1)
    lower = lane < 64

    def one(i, _):
        block = order_ref[0, base + i]
        rows = turned[pl.ds(pl.multiple_of(block * BLK, 64), CUT)]
        out_a[i] = dot(rows, key_ref[...]).astype(out_a.dtype)

        block = order_ref[1, base + i]
        odd = block & 1
        rows = turned[pl.ds(pl.multiple_of(block * BLK, 64), BLK)]
        out_b[i, : BLK - CUT] = dot(rows[CUT:], key_ref[...]).astype(out_b.dtype)
        window = pl.multiple_of((block >> 1) * PAIR + odd * 128, 128)
        gram = dot(rows, x_ref[0, :, pl.ds(window, 256)])
        near, far = gram[:, :128], gram[:, 128:]
        even_top = jnp.where(lower, near[:64], pltpu.roll(far[128:], 64, 1))
        odd_end = jnp.where(lower, pltpu.roll(near[:64], 64, 1), far[128:])
        is_odd = odd == 1
        packed = jnp.concatenate(
            [
                jnp.where(is_odd, far[:64], even_top),
                jnp.where(is_odd, far[64:128], near[64:128]),
                jnp.where(is_odd, odd_end, near[128:]),
            ],
            axis=0,
        )
        for c in range(4):
            part = packed[c * FOLD : (c + 1) * FOLD].astype(out_b.dtype)
            out_b[i, BLK - CUT :, c * 128 : (c + 1) * 128] = part
        return 0

    lax.fori_loop(0, out_a.shape[0], one, 0, unroll=4)


def sent_kernel(order_ref, x_ref, key_ref, send_a, send_b, turned):
    for c in range(DP // 4):
        wide = slice(c * 4 * BLK, (c + 1) * 4 * BLK)
        turned[wide] = x_ref[0, :, wide].T
    products_loop(order_ref, x_ref, key_ref, turned, send_a, send_b, DP // 2)


def kept_kernel(order_ref, x_ref, key_ref, turned, far_a, far_b, near_a, near_b):
    products_loop(order_ref, x_ref, key_ref, turned, far_a, far_b, DP // 4)
    products_loop(order_ref, x_ref, key_ref, turned, near_a, near_b, 0)


SEND = jax.ShapeDtypeStruct((DP // 2, CUT, KO), jnp.bfloat16)
KEEP = jax.ShapeDtypeStruct((DP // 4, CUT, KO), jnp.float32)
NEXT = jax.ShapeDtypeStruct((DP // 4, CUT, KO), jnp.bfloat16)


def products(kernel, name, out_shape, *args):
    smem = pl.BlockSpec(memory_space=pltpu.SMEM)
    vmem = pl.BlockSpec(memory_space=pltpu.VMEM)
    return pl.pallas_call(
        kernel,
        out_shape=out_shape,
        in_specs=[smem] + [vmem] * (len(args) - 1),
        out_specs=(vmem,) * len(out_shape),
        compiler_params=pltpu.CompilerParams(vmem_limit_bytes=24 * 2**20),
        cost_estimate=pl.CostEstimate(
            flops=256 * 6144 * 704, bytes_accessed=10 * 2**20, transcendentals=0
        ),
        name=name,
    )(*args)


def sent_products(order, layer_inputs, key_pre):
    rows, width = layer_inputs.shape[1:]
    turned = jax.ShapeDtypeStruct((width, rows), jnp.bfloat16)
    return products(
        sent_kernel, "sent_products", (SEND, SEND, turned), order, layer_inputs, key_pre
    )


def kept_products(order, layer_inputs, key_pre, turned):
    return products(
        kept_kernel, "kept_products", (KEEP,) * 4, order, layer_inputs, key_pre, turned
    )


def halved_kernel(far_a, got_a, far_b, got_b, send_a, send_b):
    for far, got, send in ((far_a, got_a, send_a), (far_b, got_b, send_b)):
        for i in range(8):
            send[i] = (far[i] + got[8 + i].astype(jnp.float32)).astype(jnp.bfloat16)


def halved(far_a, got_a, far_b, got_b):
    vmem = pl.BlockSpec(memory_space=pltpu.VMEM)
    return pl.pallas_call(
        halved_kernel,
        out_shape=(NEXT, NEXT),
        in_specs=[vmem] * 4,
        out_specs=(vmem,) * 2,
        compiler_params=pltpu.CompilerParams(vmem_limit_bytes=16 * 2**20),
        name="halved",
    )(far_a, got_a, far_b, got_b)


RING_ROWS = 4 * CUT


def ring_sums_kernel(near_a, first_a, got_a, near_b, first_b, got_b, head, own, to_a, to_b, to_ab):
    groups = ((near_a, first_a, got_a), (near_b, first_b, got_b))
    for s, (near, first, got) in enumerate(groups):
        for i in range(8):
            total = near[i] + first[i].astype(jnp.float32) + got[i].astype(jnp.float32)
            out = (own, to_b, to_a, to_ab)[i // 2]
            row = (s * 2 + i % 2) * CUT
            out[row : row + CUT] = total.astype(out.dtype)
    for out in (to_a, to_b, to_ab):
        out[RING_ROWS:] = head[...]


def ring_sums(*parts):
    vmem = pl.BlockSpec(memory_space=pltpu.VMEM)
    sent = jax.ShapeDtypeStruct((RING_ROWS + HD, KO), jnp.bfloat16)
    return pl.pallas_call(
        ring_sums_kernel,
        out_shape=(jax.ShapeDtypeStruct((RING_ROWS, KO), jnp.float32), sent, sent, sent),
        in_specs=[vmem] * 7,
        out_specs=(vmem,) * 4,
        compiler_params=pltpu.CompilerParams(vmem_limit_bytes=20 * 2**20),
        name="ring_sums",
    )(*parts)


def last_sums_kernel(total, own, head, got_a, got_b, got_ab, keep, send, head_ref):
    def added(mine, rows):
        terms = [got[rows].astype(jnp.float32) for got in (got_a, got_b, got_ab)]
        return (mine + terms[0]) + (terms[1] + terms[2])

    for s in range(2):
        for i, out in enumerate((send, keep)):
            row = (s * 2 + 1 - i) * CUT
            rows = slice(row, row + CUT)
            out[s] = added(own[rows], rows).astype(out.dtype)
    heads = added(head[...].astype(jnp.float32), slice(RING_ROWS, RING_ROWS + HD))
    for h in range(KVH):
        head_ref[0, h] = heads[:, h * HD : (h + 1) * HD] * jnp.float32(1.0 / total)


def last_sums(total, *parts):
    vmem = pl.BlockSpec(memory_space=pltpu.VMEM)
    shape = (2, CUT, KO)

    def kernel(*refs):
        last_sums_kernel(total, *refs)

    return pl.pallas_call(
        kernel,
        out_shape=(
            jax.ShapeDtypeStruct(shape, jnp.float32),
            jax.ShapeDtypeStruct(shape, jnp.bfloat16),
            jax.ShapeDtypeStruct((1, KVH, HD, HD), jnp.float32),
        ),
        in_specs=[vmem] * 5,
        out_specs=(vmem,) * 3,
        compiler_params=pltpu.CompilerParams(vmem_limit_bytes=8 * 2**20),
        name="last_sums",
    )(*parts)


def pair_kernel(straight, crossed, head, other, out):
    first = lax.axis_index("dp") & 1

    def turn(top, bottom):
        out[:, :PAIR] = jnp.concatenate([top[:BLK], bottom[:BLK]], axis=0).T

    pl.when(first == 0)(lambda: turn(straight, crossed))
    pl.when(first == 1)(lambda: turn(crossed, straight))
    both = head[...].astype(jnp.float32) + other[...].astype(jnp.float32)
    out[:, PAIR:] = both.astype(jnp.bfloat16)


def weight_pair(straight, crossed, head, other):
    vmem = pl.BlockSpec(memory_space=pltpu.VMEM)
    return pl.pallas_call(
        pair_kernel,
        out_shape=jax.ShapeDtypeStruct((KO, PAIR + HD), jnp.bfloat16),
        in_specs=[vmem] * 4,
        out_specs=vmem,
        compiler_params=pltpu.CompilerParams(vmem_limit_bytes=8 * 2**20),
        name="weight_pair",
    )(straight, crossed, head, other)


def stack_kernel(own, near_a, near_b, near_ab, held_a, held_b, head):
    pieces = (own, near_a, near_b, near_ab)
    for i, piece in enumerate(pieces):
        held_a[i] = piece[: KO // 2, :PAIR]
        held_b[i] = piece[KO // 2 :, :PAIR]
    terms = [piece[:, PAIR:].astype(jnp.float32) for piece in pieces]
    total = ((terms[0] + terms[1]) + (terms[2] + terms[3])).astype(jnp.bfloat16)
    for h in range(KVH):
        head[:, h * HD : (h + 1) * HD] = total[h * HD : (h + 1) * HD]


def stacked(pieces):
    vmem = pl.BlockSpec(memory_space=pltpu.VMEM)
    held = jax.ShapeDtypeStruct((4, KO // 2, PAIR), jnp.bfloat16)
    return pl.pallas_call(
        stack_kernel,
        out_shape=(held, held, jax.ShapeDtypeStruct((HD, KO), jnp.bfloat16)),
        in_specs=[vmem] * 4,
        out_specs=(vmem,) * 3,
        compiler_params=pltpu.CompilerParams(vmem_limit_bytes=8 * 2**20),
        name="stacked",
    )(*pieces)


def finish_kernel(total, slot_ref, keep, got, inv_in, inv_out, precond_ref, gram_ref):
    scale = jnp.float32(1.0 / total)
    sum_a = (keep[0] + got[0].astype(jnp.float32)) * scale
    sum_b = (keep[1] + got[1].astype(jnp.float32)) * scale
    grad = jnp.concatenate([sum_a, sum_b[: BLK - CUT]], axis=0)
    packed = jnp.concatenate(
        [sum_b[BLK - CUT :, c * 128 : (c + 1) * 128] for c in range(4)], axis=0
    )
    odd = slot_ref[0, lax.axis_index("dp")] & 1

    @pl.when(odd == 0)
    def _():
        low = packed[64:]
        turned = low.T
        gram_ref[:64] = jnp.concatenate([packed[:64, :64], turned[:64]], axis=1)
        gram_ref[64:128] = jnp.concatenate([low[:64], turned[64:, 64:]], axis=1)
        gram_ref[128:] = jnp.concatenate([low[64:], packed[:64, 64:]], axis=1)

    @pl.when(odd == 1)
    def _():
        high = packed[:128]
        turned = high.T
        gram_ref[:64] = jnp.concatenate([packed[128:, :64], high[:64]], axis=1)
        gram_ref[64:128] = jnp.concatenate([turned[:64, :64], high[64:]], axis=1)
        gram_ref[128:] = jnp.concatenate([turned[64:], packed[128:, 64:]], axis=1)

    for h in range(KVH):
        cols = slice(h * HD, (h + 1) * HD)
        left = jnp.dot(
            inv_in[0],
            grad[:, cols],
            precision=lax.Precision.HIGHEST,
            preferred_element_type=jnp.float32,
        )
        precond_ref[0, :, cols] = jnp.dot(
            left,
            inv_out[h],
            precision=lax.Precision.HIGHEST,
            preferred_element_type=jnp.float32,
        )


def finished(total, slots, keep, got, inv_in, inv_out):
    vmem = pl.BlockSpec(memory_space=pltpu.VMEM)

    def kernel(*refs):
        finish_kernel(total, *refs)

    return pl.pallas_call(
        kernel,
        out_shape=(
            jax.ShapeDtypeStruct((1, BLK, KO), jnp.float32),
            jax.ShapeDtypeStruct((BLK, BLK), jnp.float32),
        ),
        in_specs=[pl.BlockSpec(memory_space=pltpu.SMEM)] + [vmem] * 4,
        out_specs=(vmem, vmem),
        compiler_params=pltpu.CompilerParams(vmem_limit_bytes=16 * 2**20),
        name="finish",
    )(slots, keep, got, inv_in, inv_out)


def passed_block(k_ref, resid_ref, pieces, i, ring):
    core, me = my_place()
    rels = [
        sum(bit(i, k) << d for k, d in enumerate(RINGS[c][0]))
        + sum(bit(ring, k) << d for k, d in enumerate(RINGS[c][1]))
        for c in range(2)
    ]
    owner = me ^ jnp.where(core == 0, rels[0], rels[1])
    x, y = gray(owner >> 3), gray((owner >> 1) & 3)
    cols = pl.ds(pl.multiple_of((x * NY + y) * PAIR, 128), PAIR)
    branch = dot(k_ref[BLK:, : KO // 2], pieces[0][i]) + dot(k_ref[BLK:, KO // 2 :], pieces[1][i])
    return cols, (resid_ref[:, cols].astype(jnp.float32) + branch).astype(jnp.bfloat16)


def passed_kernel(held_a, held_b, third_a, third_b, fourth_a, fourth_b, k_ref, resid_ref, out_ref):
    groups = ((held_a, held_b), (third_a, fourth_b), (fourth_a, third_b))
    for ring, pieces in enumerate(groups):
        for i in range(4):
            cols, block = passed_block(k_ref, resid_ref, pieces, i, ring)
            out_ref[:, cols] = block


def passed_grad(*parts):
    vmem = pl.BlockSpec(memory_space=pltpu.VMEM)
    resid = parts[-1]
    return pl.pallas_call(
        passed_kernel,
        out_shape=jax.ShapeDtypeStruct(resid.shape, jnp.bfloat16),
        in_specs=[vmem] * 8,
        out_specs=vmem,
        compiler_params=pltpu.CompilerParams(vmem_limit_bytes=24 * 2**20),
        cost_estimate=pl.CostEstimate(
            flops=2 * 256 * 4608 * 512, bytes_accessed=12 * 2**20, transcendentals=0
        ),
        name="passed_grad",
    )(*parts)


def passed_rest_kernel(both_a, both_b, k_ref, resid_ref, begun, out_ref, blocks, sems):
    copies = []
    for i in range(4):
        cols, blocks[i] = passed_block(k_ref, resid_ref, (both_a, both_b), i, 3)
        copies.append(pltpu.make_async_copy(blocks.at[i], out_ref.at[:, cols], sems.at[i]))
        copies[i].start()
    for copy in copies:
        copy.wait()


def passed_rest(both_a, both_b, key_pre, resid, begun):
    vmem = pl.BlockSpec(memory_space=pltpu.VMEM)
    hbm = pl.BlockSpec(memory_space=pl.ANY)
    return pl.pallas_call(
        passed_rest_kernel,
        out_shape=jax.ShapeDtypeStruct(resid.shape, jnp.bfloat16),
        in_specs=[vmem] * 4 + [hbm],
        out_specs=hbm,
        input_output_aliases={4: 0},
        scratch_shapes=[
            pltpu.VMEM((4, resid.shape[0], PAIR), jnp.bfloat16),
            pltpu.SemaphoreType.DMA((4,)),
        ],
        compiler_params=pltpu.CompilerParams(vmem_limit_bytes=24 * 2**20),
        cost_estimate=pl.CostEstimate(
            flops=2 * 256 * 1536 * 512, bytes_accessed=4 * 2**20, transcendentals=0
        ),
        name="passed_rest",
    )(both_a, both_b, key_pre, resid, begun)


def hop(block, route):
    return lax.ppermute(block, AXES, route)


def tie(*values):
    return lax.optimization_barrier(values)


def body(
    layer_inputs, resid_grad, key_grad, key_weight, fim_bounds, slot_block, inv_input, inv_head
):
    total = layer_inputs.shape[1] * lax.axis_size("dp")

    key_pre, head, order, weight_and_key = keys_and_order(
        total, slot_block, fim_bounds, key_grad, key_weight
    )
    send_a, send_b, turned = sent_products(order, layer_inputs, key_pre)
    straight = hop(weight_and_key, back_route(False))
    send_a, send_b, head, weight = tie(send_a, send_b, head, key_weight[0])
    first = [hop(x, step_route(SUMS, s, 0)) for s, x in enumerate((send_a, send_b))]
    far_a, far_b, near_a, near_b = kept_products(order, layer_inputs, key_pre, turned)
    crossed = hop(weight, back_route(True))
    other = hop(head, flip_route(((Z,), (Z,))))
    pair = weight_pair(straight, crossed, head, other)
    near = [pair] + [hop(pair, ring_route(0, which)) for which in (1, 2, 3)]
    resid_in, pair = tie(resid_grad[0], pair)
    resid = hop(resid_in, back_route(False))

    far_a, far_b, _ = tie(far_a, far_b, pair)
    sums = halved(far_a, first[0], far_b, first[1])
    second = [hop(sums[s], step_route(SUMS, s, 1)) for s in range(2)]

    held_a, held_b, head = stacked(near)
    held = [held_a, held_b]
    third = [hop(held[s], step_route(WEIGHTS, s, 2)) for s in range(2)]
    second[0], second[1], head = tie(*second, head)
    own, *sent = ring_sums(near_a, first[0], second[0], near_b, first[1], second[1], head)
    ring = [hop(sent[i], ring_route(1, i + 1)) for i in range(3)]
    own, held[0], held[1], third[0], third[1], _, _, _ = tie(own, *held, *third, *ring)
    fourth = [hop(held[s], step_route(WEIGHTS, s, 3)) for s in range(2)]
    both = [hop(third[s], step_route(WEIGHTS, s, 3)) for s in range(2)]
    keep, send, head_grams = last_sums(total, own, head, *ring)
    last = hop(send, flip_route(((Z,), (Z,))))
    begun = passed_grad(*held, *third, *fourth, straight, resid)
    last, both[0], both[1] = tie(last, *both)
    passed = passed_rest(*both, straight, resid, begun)
    precond, gram = finished(total, slot_block, keep, last, inv_input[0], inv_head[0])
    return (passed[None], precond[None], gram[None, None], head_grams)


def solution(mesh):
    return jax.shard_map(
        body,
        mesh=mesh,
        in_specs=(
            P("segment", "dp", None),
            P("segment", "dp", None),
            P("segment", "dp", None),
            P("segment", "dp", None),
            P("segment", None),
            P("segment", None),
            P("segment", "dp", None, None),
            P("segment", None, None, None),
        ),
        out_specs=(
            P("segment", "dp", None),
            P("segment", "dp", None, None),
            P("segment", "dp", None, None),
            P("segment", None, None, None),
        ),
        check_vma=False,
    )
```

time: 1170 us -> 132 us (0.11)
  waiting for transfers between devices: 1090 us -> 52.4 us
  starting transfers between devices: 3.94 us -> 53.1 us
  matrix products: 20.6 us -> 0 us
  Pallas kernels: 0 us -> 19.9 us
  local copies, waits for them, and re-layouts: 22.1 us -> 5.09 us
  between operations: 16.5 us -> 1 us
    reduce_scatter x2 -> x0, waiting for transfers between devices: 583 us -> none  [the longest x1 310 us: body(): lax.psum_scatter(jnp.einsum('rcb,rk->cbk', chosen, key_pre, preferred_ele...]
    psum x1 -> x0, waiting for transfers between devices: 414 us -> none  [body(): head_grams = lax.psum(head_term, 'dp') / total]
    all_gather x1 -> x0, waiting for transfers between devices: 94.7 us -> none  [body(): lax.all_gather(key_weight[0], 'dp', axis=0, tiled=True)]
    ppermute x1 -> x21, waiting for transfers between devices: 0.01 us -> 52.4 us  [hop(): return lax.ppermute(block, AXES, route)]
    ppermute x1 -> x21, starting transfers between devices: 3.78 us -> 53.1 us  [hop(): return lax.ppermute(block, AXES, route)]
    dot_general x6 -> x0, matrix products: 20.6 us -> none  [the longest x1 7.32 us: body(): jnp.einsum('rcb,rk->cbk', chosen, key_pre, preferred_element_type=jnp.flo...]
    pallas_call x0 -> x11, Pallas kernels: none -> 19.9 us  [the longest x2 7.17 us: products(): pl.pallas_call(kernel, out_shape=out_shape, in_specs=[smem] + [vmem] * (l...]
  transfers between devices with their start and end apart: 5 -> 21, of which waited for: 4 -> 11; matrix products, arithmetic and copies ran while one was open for 4% -> 0% of each run, Pallas kernels for 0% -> 7%
where the time goes in v2:
time: 132 us; the launch traced here: 131 us
  starting transfers between devices  53.1 us (40%)
  waiting for transfers between devices  52.4 us (40%)
  Pallas kernels  19.9 us (15%)
  local copies, waits for them, and re-layouts  5.09 us (4%)
    ppermute x21, starting transfers between devices, hop(): return lax.ppermute(block, AXES, route)  53.1 us
    ppermute x21, waiting for transfers between devices, hop(): return lax.ppermute(block, AXES, route)  52.4 us
    pallas_call x2, Pallas kernels, products(): pl.pallas_call(kernel, out_shape=out_shape, in_specs=[smem] + [vmem] * (l...  7.17 us
    unnamed x20, local copies, waits for them, and re-layouts  5.09 us
    pallas_call x1, Pallas kernels, finished(): pl.pallas_call(kernel, out_shape=(jax.ShapeDtypeStruct((1, BLK, KO), jnp....  3.55 us
    pallas_call x1, Pallas kernels, passed_grad(): pl.pallas_call(passed_kernel, out_shape=jax.ShapeDtypeStruct(resid.shape,...  3.53 us
  transfers between devices with their start and end apart: 21, of which 11 were waited for; matrix products, arithmetic and copies ran while one was open for 0% of the time, Pallas kernels for 7%

profile of v2, /device:TPU:96, one launch (start us, length us, event | category | flops | bytes accessed | tf_op | source)
XLA Modules:
  0.0 131.5 jit_solution(12929454087244107319)
XLA Ops:
  0.6 0.9 copy-done.1
  1.6 0.9 copy-done.3
  2.5 0.7 copy-done.6
  3.2 0.7 copy-done.8
  3.8 2.0 %keys.1 = (bf16[256,512]{1,0:T(8,128)(2,1)S(1)}, bf16[512,128]{1,0:T(8,128)(2,1)S(1)}, s32[2,32]{1,0:T(2,128)S(1)}, bf16[448,512]{1,0:T(8,128)(2,1)S(1)}) custom-call(s32[1,32]{1,0:T(1,128)S(1)} %copy-done.6, s32[1,2]{1,0:T(1,128)S(1)} %copy-done.8, bf16[1,256,512]{2,1,0:T(8,128)(2,1)S(1)} %copy-done.1, bf16[1,192,512]{2,1,0:T(8,128)(2,1)S(1)} %copy-done.3), custom_call_target="tpu_custom_call" | custom-call | tf_op jit(solution)/shard_map/keys/pallas_call | solution.py:171
  5.9 1.9 %copy-done = bf16[1,256,6144]{2,1,0:T(8,128)(2,1)S(1)} copy-done((bf16[1,256,6144]{2,1,0:T(8,128)(2,1)S(1)}, bf16[1,256,6144]{2,1,0:T(8,128)(2,1)}, u32[]{:S(2)}) %copy-start) | copy-done | bytes 3145752
  7.8 4.0 %sent_products.1 = (bf16[16,120,512]{2,1,0:T(8,128)(2,1)S(1)}, bf16[16,120,512]{2,1,0:T(8,128)(2,1)S(1)}, bf16[6144,256]{1,0:T(8,128)(2,1)S(1)}) custom-call(s32[2,32]{1,0:T(2,128)S(1)} %get-tuple-element.47.order_ref, bf16[1,256,6144]{2,1,0:T(8,128)(2,1)S(1)} %copy-done, bf16[256,512]{1,0:T(8,128)(2,1)S(1)} %get-tuple-element.48.key_ref), custom_call_target="tpu_custom_call" | custom-call | flops 1107296256 | bytes 10485760 | tf_op jit(solution)/shard_map/sent_products/pallas_call | solution.py:241
  11.8 1.6 %collective-permute-start = (bf16[16,120,512]{2,1,0:T(8,128)(2,1)S(1)}, bf16[16,120,512]{2,1,0:T(8,128)(2,1)S(1)}, u32[]{:S(2)}, u32[]{:S(2)}) collective-permute-start(bf16[16,120,512]{2,1,0:T(8,128)(2,1)S(1)} %get-tuple-element.54), channel_id=1, source_target_pairs={{0,8},{1,9},{2,10},{3,11},{4,12},{5,13},{6,14},{7,15},{8,0},{9,1},... | collective-permute-start | bytes 5898248 | tf_op jit(solution)/shard_map/ppermute | solution.py:529
  13.4 2.1 %collective-permute-start.1 = (bf16[16,120,512]{2,1,0:T(8,128)(2,1)S(1)}, bf16[16,120,512]{2,1,0:T(8,128)(2,1)S(1)}, u32[]{:S(2)}, u32[]{:S(2)}) collective-permute-start(bf16[16,120,512]{2,1,0:T(8,128)(2,1)S(1)} %get-tuple-element.59), channel_id=1, source_target_pairs={{0,24},{1,25},{2,26},{3,27},{4,28},{5,29},{6,30},{7,31},{8,16},{9,... | collective-permute-start | bytes 5898248 | tf_op jit(solution)/shard_map/ppermute | solution.py:529
  15.5 1.9 %collective-permute-start.4 = (bf16[448,512]{1,0:T(8,128)(2,1)S(1)}, bf16[448,512]{1,0:T(8,128)(2,1)S(1)}, u32[]{:S(2)}, u32[]{:S(2)}) collective-permute-start(bf16[448,512]{1,0:T(8,128)(2,1)S(1)} %get-tuple-element.62), channel_id=1, source_target_pairs={{32,0},{33,1},{34,2},{35,3},{36,4},{37,5},{38,6},{39,7},{40,8},{41... | collective-permute-start | bytes 1376264 | tf_op jit(solution)/shard_map/ppermute | solution.py:529
  17.4 6.1 %collective-permute-start.5 = (bf16[192,512]{1,0:T(8,128)(2,1)S(1)}, bf16[192,512]{1,0:T(8,128)(2,1)S(1)}, u32[]{:S(2)}, u32[]{:S(2)}) collective-permute-start(bf16[192,512]{1,0:T(8,128)(2,1)S(1)} %bitcast.8), channel_id=1, source_target_pairs={{32,1},{33,0},{34,3},{35,2},{36,5},{37,4},{38,7},{39,6},{40,9},{41... | collective-permute-start | bytes 589832 | tf_op jit(solution)/shard_map/ppermute | solution.py:529
  23.5 0.6 collective-permute-start.6
  24.1 12.2 %collective-permute-done.6.other = bf16[512,128]{1,0:T(8,128)(2,1)S(1)} collective-permute-done((bf16[512,128]{1,0:T(8,128)(2,1)S(1)}, bf16[512,128]{1,0:T(8,128)(2,1)S(1)}, u32[]{:S(2)}, u32[]{:S(2)}) %collective-permute-start.6) | collective-permute-done | bytes 131104 | tf_op jit(solution)/shard_map/ppermute | solution.py:529
  36.3 4.4 %collective-permute-done.5.crossed = bf16[192,512]{1,0:T(8,128)(2,1)S(1)} collective-permute-done((bf16[192,512]{1,0:T(8,128)(2,1)S(1)}, bf16[192,512]{1,0:T(8,128)(2,1)S(1)}, u32[]{:S(2)}, u32[]{:S(2)}) %collective-permute-start.5) | collective-permute-done | bytes 196640 | tf_op jit(solution)/shard_map/ppermute | solution.py:529
  40.7 0.2 weight_pair.1.own
  40.9 0.7 collective-permute-start.7
  41.6 3.6 %collective-permute-start.18 = (bf16[256,6144]{1,0:T(8,128)(2,1)S(1)}, bf16[256,6144]{1,0:T(8,128)(2,1)S(1)}, u32[]{:S(2)}, u32[]{:S(2)}) collective-permute-start(bf16[256,6144]{1,0:T(8,128)(2,1)S(1)} %bitcast.11), channel_id=1, source_target_pairs={{32,0},{33,1},{34,2},{35,3},{36,4},{37,5},{38,6},{39,7},{40,8},{41... | collective-permute-start | bytes 9437192 | tf_op jit(solution)/shard_map/ppermute | solution.py:529
  45.1 1.2 collective-permute-start.8
  46.4 1.5 %collective-permute-start.9 = (bf16[512,512]{1,0:T(8,128)(2,1)S(1)}, bf16[512,512]{1,0:T(8,128)(2,1)S(1)}, u32[]{:S(2)}, u32[]{:S(2)}) collective-permute-start(bf16[512,512]{1,0:T(8,128)(2,1)S(1)} %weight_pair.1.own), channel_id=1, source_target_pairs={{0,16},{1,17},{2,18},{3,19},{4,20},{5,21},{6,22},{7,23},{8,24},{9,... | collective-permute-start | bytes 1572872 | tf_op jit(solution)/shard_map/ppermute | solution.py:529
  47.9 3.1 %kept_products.1 = (f32[8,120,512]{2,1,0:T(8,128)S(1)}, f32[8,120,512]{2,1,0:T(8,128)S(1)}, f32[8,120,512]{2,1,0:T(8,128)S(1)}, f32[8,120,512]{2,1,0:T(8,128)S(1)}) custom-call(s32[2,32]{1,0:T(2,128)S(1)} %get-tuple-element.47.order_ref, bf16[1,256,6144]{2,1,0:T(8,128)(2,1)S(1)} %copy-done, bf16[256,512]{1,0:T(8,128)(2,1)S(1)} %get-tuple-element.48.key_ref, ...), custom_call_target="tpu_custom_call" | custom-call | flops 1107296256 | bytes 10485760 | tf_op jit(solution)/shard_map/kept_products/pallas_call | solution.py:241
  51.1 0.3 halved.1
  51.4 0.9 collective-permute-start.2
  52.3 1.2 collective-permute-start.3
  53.5 7.8 %collective-permute-done.8.near_b = bf16[512,512]{1,0:T(8,128)(2,1)S(1)} collective-permute-done((bf16[512,512]{1,0:T(8,128)(2,1)S(1)}, bf16[512,512]{1,0:T(8,128)(2,1)S(1)}, u32[]{:S(2)}, u32[]{:S(2)}) %collective-permute-start.8) | collective-permute-done | bytes 524320 | tf_op jit(solution)/shard_map/ppermute | solution.py:529
  61.2 0.2 stacked.1
  61.5 2.4 %collective-permute-start.10 = (bf16[4,256,384]{2,1,0:T(8,128)(2,1)S(1)}, bf16[4,256,384]{2,1,0:T(8,128)(2,1)S(1)}, u32[]{:S(2)}, u32[]{:S(2)}) collective-permute-start(bf16[4,256,384]{2,1,0:T(8,128)(2,1)S(1)} %get-tuple-element.83.held_a), channel_id=1, source_target_pairs={{0,2},{1,3},{2,0},{3,1},{4,6},{5,7},{6,4},{7,5},{8,10},{9,11},{10,... | collective-permute-start | bytes 2359304 | tf_op jit(solution)/shard_map/ppermute | solution.py:529
  63.8 4.9 %collective-permute-start.11 = (bf16[4,256,384]{2,1,0:T(8,128)(2,1)S(1)}, bf16[4,256,384]{2,1,0:T(8,128)(2,1)S(1)}, u32[]{:S(2)}, u32[]{:S(2)}) collective-permute-start(bf16[4,256,384]{2,1,0:T(8,128)(2,1)S(1)} %get-tuple-element.84.held_b), channel_id=1, source_target_pairs={{0,6},{1,7},{2,4},{3,5},{4,2},{5,3},{6,0},{7,1},{8,14},{9,15},{10,... | collective-permute-start | bytes 2359304 | tf_op jit(solution)/shard_map/ppermute | solution.py:529
  68.8 3.0 %collective-permute-done.2.got_a = bf16[8,120,512]{2,1,0:T(8,128)(2,1)S(1)} collective-permute-done((bf16[8,120,512]{2,1,0:T(8,128)(2,1)S(1)}, bf16[8,120,512]{2,1,0:T(8,128)(2,1)S(1)}, u32[]{:S(2)}, u32[]{:S(2)}) %collective-permute-start.2) | collective-permute-done | bytes 983072 | tf_op jit(solution)/shard_map/ppermute | solution.py:529
  71.8 0.6 ring_sums.1
  72.4 0.5 collective-permute-start.12
  73.0 3.0 %collective-permute-start.13 = (bf16[608,512]{1,0:T(8,128)(2,1)S(1)}, bf16[608,512]{1,0:T(8,128)(2,1)S(1)}, u32[]{:S(2)}, u32[]{:S(2)}) collective-permute-start(bf16[608,512]{1,0:T(8,128)(2,1)S(1)} %get-tuple-element.74), channel_id=1, source_target_pairs={{0,6},{1,7},{2,4},{3,5},{4,2},{5,3},{6,0},{7,1},{8,14},{9,15},{10,... | collective-permute-start | bytes 1867784 | tf_op jit(solution)/shard_map/ppermute | solution.py:529
  76.0 2.2 %collective-permute-start.14 = (bf16[608,512]{1,0:T(8,128)(2,1)S(1)}, bf16[608,512]{1,0:T(8,128)(2,1)S(1)}, u32[]{:S(2)}, u32[]{:S(2)}) collective-permute-start(bf16[608,512]{1,0:T(8,128)(2,1)S(1)} %get-tuple-element.75), channel_id=1, source_target_pairs={{0,4},{1,5},{2,6},{3,7},{4,0},{5,1},{6,2},{7,3},{8,12},{9,13},{10,... | collective-permute-start | bytes 1867784 | tf_op jit(solution)/shard_map/ppermute | solution.py:529
  78.2 0.7 collective-permute-done.11.third_b
  78.9 3.9 %collective-permute-done.12.refs_2_ = bf16[608,512]{1,0:T(8,128)(2,1)S(1)} collective-permute-done((bf16[608,512]{1,0:T(8,128)(2,1)S(1)}, bf16[608,512]{1,0:T(8,128)(2,1)S(1)}, u32[]{:S(2)}, u32[]{:S(2)}) %collective-permute-start.12) | collective-permute-done | bytes 622624 | tf_op jit(solution)/shard_map/ppermute | solution.py:529
  82.8 9.5 %collective-permute-done.13.refs_3_ = bf16[608,512]{1,0:T(8,128)(2,1)S(1)} collective-permute-done((bf16[608,512]{1,0:T(8,128)(2,1)S(1)}, bf16[608,512]{1,0:T(8,128)(2,1)S(1)}, u32[]{:S(2)}, u32[]{:S(2)}) %collective-permute-start.13) | collective-permute-done | bytes 622624 | tf_op jit(solution)/shard_map/ppermute | solution.py:529
  92.3 0.8 last_sums.1
  93.0 5.8 %collective-permute-start.15 = (bf16[2,120,512]{2,1,0:T(8,128)(2,1)S(1)}, bf16[2,120,512]{2,1,0:T(8,128)(2,1)S(1)}, u32[]{:S(2)}, u32[]{:S(2)}) collective-permute-start(bf16[2,120,512]{2,1,0:T(8,128)(2,1)S(1)} %get-tuple-element.77), channel_id=1, source_target_pairs={{0,1},{1,0},{2,3},{3,2},{4,5},{5,4},{6,7},{7,6},{8,9},{9,8},{10,11... | collective-permute-start | bytes 737288 | tf_op jit(solution)/shard_map/ppermute | solution.py:529
  98.9 5.1 %collective-permute-start.16 = (bf16[4,256,384]{2,1,0:T(8,128)(2,1)S(1)}, bf16[4,256,384]{2,1,0:T(8,128)(2,1)S(1)}, u32[]{:S(2)}, u32[]{:S(2)}) collective-permute-start(bf16[4,256,384]{2,1,0:T(8,128)(2,1)S(1)} %collective-permute-done.10.third_a), channel_id=1, source_target_pairs={{0,6},{1,7},{2,4},{3,5},{4,2},{5,3},{6,0},{7,1},{8,14},{9,15},{10,... | collective-permute-start | bytes 2359304 | tf_op jit(solution)/shard_map/ppermute | solution.py:529
  104.0 1.9 %collective-permute-start.17 = (bf16[4,256,384]{2,1,0:T(8,128)(2,1)S(1)}, bf16[4,256,384]{2,1,0:T(8,128)(2,1)S(1)}, u32[]{:S(2)}, u32[]{:S(2)}) collective-permute-start(bf16[4,256,384]{2,1,0:T(8,128)(2,1)S(1)} %collective-permute-done.11.third_b), channel_id=1, source_target_pairs={{0,2},{1,3},{2,0},{3,1},{4,6},{5,7},{6,4},{7,5},{8,10},{9,11},{10,... | collective-permute-start | bytes 2359304 | tf_op jit(solution)/shard_map/ppermute | solution.py:529
  105.9 2.1 %collective-permute-start.19 = (bf16[4,256,384]{2,1,0:T(8,128)(2,1)S(1)}, bf16[4,256,384]{2,1,0:T(8,128)(2,1)S(1)}, u32[]{:S(2)}, u32[]{:S(2)}) collective-permute-start(bf16[4,256,384]{2,1,0:T(8,128)(2,1)S(1)} %get-tuple-element.83.held_a), channel_id=1, source_target_pairs={{0,6},{1,7},{2,4},{3,5},{4,2},{5,3},{6,0},{7,1},{8,14},{9,15},{10,... | collective-permute-start | bytes 2359304 | tf_op jit(solution)/shard_map/ppermute | solution.py:529
  108.1 3.7 %collective-permute-start.20 = (bf16[4,256,384]{2,1,0:T(8,128)(2,1)S(1)}, bf16[4,256,384]{2,1,0:T(8,128)(2,1)S(1)}, u32[]{:S(2)}, u32[]{:S(2)}) collective-permute-start(bf16[4,256,384]{2,1,0:T(8,128)(2,1)S(1)} %get-tuple-element.84.held_b), channel_id=1, source_target_pairs={{0,2},{1,3},{2,0},{3,1},{4,6},{5,7},{6,4},{7,5},{8,10},{9,11},{10,... | collective-permute-start | bytes 2359304 | tf_op jit(solution)/shard_map/ppermute | solution.py:529
  111.8 2.2 %collective-permute-done.16.both_a = bf16[4,256,384]{2,1,0:T(8,128)(2,1)S(1)} collective-permute-done((bf16[4,256,384]{2,1,0:T(8,128)(2,1)S(1)}, bf16[4,256,384]{2,1,0:T(8,128)(2,1)S(1)}, u32[]{:S(2)}, u32[]{:S(2)}) %collective-permute-start.16) | collective-permute-done | bytes 786464 | tf_op jit(solution)/shard_map/ppermute | solution.py:529
  114.0 3.9 %collective-permute-done.17.both_b = bf16[4,256,384]{2,1,0:T(8,128)(2,1)S(1)} collective-permute-done((bf16[4,256,384]{2,1,0:T(8,128)(2,1)S(1)}, bf16[4,256,384]{2,1,0:T(8,128)(2,1)S(1)}, u32[]{:S(2)}, u32[]{:S(2)}) %collective-permute-start.17) | collective-permute-done | bytes 786464 | tf_op jit(solution)/shard_map/ppermute | solution.py:529
  117.9 3.6 %finish.1 = (f32[1,192,512]{2,1,0:T(8,128)}, f32[192,192]{1,0:T(8,128)}) custom-call(s32[1,32]{1,0:T(1,128)S(1)} %copy-done.7, f32[2,120,512]{2,1,0:T(8,128)S(1)} %get-tuple-element.85.refs_1_, bf16[2,120,512]{2,1,0:T(8,128)(2,1)S(1)} %collective-permute-done.15.refs_2_, f32[1,192,192]{2,1,0:T(8,128)S(1)} %bitcast.9, f32[4,128,128]{2,1,0:T(8,128)S(1)} %bitcast.7), custom_call_target="tpu_custom_call" | custom-call | tf_op jit(solution)/shard_map/finish/pallas_call | solution.py:446
  121.5 0.9 collective-permute-done.19.fourth_a
  122.4 3.9 %collective-permute-done.20.fourth_b = bf16[4,256,384]{2,1,0:T(8,128)(2,1)S(1)} collective-permute-done((bf16[4,256,384]{2,1,0:T(8,128)(2,1)S(1)}, bf16[4,256,384]{2,1,0:T(8,128)(2,1)S(1)}, u32[]{:S(2)}, u32[]{:S(2)}) %collective-permute-start.20) | collective-permute-done | bytes 786464 | tf_op jit(solution)/shard_map/ppermute | solution.py:529
  126.3 3.5 %passed_grad.1.begun = bf16[256,6144]{1,0:T(8,128)(2,1)} custom-call(bf16[4,256,384]{2,1,0:T(8,128)(2,1)S(1)} %get-tuple-element.83.held_a, bf16[4,256,384]{2,1,0:T(8,128)(2,1)S(1)} %get-tuple-element.84.held_b, bf16[4,256,384]{2,1,0:T(8,128)(2,1)S(1)} %collective-permute-done.10.third_a, bf16[4,256,384]{2,1,0:T(8,128)(2,1)S(1)} %collective-permute-done.11.third_b, ...), custom_call_target="tpu_custom_call" | custom-call | flops 1207959552 | bytes 12582912 | tf_op jit(solution)/shard_map/passed_grad/pallas_call | solution.py:484
  129.9 1.4 %passed_rest.1 = bf16[256,6144]{1,0:T(8,128)(2,1)} custom-call(bf16[4,256,384]{2,1,0:T(8,128)(2,1)S(1)} %collective-permute-done.16.both_a, bf16[4,256,384]{2,1,0:T(8,128)(2,1)S(1)} %collective-permute-done.17.both_b, bf16[448,512]{1,0:T(8,128)(2,1)S(1)} %collective-permute-done.4.straight.k_ref, ...), custom_call_target="tpu_custom_call", output_to_operand_aliasing={{}: (4, {})} | custom-call | flops 402653184 | bytes 4194304 | tf_op jit(solution)/shard_map/passed_rest/pallas_call | solution.py:510
  (25 shorter events, 0.1 us)
Async XLA Ops:
  0.6 1.0 copy-start.1
  1.6 0.9 copy-start.3
  2.5 0.7 copy-start.6
  3.2 0.7 copy-start.8
  5.9 1.9 %copy-start = (bf16[1,256,6144]{2,1,0:T(8,128)(2,1)S(1)}, bf16[1,256,6144]{2,1,0:T(8,128)(2,1)}, u32[]{:S(2)}) copy-start(bf16[1,256,6144]{2,1,0:T(8,128)(2,1)} %x_ref.3) | copy-start | bytes 9437188
  7.8 9.6 %copy-start.4 = (bf16[1,192,512]{2,1,0:T(8,128)(2,1)S(1)}, bf16[1,192,512]{2,1,0:T(8,128)(2,1)}, u32[]{:S(2)}) copy-start(bf16[1,192,512]{2,1,0:T(8,128)(2,1)} %refs_3_.1) | copy-start | bytes 589828
  7.8 33.8 %copy-start.9 = (bf16[1,256,6144]{2,1,0:T(8,128)(2,1)S(1)}, bf16[1,256,6144]{2,1,0:T(8,128)(2,1)}, u32[]{:S(2)}) copy-start(bf16[1,256,6144]{2,1,0:T(8,128)(2,1)} %param.9) | copy-start | bytes 9437188
  11.8 34.6 %collective-permute-start = (bf16[16,120,512]{2,1,0:T(8,128)(2,1)S(1)}, bf16[16,120,512]{2,1,0:T(8,128)(2,1)S(1)}, u32[]{:S(2)}, u32[]{:S(2)}) collective-permute-start(bf16[16,120,512]{2,1,0:T(8,128)(2,1)S(1)} %get-tuple-element.54), channel_id=1, source_target_pairs={{0,8},{1,9},{2,10},{3,11},{4,12},{5,13},{6,14},{7,15},{8,0},{9,1},... | collective-permute-start | bytes 5898248 | tf_op jit(solution)/shard_map/ppermute | solution.py:529
  13.4 37.7 %collective-permute-start.1 = (bf16[16,120,512]{2,1,0:T(8,128)(2,1)S(1)}, bf16[16,120,512]{2,1,0:T(8,128)(2,1)S(1)}, u32[]{:S(2)}, u32[]{:S(2)}) collective-permute-start(bf16[16,120,512]{2,1,0:T(8,128)(2,1)S(1)} %get-tuple-element.59), channel_id=1, source_target_pairs={{0,24},{1,25},{2,26},{3,27},{4,28},{5,29},{6,30},{7,31},{8,16},{9,... | collective-permute-start | bytes 5898248 | tf_op jit(solution)/shard_map/ppermute | solution.py:529
  15.5 25.2 %collective-permute-start.4 = (bf16[448,512]{1,0:T(8,128)(2,1)S(1)}, bf16[448,512]{1,0:T(8,128)(2,1)S(1)}, u32[]{:S(2)}, u32[]{:S(2)}) collective-permute-start(bf16[448,512]{1,0:T(8,128)(2,1)S(1)} %get-tuple-element.62), channel_id=1, source_target_pairs={{32,0},{33,1},{34,2},{35,3},{36,4},{37,5},{38,6},{39,7},{40,8},{41... | collective-permute-start | bytes 1376264 | tf_op jit(solution)/shard_map/ppermute | solution.py:529
  17.4 23.3 %collective-permute-start.5 = (bf16[192,512]{1,0:T(8,128)(2,1)S(1)}, bf16[192,512]{1,0:T(8,128)(2,1)S(1)}, u32[]{:S(2)}, u32[]{:S(2)}) collective-permute-start(bf16[192,512]{1,0:T(8,128)(2,1)S(1)} %bitcast.8), channel_id=1, source_target_pairs={{32,1},{33,0},{34,3},{35,2},{36,5},{37,4},{38,7},{39,6},{40,9},{41... | collective-permute-start | bytes 589832 | tf_op jit(solution)/shard_map/ppermute | solution.py:529
  23.5 12.8 %collective-permute-start.6 = (bf16[512,128]{1,0:T(8,128)(2,1)S(1)}, bf16[512,128]{1,0:T(8,128)(2,1)S(1)}, u32[]{:S(2)}, u32[]{:S(2)}) collective-permute-start(bf16[512,128]{1,0:T(8,128)(2,1)S(1)} %get-tuple-element.64.head), channel_id=1, source_target_pairs={{0,1},{1,0},{2,3},{3,2},{4,5},{5,4},{6,7},{7,6},{8,9},{9,8},{10,11... | collective-permute-start | bytes 393224 | tf_op jit(solution)/shard_map/ppermute | solution.py:529
  40.9 11.4 %collective-permute-start.7 = (bf16[512,512]{1,0:T(8,128)(2,1)S(1)}, bf16[512,512]{1,0:T(8,128)(2,1)S(1)}, u32[]{:S(2)}, u32[]{:S(2)}) collective-permute-start(bf16[512,512]{1,0:T(8,128)(2,1)S(1)} %weight_pair.1.own), channel_id=1, source_target_pairs={{0,8},{1,9},{2,10},{3,11},{4,12},{5,13},{6,14},{7,15},{8,0},{9,1},... | collective-permute-start | bytes 1572872 | tf_op jit(solution)/shard_map/ppermute | solution.py:529
  41.6 79.9 %collective-permute-start.18 = (bf16[256,6144]{1,0:T(8,128)(2,1)S(1)}, bf16[256,6144]{1,0:T(8,128)(2,1)S(1)}, u32[]{:S(2)}, u32[]{:S(2)}) collective-permute-start(bf16[256,6144]{1,0:T(8,128)(2,1)S(1)} %bitcast.11), channel_id=1, source_target_pairs={{32,0},{33,1},{34,2},{35,3},{36,4},{37,5},{38,6},{39,7},{40,8},{41... | collective-permute-start | bytes 9437192 | tf_op jit(solution)/shard_map/ppermute | solution.py:529
  45.1 16.1 %collective-permute-start.8 = (bf16[512,512]{1,0:T(8,128)(2,1)S(1)}, bf16[512,512]{1,0:T(8,128)(2,1)S(1)}, u32[]{:S(2)}, u32[]{:S(2)}) collective-permute-start(bf16[512,512]{1,0:T(8,128)(2,1)S(1)} %weight_pair.1.own), channel_id=1, source_target_pairs={{0,24},{1,25},{2,26},{3,27},{4,28},{5,29},{6,30},{7,31},{8,16},{9,... | collective-permute-start | bytes 1572872 | tf_op jit(solution)/shard_map/ppermute | solution.py:529
  46.4 14.9 %collective-permute-start.9 = (bf16[512,512]{1,0:T(8,128)(2,1)S(1)}, bf16[512,512]{1,0:T(8,128)(2,1)S(1)}, u32[]{:S(2)}, u32[]{:S(2)}) collective-permute-start(bf16[512,512]{1,0:T(8,128)(2,1)S(1)} %weight_pair.1.own), channel_id=1, source_target_pairs={{0,16},{1,17},{2,18},{3,19},{4,20},{5,21},{6,22},{7,23},{8,24},{9,... | collective-permute-start | bytes 1572872 | tf_op jit(solution)/shard_map/ppermute | solution.py:529
  51.4 20.4 %collective-permute-start.2 = (bf16[8,120,512]{2,1,0:T(8,128)(2,1)S(1)}, bf16[8,120,512]{2,1,0:T(8,128)(2,1)S(1)}, u32[]{:S(2)}, u32[]{:S(2)}) collective-permute-start(bf16[8,120,512]{2,1,0:T(8,128)(2,1)S(1)} %get-tuple-element.60), channel_id=1, source_target_pairs={{0,24},{1,25},{2,26},{3,27},{4,28},{5,29},{6,30},{7,31},{8,16},{9,... | collective-permute-start | bytes 2949128 | tf_op jit(solution)/shard_map/ppermute | solution.py:529
  52.3 19.5 %collective-permute-start.3 = (bf16[8,120,512]{2,1,0:T(8,128)(2,1)S(1)}, bf16[8,120,512]{2,1,0:T(8,128)(2,1)S(1)}, u32[]{:S(2)}, u32[]{:S(2)}) collective-permute-start(bf16[8,120,512]{2,1,0:T(8,128)(2,1)S(1)} %get-tuple-element.61), channel_id=1, source_target_pairs={{0,8},{1,9},{2,10},{3,11},{4,12},{5,13},{6,14},{7,15},{8,0},{9,1},... | collective-permute-start | bytes 2949128 | tf_op jit(solution)/shard_map/ppermute | solution.py:529
  61.5 14.6 %collective-permute-start.10 = (bf16[4,256,384]{2,1,0:T(8,128)(2,1)S(1)}, bf16[4,256,384]{2,1,0:T(8,128)(2,1)S(1)}, u32[]{:S(2)}, u32[]{:S(2)}) collective-permute-start(bf16[4,256,384]{2,1,0:T(8,128)(2,1)S(1)} %get-tuple-element.83.held_a), channel_id=1, source_target_pairs={{0,2},{1,3},{2,0},{3,1},{4,6},{5,7},{6,4},{7,5},{8,10},{9,11},{10,... | collective-permute-start | bytes 2359304 | tf_op jit(solution)/shard_map/ppermute | solution.py:529
  63.8 15.1 %collective-permute-start.11 = (bf16[4,256,384]{2,1,0:T(8,128)(2,1)S(1)}, bf16[4,256,384]{2,1,0:T(8,128)(2,1)S(1)}, u32[]{:S(2)}, u32[]{:S(2)}) collective-permute-start(bf16[4,256,384]{2,1,0:T(8,128)(2,1)S(1)} %get-tuple-element.84.held_b), channel_id=1, source_target_pairs={{0,6},{1,7},{2,4},{3,5},{4,2},{5,3},{6,0},{7,1},{8,14},{9,15},{10,... | collective-permute-start | bytes 2359304 | tf_op jit(solution)/shard_map/ppermute | solution.py:529
  72.4 45.5 %copy-start.2 = (f32[1,4,128,128]{3,2,1,0:T(8,128)S(1)}, f32[1,4,128,128]{3,2,1,0:T(8,128)}, u32[]{:S(2)}) copy-start(f32[1,4,128,128]{3,2,1,0:T(8,128)} %param.15) | copy-start | bytes 786436
  72.4 45.5 %copy-start.5 = (f32[1,1,192,192]{3,2,1,0:T(8,128)S(1)}, f32[1,1,192,192]{3,2,1,0:T(8,128)}, u32[]{:S(2)}) copy-start(f32[1,1,192,192]{3,2,1,0:T(8,128)} %param.14) | copy-start | bytes 442372
  72.4 45.5 %copy-start.7 = (s32[1,32]{1,0:T(1,128)S(1)}, s32[1,32]{1,0:T(1,128)}, u32[]{:S(2)}) copy-start(s32[1,32]{1,0:T(1,128)} %refs_0_.3) | copy-start | bytes 388
  72.4 10.3 %collective-permute-start.12 = (bf16[608,512]{1,0:T(8,128)(2,1)S(1)}, bf16[608,512]{1,0:T(8,128)(2,1)S(1)}, u32[]{:S(2)}, u32[]{:S(2)}) collective-permute-start(bf16[608,512]{1,0:T(8,128)(2,1)S(1)} %get-tuple-element.73), channel_id=1, source_target_pairs={{0,2},{1,3},{2,0},{3,1},{4,6},{5,7},{6,4},{7,5},{8,10},{9,11},{10,... | collective-permute-start | bytes 1867784 | tf_op jit(solution)/shard_map/ppermute | solution.py:529
  73.0 19.3 %collective-permute-start.13 = (bf16[608,512]{1,0:T(8,128)(2,1)S(1)}, bf16[608,512]{1,0:T(8,128)(2,1)S(1)}, u32[]{:S(2)}, u32[]{:S(2)}) collective-permute-start(bf16[608,512]{1,0:T(8,128)(2,1)S(1)} %get-tuple-element.74), channel_id=1, source_target_pairs={{0,6},{1,7},{2,4},{3,5},{4,2},{5,3},{6,0},{7,1},{8,14},{9,15},{10,... | collective-permute-start | bytes 1867784 | tf_op jit(solution)/shard_map/ppermute | solution.py:529
  76.0 16.2 %collective-permute-start.14 = (bf16[608,512]{1,0:T(8,128)(2,1)S(1)}, bf16[608,512]{1,0:T(8,128)(2,1)S(1)}, u32[]{:S(2)}, u32[]{:S(2)}) collective-permute-start(bf16[608,512]{1,0:T(8,128)(2,1)S(1)} %get-tuple-element.75), channel_id=1, source_target_pairs={{0,4},{1,5},{2,6},{3,7},{4,0},{5,1},{6,2},{7,3},{8,12},{9,13},{10,... | collective-permute-start | bytes 1867784 | tf_op jit(solution)/shard_map/ppermute | solution.py:529
  93.0 15.1 %collective-permute-start.15 = (bf16[2,120,512]{2,1,0:T(8,128)(2,1)S(1)}, bf16[2,120,512]{2,1,0:T(8,128)(2,1)S(1)}, u32[]{:S(2)}, u32[]{:S(2)}) collective-permute-start(bf16[2,120,512]{2,1,0:T(8,128)(2,1)S(1)} %get-tuple-element.77), channel_id=1, source_target_pairs={{0,1},{1,0},{2,3},{3,2},{4,5},{5,4},{6,7},{7,6},{8,9},{9,8},{10,11... | collective-permute-start | bytes 737288 | tf_op jit(solution)/shard_map/ppermute | solution.py:529
  98.9 15.1 %collective-permute-start.16 = (bf16[4,256,384]{2,1,0:T(8,128)(2,1)S(1)}, bf16[4,256,384]{2,1,0:T(8,128)(2,1)S(1)}, u32[]{:S(2)}, u32[]{:S(2)}) collective-permute-start(bf16[4,256,384]{2,1,0:T(8,128)(2,1)S(1)} %collective-permute-done.10.third_a), channel_id=1, source_target_pairs={{0,6},{1,7},{2,4},{3,5},{4,2},{5,3},{6,0},{7,1},{8,14},{9,15},{10,... | collective-permute-start | bytes 2359304 | tf_op jit(solution)/shard_map/ppermute | solution.py:529
  104.0 13.9 %collective-permute-start.17 = (bf16[4,256,384]{2,1,0:T(8,128)(2,1)S(1)}, bf16[4,256,384]{2,1,0:T(8,128)(2,1)S(1)}, u32[]{:S(2)}, u32[]{:S(2)}) collective-permute-start(bf16[4,256,384]{2,1,0:T(8,128)(2,1)S(1)} %collective-permute-done.11.third_b), channel_id=1, source_target_pairs={{0,2},{1,3},{2,0},{3,1},{4,6},{5,7},{6,4},{7,5},{8,10},{9,11},{10,... | collective-permute-start | bytes 2359304 | tf_op jit(solution)/shard_map/ppermute | solution.py:529
  105.9 16.5 %collective-permute-start.19 = (bf16[4,256,384]{2,1,0:T(8,128)(2,1)S(1)}, bf16[4,256,384]{2,1,0:T(8,128)(2,1)S(1)}, u32[]{:S(2)}, u32[]{:S(2)}) collective-permute-start(bf16[4,256,384]{2,1,0:T(8,128)(2,1)S(1)} %get-tuple-element.83.held_a), channel_id=1, source_target_pairs={{0,6},{1,7},{2,4},{3,5},{4,2},{5,3},{6,0},{7,1},{8,14},{9,15},{10,... | collective-permute-start | bytes 2359304 | tf_op jit(solution)/shard_map/ppermute | solution.py:529
  108.1 18.2 %collective-permute-start.20 = (bf16[4,256,384]{2,1,0:T(8,128)(2,1)S(1)}, bf16[4,256,384]{2,1,0:T(8,128)(2,1)S(1)}, u32[]{:S(2)}, u32[]{:S(2)}) collective-permute-start(bf16[4,256,384]{2,1,0:T(8,128)(2,1)S(1)} %get-tuple-element.84.held_b), channel_id=1, source_target_pairs={{0,2},{1,3},{2,0},{3,1},{4,6},{5,7},{6,4},{7,5},{8,10},{9,11},{10,... | collective-permute-start | bytes 2359304 | tf_op jit(solution)/shard_map/ppermute | solution.py:529

commit v3 on v2

--- a/solution.py
+++ b/solution.py
@@ -470,8 +470,9 @@
     return cols, (resid_ref[:, cols].astype(jnp.float32) + branch).astype(jnp.bfloat16)
 
 
-def passed_kernel(held_a, held_b, third_a, third_b, fourth_a, fourth_b, k_ref, resid_ref, out_ref):
-    groups = ((held_a, held_b), (third_a, fourth_b), (fourth_a, third_b))
+def passed_kernel(held_a, held_b, third_a, third_b, last_a, last_b, k_ref, resid_ref, out_ref):
+    fourth_a, fourth_b, both_a, both_b = last_a.at[:4], last_b.at[:4], last_a.at[4:], last_b.at[4:]
+    groups = ((held_a, held_b), (third_a, fourth_b), (fourth_a, third_b), (both_a, both_b))
     for ring, pieces in enumerate(groups):
         for i in range(4):
             cols, block = passed_block(k_ref, resid_ref, pieces, i, ring)
@@ -488,41 +489,10 @@
         out_specs=vmem,
         compiler_params=pltpu.CompilerParams(vmem_limit_bytes=24 * 2**20),
         cost_estimate=pl.CostEstimate(
-            flops=2 * 256 * 4608 * 512, bytes_accessed=12 * 2**20, transcendentals=0
+            flops=2 * 256 * 6144 * 512, bytes_accessed=12 * 2**20, transcendentals=0
         ),
         name="passed_grad",
     )(*parts)
-
-
-def passed_rest_kernel(both_a, both_b, k_ref, resid_ref, begun, out_ref, blocks, sems):
-    copies = []
-    for i in range(4):
-        cols, blocks[i] = passed_block(k_ref, resid_ref, (both_a, both_b), i, 3)
-        copies.append(pltpu.make_async_copy(blocks.at[i], out_ref.at[:, cols], sems.at[i]))
-        copies[i].start()
-    for copy in copies:
-        copy.wait()
-
-
-def passed_rest(both_a, both_b, key_pre, resid, begun):
-    vmem = pl.BlockSpec(memory_space=pltpu.VMEM)
-    hbm = pl.BlockSpec(memory_space=pl.ANY)
-    return pl.pallas_call(
-        passed_rest_kernel,
-        out_shape=jax.ShapeDtypeStruct(resid.shape, jnp.bfloat16),
-        in_specs=[vmem] * 4 + [hbm],
-        out_specs=hbm,
-        input_output_aliases={4: 0},
-        scratch_shapes=[
-            pltpu.VMEM((4, resid.shape[0], PAIR), jnp.bfloat16),
-            pltpu.SemaphoreType.DMA((4,)),
-        ],
-        compiler_params=pltpu.CompilerParams(vmem_limit_bytes=24 * 2**20),
-        cost_estimate=pl.CostEstimate(
-            flops=2 * 256 * 1536 * 512, bytes_accessed=4 * 2**20, transcendentals=0
-        ),
-        name="passed_rest",
-    )(both_a, both_b, key_pre, resid, begun)
 
 
 def hop(block, route):
@@ -548,6 +518,7 @@
     far_a, far_b, near_a, near_b = kept_products(order, layer_inputs, key_pre, turned)
     crossed = hop(weight, back_route(True))
     other = hop(head, flip_route(((Z,), (Z,))))
+    crossed, other, far_a, near_a = tie(crossed, other, far_a, near_a)
     pair = weight_pair(straight, crossed, head, other)
     near = [pair] + [hop(pair, ring_route(0, which)) for which in (1, 2, 3)]
     resid_in, pair = tie(resid_grad[0], pair)
@@ -564,13 +535,11 @@
     own, *sent = ring_sums(near_a, first[0], second[0], near_b, first[1], second[1], head)
     ring = [hop(sent[i], ring_route(1, i + 1)) for i in range(3)]
     own, held[0], held[1], third[0], third[1], _, _, _ = tie(own, *held, *third, *ring)
-    fourth = [hop(held[s], step_route(WEIGHTS, s, 3)) for s in range(2)]
-    both = [hop(third[s], step_route(WEIGHTS, s, 3)) for s in range(2)]
+    more = [jnp.concatenate([held[s], third[s]], axis=0) for s in range(2)]
+    fourth = [hop(more[s], step_route(WEIGHTS, s, 3)) for s in range(2)]
     keep, send, head_grams = last_sums(total, own, head, *ring)
     last = hop(send, flip_route(((Z,), (Z,))))
-    begun = passed_grad(*held, *third, *fourth, straight, resid)
-    last, both[0], both[1] = tie(last, *both)
-    passed = passed_rest(*both, straight, resid, begun)
+    passed = passed_grad(*held, *third, *fourth, straight, resid)
     precond, gram = finished(total, slot_block, keep, last, inv_input[0], inv_head[0])
     return (passed[None], precond[None], gram[None, None], head_grams)
 

time: 132 us -> 124 us (0.939)
  starting transfers between devices: 53.1 us -> 44.7 us
    ppermute x21 -> x19, starting transfers between devices: 53.1 us -> 44.7 us  [hop(): return lax.ppermute(block, AXES, route)]
    pallas_call x1 -> x0, Pallas kernels: 1.44 us -> none  [passed_rest(): pl.pallas_call(passed_rest_kernel, out_shape=jax.ShapeDtypeStruct(resid.s...]
    ppermute x21 -> x19, waiting for transfers between devices: 52.4 us -> 52.7 us  [hop(): return lax.ppermute(block, AXES, route)]
  transfers between devices with their start and end apart: 21 -> 19, of which waited for: 11 -> 10; matrix products, arithmetic and copies ran while one was open for 0% -> 0% of each run, Pallas kernels for 7% -> 7%
where the time goes in v3:
time: 124 us; the launch traced here: 123 us
  waiting for transfers between devices  52.7 us (42%)
  starting transfers between devices  44.7 us (36%)
  Pallas kernels  19.1 us (15%)
  local copies, waits for them, and re-layouts  5.09 us (4%)
    ppermute x19, waiting for transfers between devices, hop(): return lax.ppermute(block, AXES, route)  52.7 us
    ppermute x19, starting transfers between devices, hop(): return lax.ppermute(block, AXES, route)  44.7 us
    pallas_call x2, Pallas kernels, products(): pl.pallas_call(kernel, out_shape=out_shape, in_specs=[smem] + [vmem] * (l...  7.17 us
    unnamed x20, local copies, waits for them, and re-layouts  5.09 us
    pallas_call x1, Pallas kernels, passed_grad(): pl.pallas_call(passed_kernel, out_shape=jax.ShapeDtypeStruct(resid.shape,...  4.06 us
    pallas_call x1, Pallas kernels, finished(): pl.pallas_call(kernel, out_shape=(jax.ShapeDtypeStruct((1, BLK, KO), jnp....  3.56 us
  transfers between devices with their start and end apart: 19, of which 10 were waited for; matrix products, arithmetic and copies ran while one was open for 0% of the time, Pallas kernels for 7%

profile of v3, /device:TPU:96, one launch (start us, length us, event | category | flops | bytes accessed | tf_op | source)
XLA Modules:
  0.0 122.8 jit_solution(18365898509655916512)
XLA Ops:
  0.6 0.9 copy-done.1
  1.6 0.9 copy-done.3
  2.5 0.7 copy-done.6
  3.2 0.7 copy-done.8
  3.8 2.0 %keys.1 = (bf16[256,512]{1,0:T(8,128)(2,1)S(1)}, bf16[512,128]{1,0:T(8,128)(2,1)S(1)}, s32[2,32]{1,0:T(2,128)S(1)}, bf16[448,512]{1,0:T(8,128)(2,1)S(1)}) custom-call(s32[1,32]{1,0:T(1,128)S(1)} %copy-done.6, s32[1,2]{1,0:T(1,128)S(1)} %copy-done.8, bf16[1,256,512]{2,1,0:T(8,128)(2,1)S(1)} %copy-done.1, bf16[1,192,512]{2,1,0:T(8,128)(2,1)S(1)} %copy-done.3), custom_call_target="tpu_custom_call" | custom-call | tf_op jit(solution)/shard_map/keys/pallas_call | solution.py:171
  5.9 0.0 copy-start
  5.9 1.9 %copy-done = bf16[1,256,6144]{2,1,0:T(8,128)(2,1)S(1)} copy-done((bf16[1,256,6144]{2,1,0:T(8,128)(2,1)S(1)}, bf16[1,256,6144]{2,1,0:T(8,128)(2,1)}, u32[]{:S(2)}) %copy-start) | copy-done | bytes 3145752
  7.8 4.0 %sent_products.1 = (bf16[16,120,512]{2,1,0:T(8,128)(2,1)S(1)}, bf16[16,120,512]{2,1,0:T(8,128)(2,1)S(1)}, bf16[6144,256]{1,0:T(8,128)(2,1)S(1)}) custom-call(s32[2,32]{1,0:T(2,128)S(1)} %get-tuple-element.48.order_ref, bf16[1,256,6144]{2,1,0:T(8,128)(2,1)S(1)} %copy-done, bf16[256,512]{1,0:T(8,128)(2,1)S(1)} %get-tuple-element.49.key_ref), custom_call_target="tpu_custom_call" | custom-call | flops 1107296256 | bytes 10485760 | tf_op jit(solution)/shard_map/sent_products/pallas_call | solution.py:241
  11.8 1.6 %collective-permute-start.2 = (bf16[16,120,512]{2,1,0:T(8,128)(2,1)S(1)}, bf16[16,120,512]{2,1,0:T(8,128)(2,1)S(1)}, u32[]{:S(2)}, u32[]{:S(2)}) collective-permute-start(bf16[16,120,512]{2,1,0:T(8,128)(2,1)S(1)} %get-tuple-element.59), channel_id=1, source_target_pairs={{0,8},{1,9},{2,10},{3,11},{4,12},{5,13},{6,14},{7,15},{8,0},{9,1},... | collective-permute-start | bytes 5898248 | tf_op jit(solution)/shard_map/ppermute | solution.py:499
  13.4 2.1 %collective-permute-start.3 = (bf16[16,120,512]{2,1,0:T(8,128)(2,1)S(1)}, bf16[16,120,512]{2,1,0:T(8,128)(2,1)S(1)}, u32[]{:S(2)}, u32[]{:S(2)}) collective-permute-start(bf16[16,120,512]{2,1,0:T(8,128)(2,1)S(1)} %get-tuple-element.64), channel_id=1, source_target_pairs={{0,24},{1,25},{2,26},{3,27},{4,28},{5,29},{6,30},{7,31},{8,16},{9,... | collective-permute-start | bytes 5898248 | tf_op jit(solution)/shard_map/ppermute | solution.py:499
  15.5 1.9 %collective-permute-start.6 = (bf16[448,512]{1,0:T(8,128)(2,1)S(1)}, bf16[448,512]{1,0:T(8,128)(2,1)S(1)}, u32[]{:S(2)}, u32[]{:S(2)}) collective-permute-start(bf16[448,512]{1,0:T(8,128)(2,1)S(1)} %get-tuple-element.67), channel_id=1, source_target_pairs={{32,0},{33,1},{34,2},{35,3},{36,4},{37,5},{38,6},{39,7},{40,8},{41... | collective-permute-start | bytes 1376264 | tf_op jit(solution)/shard_map/ppermute | solution.py:499
  17.4 6.0 %collective-permute-start = (bf16[192,512]{1,0:T(8,128)(2,1)S(1)}, bf16[192,512]{1,0:T(8,128)(2,1)S(1)}, u32[]{:S(2)}, u32[]{:S(2)}) collective-permute-start(bf16[192,512]{1,0:T(8,128)(2,1)S(1)} %bitcast.8), channel_id=1, source_target_pairs={{32,1},{33,0},{34,3},{35,2},{36,5},{37,4},{38,7},{39,6},{40,9},{41... | collective-permute-start | bytes 589832 | tf_op jit(solution)/shard_map/ppermute | solution.py:499
  23.5 0.6 collective-permute-start.1
  24.1 3.1 %kept_products.1 = (f32[8,120,512]{2,1,0:T(8,128)S(1)}, f32[8,120,512]{2,1,0:T(8,128)S(1)}, f32[8,120,512]{2,1,0:T(8,128)S(1)}, f32[8,120,512]{2,1,0:T(8,128)S(1)}) custom-call(s32[2,32]{1,0:T(2,128)S(1)} %get-tuple-element.48.order_ref, bf16[1,256,6144]{2,1,0:T(8,128)(2,1)S(1)} %copy-done, bf16[256,512]{1,0:T(8,128)(2,1)S(1)} %get-tuple-element.49.key_ref, ...), custom_call_target="tpu_custom_call" | custom-call | flops 1107296256 | bytes 10485760 | tf_op jit(solution)/shard_map/kept_products/pallas_call | solution.py:241
  27.2 9.1 %collective-permute-done.1.other = bf16[512,128]{1,0:T(8,128)(2,1)S(1)} collective-permute-done((bf16[512,128]{1,0:T(8,128)(2,1)S(1)}, bf16[512,128]{1,0:T(8,128)(2,1)S(1)}, u32[]{:S(2)}, u32[]{:S(2)}) %collective-permute-start.1) | collective-permute-done | bytes 131104 | tf_op jit(solution)/shard_map/ppermute | solution.py:499
  36.3 4.4 %collective-permute-done.crossed = bf16[192,512]{1,0:T(8,128)(2,1)S(1)} collective-permute-done((bf16[192,512]{1,0:T(8,128)(2,1)S(1)}, bf16[192,512]{1,0:T(8,128)(2,1)S(1)}, u32[]{:S(2)}, u32[]{:S(2)}) %collective-permute-start) | collective-permute-done | bytes 196640 | tf_op jit(solution)/shard_map/ppermute | solution.py:499
  40.7 0.2 weight_pair.1.own
  40.9 0.7 collective-permute-start.7
  41.6 1.1 collective-permute-start.8
  42.7 2.4 %collective-permute-start.9 = (bf16[512,512]{1,0:T(8,128)(2,1)S(1)}, bf16[512,512]{1,0:T(8,128)(2,1)S(1)}, u32[]{:S(2)}, u32[]{:S(2)}) collective-permute-start(bf16[512,512]{1,0:T(8,128)(2,1)S(1)} %weight_pair.1.own), channel_id=1, source_target_pairs={{0,16},{1,17},{2,18},{3,19},{4,20},{5,21},{6,22},{7,23},{8,24},{9,... | collective-permute-start | bytes 1572872 | tf_op jit(solution)/shard_map/ppermute | solution.py:499
  45.1 0.4 halved.1
  45.5 1.7 %collective-permute-start.4 = (bf16[8,120,512]{2,1,0:T(8,128)(2,1)S(1)}, bf16[8,120,512]{2,1,0:T(8,128)(2,1)S(1)}, u32[]{:S(2)}, u32[]{:S(2)}) collective-permute-start(bf16[8,120,512]{2,1,0:T(8,128)(2,1)S(1)} %get-tuple-element.65), channel_id=1, source_target_pairs={{0,24},{1,25},{2,26},{3,27},{4,28},{5,29},{6,30},{7,31},{8,16},{9,... | collective-permute-start | bytes 2949128 | tf_op jit(solution)/shard_map/ppermute | solution.py:499
  47.2 2.9 %collective-permute-done.7.near_a = bf16[512,512]{1,0:T(8,128)(2,1)S(1)} collective-permute-done((bf16[512,512]{1,0:T(8,128)(2,1)S(1)}, bf16[512,512]{1,0:T(8,128)(2,1)S(1)}, u32[]{:S(2)}, u32[]{:S(2)}) %collective-permute-start.7) | collective-permute-done | bytes 524320 | tf_op jit(solution)/shard_map/ppermute | solution.py:499
  50.1 7.4 %collective-permute-done.8.near_b = bf16[512,512]{1,0:T(8,128)(2,1)S(1)} collective-permute-done((bf16[512,512]{1,0:T(8,128)(2,1)S(1)}, bf16[512,512]{1,0:T(8,128)(2,1)S(1)}, u32[]{:S(2)}, u32[]{:S(2)}) %collective-permute-start.8) | collective-permute-done | bytes 524320 | tf_op jit(solution)/shard_map/ppermute | solution.py:499
  57.6 0.2 stacked.1
  57.8 3.5 %collective-permute-start.10 = (bf16[4,256,384]{2,1,0:T(8,128)(2,1)S(1)}, bf16[4,256,384]{2,1,0:T(8,128)(2,1)S(1)}, u32[]{:S(2)}, u32[]{:S(2)}) collective-permute-start(bf16[4,256,384]{2,1,0:T(8,128)(2,1)S(1)} %get-tuple-element.81.held_a), channel_id=1, source_target_pairs={{0,2},{1,3},{2,0},{3,1},{4,6},{5,7},{6,4},{7,5},{8,10},{9,11},{10,... | collective-permute-start | bytes 2359304 | tf_op jit(solution)/shard_map/ppermute | solution.py:499
  61.3 1.9 %collective-permute-start.17 = (bf16[256,6144]{1,0:T(8,128)(2,1)S(1)}, bf16[256,6144]{1,0:T(8,128)(2,1)S(1)}, u32[]{:S(2)}, u32[]{:S(2)}) collective-permute-start(bf16[256,6144]{1,0:T(8,128)(2,1)S(1)} %bitcast.11), channel_id=1, source_target_pairs={{32,0},{33,1},{34,2},{35,3},{36,4},{37,5},{38,6},{39,7},{40,8},{41... | collective-permute-start | bytes 9437192 | tf_op jit(solution)/shard_map/ppermute | solution.py:499
  63.2 4.1 %collective-permute-start.11 = (bf16[4,256,384]{2,1,0:T(8,128)(2,1)S(1)}, bf16[4,256,384]{2,1,0:T(8,128)(2,1)S(1)}, u32[]{:S(2)}, u32[]{:S(2)}) collective-permute-start(bf16[4,256,384]{2,1,0:T(8,128)(2,1)S(1)} %get-tuple-element.82.held_b), channel_id=1, source_target_pairs={{0,6},{1,7},{2,4},{3,5},{4,2},{5,3},{6,0},{7,1},{8,14},{9,15},{10,... | collective-permute-start | bytes 2359304 | tf_op jit(solution)/shard_map/ppermute | solution.py:499
  67.3 0.8 collective-permute-done.4.got_a
  68.1 0.6 ring_sums.1
  68.7 1.7 %collective-permute-start.12 = (bf16[608,512]{1,0:T(8,128)(2,1)S(1)}, bf16[608,512]{1,0:T(8,128)(2,1)S(1)}, u32[]{:S(2)}, u32[]{:S(2)}) collective-permute-start(bf16[608,512]{1,0:T(8,128)(2,1)S(1)} %get-tuple-element.78), channel_id=1, source_target_pairs={{0,2},{1,3},{2,0},{3,1},{4,6},{5,7},{6,4},{7,5},{8,10},{9,11},{10,... | collective-permute-start | bytes 1867784 | tf_op jit(solution)/shard_map/ppermute | solution.py:499
  70.4 2.2 %collective-permute-start.13 = (bf16[608,512]{1,0:T(8,128)(2,1)S(1)}, bf16[608,512]{1,0:T(8,128)(2,1)S(1)}, u32[]{:S(2)}, u32[]{:S(2)}) collective-permute-start(bf16[608,512]{1,0:T(8,128)(2,1)S(1)} %get-tuple-element.79), channel_id=1, source_target_pairs={{0,6},{1,7},{2,4},{3,5},{4,2},{5,3},{6,0},{7,1},{8,14},{9,15},{10,... | collective-permute-start | bytes 1867784 | tf_op jit(solution)/shard_map/ppermute | solution.py:499
  72.6 2.3 %collective-permute-start.14 = (bf16[608,512]{1,0:T(8,128)(2,1)S(1)}, bf16[608,512]{1,0:T(8,128)(2,1)S(1)}, u32[]{:S(2)}, u32[]{:S(2)}) collective-permute-start(bf16[608,512]{1,0:T(8,128)(2,1)S(1)} %get-tuple-element.80), channel_id=1, source_target_pairs={{0,4},{1,5},{2,6},{3,7},{4,0},{5,1},{6,2},{7,3},{8,12},{9,13},{10,... | collective-permute-start | bytes 1867784 | tf_op jit(solution)/shard_map/ppermute | solution.py:499
  74.9 3.4 %collective-permute-done.11.third_b = bf16[4,256,384]{2,1,0:T(8,128)(2,1)S(1)} collective-permute-done((bf16[4,256,384]{2,1,0:T(8,128)(2,1)S(1)}, bf16[4,256,384]{2,1,0:T(8,128)(2,1)S(1)}, u32[]{:S(2)}, u32[]{:S(2)}) %collective-permute-start.11) | collective-permute-done | bytes 786464 | tf_op jit(solution)/shard_map/ppermute | solution.py:499
  78.3 0.8 collective-permute-done.12.refs_2_
  79.1 12.6 %collective-permute-done.13.refs_3_ = bf16[608,512]{1,0:T(8,128)(2,1)S(1)} collective-permute-done((bf16[608,512]{1,0:T(8,128)(2,1)S(1)}, bf16[608,512]{1,0:T(8,128)(2,1)S(1)}, u32[]{:S(2)}, u32[]{:S(2)}) %collective-permute-start.13) | collective-permute-done | bytes 622624 | tf_op jit(solution)/shard_map/ppermute | solution.py:499
  91.6 0.2 pad_maximum_fusion
  91.8 4.3 %collective-permute-start.15 = (bf16[8,256,384]{2,1,0:T(8,128)(2,1)S(1)}, bf16[8,256,384]{2,1,0:T(8,128)(2,1)S(1)}, u32[]{:S(2)}, u32[]{:S(2)}) collective-permute-start(bf16[8,256,384]{2,1,0:T(8,128)(2,1)S(1)} %pad_maximum_fusion), channel_id=1, source_target_pairs={{0,6},{1,7},{2,4},{3,5},{4,2},{5,3},{6,0},{7,1},{8,14},{9,15},{10,... | collective-permute-start | bytes 4718600 | tf_op jit(solution)/shard_map/ppermute | solution.py:499
  96.1 0.2 pad_maximum_fusion.1
  96.3 0.0 copy-start.2
  96.3 0.0 copy-start.7
  96.3 2.1 %collective-permute-start.16 = (bf16[8,256,384]{2,1,0:T(8,128)(2,1)S(1)}, bf16[8,256,384]{2,1,0:T(8,128)(2,1)S(1)}, u32[]{:S(2)}, u32[]{:S(2)}) collective-permute-start(bf16[8,256,384]{2,1,0:T(8,128)(2,1)S(1)} %pad_maximum_fusion.1), channel_id=1, source_target_pairs={{0,2},{1,3},{2,0},{3,1},{4,6},{5,7},{6,4},{7,5},{8,10},{9,11},{10,... | collective-permute-start | bytes 4718600 | tf_op jit(solution)/shard_map/ppermute | solution.py:499
  98.4 0.8 last_sums.1
  99.2 4.7 %collective-permute-start.18 = (bf16[2,120,512]{2,1,0:T(8,128)(2,1)S(1)}, bf16[2,120,512]{2,1,0:T(8,128)(2,1)S(1)}, u32[]{:S(2)}, u32[]{:S(2)}) collective-permute-start(bf16[2,120,512]{2,1,0:T(8,128)(2,1)S(1)} %get-tuple-element.88), channel_id=1, source_target_pairs={{0,1},{1,0},{2,3},{3,2},{4,5},{5,4},{6,7},{7,6},{8,9},{9,8},{10,11... | collective-permute-start | bytes 737288 | tf_op jit(solution)/shard_map/ppermute | solution.py:499
  103.8 9.8 %collective-permute-done.18.refs_2_ = bf16[2,120,512]{2,1,0:T(8,128)(2,1)S(1)} collective-permute-done((bf16[2,120,512]{2,1,0:T(8,128)(2,1)S(1)}, bf16[2,120,512]{2,1,0:T(8,128)(2,1)S(1)}, u32[]{:S(2)}, u32[]{:S(2)}) %collective-permute-start.18) | collective-permute-done | bytes 245792 | tf_op jit(solution)/shard_map/ppermute | solution.py:499
  113.7 3.6 %finish.1 = (f32[1,192,512]{2,1,0:T(8,128)}, f32[192,192]{1,0:T(8,128)}) custom-call(s32[1,32]{1,0:T(1,128)S(1)} %copy-done.7, f32[2,120,512]{2,1,0:T(8,128)S(1)} %get-tuple-element.87.refs_1_, bf16[2,120,512]{2,1,0:T(8,128)(2,1)S(1)} %collective-permute-done.18.refs_2_, f32[1,192,192]{2,1,0:T(8,128)S(1)} %bitcast.9, f32[4,128,128]{2,1,0:T(8,128)S(1)} %bitcast.7), custom_call_target="tpu_custom_call" | custom-call | tf_op jit(solution)/shard_map/finish/pallas_call | solution.py:446
  117.2 1.5 %collective-permute-done.16.last_b = bf16[8,256,384]{2,1,0:T(8,128)(2,1)S(1)} collective-permute-done((bf16[8,256,384]{2,1,0:T(8,128)(2,1)S(1)}, bf16[8,256,384]{2,1,0:T(8,128)(2,1)S(1)}, u32[]{:S(2)}, u32[]{:S(2)}) %collective-permute-start.16) | collective-permute-done | bytes 1572896 | tf_op jit(solution)/shard_map/ppermute | solution.py:499
  118.8 4.1 %passed_grad.1 = bf16[256,6144]{1,0:T(8,128)(2,1)} custom-call(bf16[4,256,384]{2,1,0:T(8,128)(2,1)S(1)} %get-tuple-element.81.held_a, bf16[4,256,384]{2,1,0:T(8,128)(2,1)S(1)} %get-tuple-element.82.held_b, bf16[4,256,384]{2,1,0:T(8,128)(2,1)S(1)} %collective-permute-done.10.third_a, bf16[4,256,384]{2,1,0:T(8,128)(2,1)S(1)} %collective-permute-done.11.third_b, ...), custom_call_target="tpu_custom_call" | custom-call | flops 1610612736 | bytes 12582912 | tf_op jit(solution)/shard_map/passed_grad/pallas_call | solution.py:485
  (22 shorter events, 0.1 us)
Async XLA Ops:
  0.6 1.0 copy-start.1
  1.6 0.9 copy-start.3
  2.5 0.7 copy-start.6
  3.2 0.7 copy-start.8
  5.9 1.9 %copy-start = (bf16[1,256,6144]{2,1,0:T(8,128)(2,1)S(1)}, bf16[1,256,6144]{2,1,0:T(8,128)(2,1)}, u32[]{:S(2)}) copy-start(bf16[1,256,6144]{2,1,0:T(8,128)(2,1)} %x_ref.3) | copy-start | bytes 9437188
  7.8 9.6 %copy-start.4 = (bf16[1,192,512]{2,1,0:T(8,128)(2,1)S(1)}, bf16[1,192,512]{2,1,0:T(8,128)(2,1)}, u32[]{:S(2)}) copy-start(bf16[1,192,512]{2,1,0:T(8,128)(2,1)} %refs_3_.1) | copy-start | bytes 589828
  11.8 33.3 %collective-permute-start.2 = (bf16[16,120,512]{2,1,0:T(8,128)(2,1)S(1)}, bf16[16,120,512]{2,1,0:T(8,128)(2,1)S(1)}, u32[]{:S(2)}, u32[]{:S(2)}) collective-permute-start(bf16[16,120,512]{2,1,0:T(8,128)(2,1)S(1)} %get-tuple-element.59), channel_id=1, source_target_pairs={{0,8},{1,9},{2,10},{3,11},{4,12},{5,13},{6,14},{7,15},{8,0},{9,1},... | collective-permute-start | bytes 5898248 | tf_op jit(solution)/shard_map/ppermute | solution.py:499
  13.4 31.7 %collective-permute-start.3 = (bf16[16,120,512]{2,1,0:T(8,128)(2,1)S(1)}, bf16[16,120,512]{2,1,0:T(8,128)(2,1)S(1)}, u32[]{:S(2)}, u32[]{:S(2)}) collective-permute-start(bf16[16,120,512]{2,1,0:T(8,128)(2,1)S(1)} %get-tuple-element.64), channel_id=1, source_target_pairs={{0,24},{1,25},{2,26},{3,27},{4,28},{5,29},{6,30},{7,31},{8,16},{9,... | collective-permute-start | bytes 5898248 | tf_op jit(solution)/shard_map/ppermute | solution.py:499
  15.5 25.2 %collective-permute-start.6 = (bf16[448,512]{1,0:T(8,128)(2,1)S(1)}, bf16[448,512]{1,0:T(8,128)(2,1)S(1)}, u32[]{:S(2)}, u32[]{:S(2)}) collective-permute-start(bf16[448,512]{1,0:T(8,128)(2,1)S(1)} %get-tuple-element.67), channel_id=1, source_target_pairs={{32,0},{33,1},{34,2},{35,3},{36,4},{37,5},{38,6},{39,7},{40,8},{41... | collective-permute-start | bytes 1376264 | tf_op jit(solution)/shard_map/ppermute | solution.py:499
  17.4 23.3 %collective-permute-start = (bf16[192,512]{1,0:T(8,128)(2,1)S(1)}, bf16[192,512]{1,0:T(8,128)(2,1)S(1)}, u32[]{:S(2)}, u32[]{:S(2)}) collective-permute-start(bf16[192,512]{1,0:T(8,128)(2,1)S(1)} %bitcast.8), channel_id=1, source_target_pairs={{32,1},{33,0},{34,3},{35,2},{36,5},{37,4},{38,7},{39,6},{40,9},{41... | collective-permute-start | bytes 589832 | tf_op jit(solution)/shard_map/ppermute | solution.py:499
  23.5 12.9 %collective-permute-start.1 = (bf16[512,128]{1,0:T(8,128)(2,1)S(1)}, bf16[512,128]{1,0:T(8,128)(2,1)S(1)}, u32[]{:S(2)}, u32[]{:S(2)}) collective-permute-start(bf16[512,128]{1,0:T(8,128)(2,1)S(1)} %get-tuple-element.54.head), channel_id=1, source_target_pairs={{0,1},{1,0},{2,3},{3,2},{4,5},{5,4},{6,7},{7,6},{8,9},{9,8},{10,11... | collective-permute-start | bytes 393224 | tf_op jit(solution)/shard_map/ppermute | solution.py:499
  40.9 9.3 %collective-permute-start.7 = (bf16[512,512]{1,0:T(8,128)(2,1)S(1)}, bf16[512,512]{1,0:T(8,128)(2,1)S(1)}, u32[]{:S(2)}, u32[]{:S(2)}) collective-permute-start(bf16[512,512]{1,0:T(8,128)(2,1)S(1)} %weight_pair.1.own), channel_id=1, source_target_pairs={{0,8},{1,9},{2,10},{3,11},{4,12},{5,13},{6,14},{7,15},{8,0},{9,1},... | collective-permute-start | bytes 1572872 | tf_op jit(solution)/shard_map/ppermute | solution.py:499
  41.6 16.0 %collective-permute-start.8 = (bf16[512,512]{1,0:T(8,128)(2,1)S(1)}, bf16[512,512]{1,0:T(8,128)(2,1)S(1)}, u32[]{:S(2)}, u32[]{:S(2)}) collective-permute-start(bf16[512,512]{1,0:T(8,128)(2,1)S(1)} %weight_pair.1.own), channel_id=1, source_target_pairs={{0,24},{1,25},{2,26},{3,27},{4,28},{5,29},{6,30},{7,31},{8,16},{9,... | collective-permute-start | bytes 1572872 | tf_op jit(solution)/shard_map/ppermute | solution.py:499
  42.7 14.9 %collective-permute-start.9 = (bf16[512,512]{1,0:T(8,128)(2,1)S(1)}, bf16[512,512]{1,0:T(8,128)(2,1)S(1)}, u32[]{:S(2)}, u32[]{:S(2)}) collective-permute-start(bf16[512,512]{1,0:T(8,128)(2,1)S(1)} %weight_pair.1.own), channel_id=1, source_target_pairs={{0,16},{1,17},{2,18},{3,19},{4,20},{5,21},{6,22},{7,23},{8,24},{9,... | collective-permute-start | bytes 1572872 | tf_op jit(solution)/shard_map/ppermute | solution.py:499
  45.1 16.2 %copy-start.9 = (bf16[1,256,6144]{2,1,0:T(8,128)(2,1)S(1)}, bf16[1,256,6144]{2,1,0:T(8,128)(2,1)}, u32[]{:S(2)}) copy-start(bf16[1,256,6144]{2,1,0:T(8,128)(2,1)} %param.9) | copy-start | bytes 9437188
  45.5 22.6 %collective-permute-start.4 = (bf16[8,120,512]{2,1,0:T(8,128)(2,1)S(1)}, bf16[8,120,512]{2,1,0:T(8,128)(2,1)S(1)}, u32[]{:S(2)}, u32[]{:S(2)}) collective-permute-start(bf16[8,120,512]{2,1,0:T(8,128)(2,1)S(1)} %get-tuple-element.65), channel_id=1, source_target_pairs={{0,24},{1,25},{2,26},{3,27},{4,28},{5,29},{6,30},{7,31},{8,16},{9,... | collective-permute-start | bytes 2949128 | tf_op jit(solution)/shard_map/ppermute | solution.py:499
  47.2 20.9 %collective-permute-start.5 = (bf16[8,120,512]{2,1,0:T(8,128)(2,1)S(1)}, bf16[8,120,512]{2,1,0:T(8,128)(2,1)S(1)}, u32[]{:S(2)}, u32[]{:S(2)}) collective-permute-start(bf16[8,120,512]{2,1,0:T(8,128)(2,1)S(1)} %get-tuple-element.66), channel_id=1, source_target_pairs={{0,8},{1,9},{2,10},{3,11},{4,12},{5,13},{6,14},{7,15},{8,0},{9,1},... | collective-permute-start | bytes 2949128 | tf_op jit(solution)/shard_map/ppermute | solution.py:499
  57.8 14.8 %collective-permute-start.10 = (bf16[4,256,384]{2,1,0:T(8,128)(2,1)S(1)}, bf16[4,256,384]{2,1,0:T(8,128)(2,1)S(1)}, u32[]{:S(2)}, u32[]{:S(2)}) collective-permute-start(bf16[4,256,384]{2,1,0:T(8,128)(2,1)S(1)} %get-tuple-element.81.held_a), channel_id=1, source_target_pairs={{0,2},{1,3},{2,0},{3,1},{4,6},{5,7},{6,4},{7,5},{8,10},{9,11},{10,... | collective-permute-start | bytes 2359304 | tf_op jit(solution)/shard_map/ppermute | solution.py:499
  61.3 56.0 %collective-permute-start.17 = (bf16[256,6144]{1,0:T(8,128)(2,1)S(1)}, bf16[256,6144]{1,0:T(8,128)(2,1)S(1)}, u32[]{:S(2)}, u32[]{:S(2)}) collective-permute-start(bf16[256,6144]{1,0:T(8,128)(2,1)S(1)} %bitcast.11), channel_id=1, source_target_pairs={{32,0},{33,1},{34,2},{35,3},{36,4},{37,5},{38,6},{39,7},{40,8},{41... | collective-permute-start | bytes 9437192 | tf_op jit(solution)/shard_map/ppermute | solution.py:499
  63.2 15.1 %collective-permute-start.11 = (bf16[4,256,384]{2,1,0:T(8,128)(2,1)S(1)}, bf16[4,256,384]{2,1,0:T(8,128)(2,1)S(1)}, u32[]{:S(2)}, u32[]{:S(2)}) collective-permute-start(bf16[4,256,384]{2,1,0:T(8,128)(2,1)S(1)} %get-tuple-element.82.held_b), channel_id=1, source_target_pairs={{0,6},{1,7},{2,4},{3,5},{4,2},{5,3},{6,0},{7,1},{8,14},{9,15},{10,... | collective-permute-start | bytes 2359304 | tf_op jit(solution)/shard_map/ppermute | solution.py:499
  68.7 10.3 %collective-permute-start.12 = (bf16[608,512]{1,0:T(8,128)(2,1)S(1)}, bf16[608,512]{1,0:T(8,128)(2,1)S(1)}, u32[]{:S(2)}, u32[]{:S(2)}) collective-permute-start(bf16[608,512]{1,0:T(8,128)(2,1)S(1)} %get-tuple-element.78), channel_id=1, source_target_pairs={{0,2},{1,3},{2,0},{3,1},{4,6},{5,7},{6,4},{7,5},{8,10},{9,11},{10,... | collective-permute-start | bytes 1867784 | tf_op jit(solution)/shard_map/ppermute | solution.py:499
  70.4 21.2 %collective-permute-start.13 = (bf16[608,512]{1,0:T(8,128)(2,1)S(1)}, bf16[608,512]{1,0:T(8,128)(2,1)S(1)}, u32[]{:S(2)}, u32[]{:S(2)}) collective-permute-start(bf16[608,512]{1,0:T(8,128)(2,1)S(1)} %get-tuple-element.79), channel_id=1, source_target_pairs={{0,6},{1,7},{2,4},{3,5},{4,2},{5,3},{6,0},{7,1},{8,14},{9,15},{10,... | collective-permute-start | bytes 1867784 | tf_op jit(solution)/shard_map/ppermute | solution.py:499
  72.6 19.1 %collective-permute-start.14 = (bf16[608,512]{1,0:T(8,128)(2,1)S(1)}, bf16[608,512]{1,0:T(8,128)(2,1)S(1)}, u32[]{:S(2)}, u32[]{:S(2)}) collective-permute-start(bf16[608,512]{1,0:T(8,128)(2,1)S(1)} %get-tuple-element.80), channel_id=1, source_target_pairs={{0,4},{1,5},{2,6},{3,7},{4,0},{5,1},{6,2},{7,3},{8,12},{9,13},{10,... | collective-permute-start | bytes 1867784 | tf_op jit(solution)/shard_map/ppermute | solution.py:499
  91.8 25.4 %collective-permute-start.15 = (bf16[8,256,384]{2,1,0:T(8,128)(2,1)S(1)}, bf16[8,256,384]{2,1,0:T(8,128)(2,1)S(1)}, u32[]{:S(2)}, u32[]{:S(2)}) collective-permute-start(bf16[8,256,384]{2,1,0:T(8,128)(2,1)S(1)} %pad_maximum_fusion), channel_id=1, source_target_pairs={{0,6},{1,7},{2,4},{3,5},{4,2},{5,3},{6,0},{7,1},{8,14},{9,15},{10,... | collective-permute-start | bytes 4718600 | tf_op jit(solution)/shard_map/ppermute | solution.py:499
  96.3 17.4 %copy-start.2 = (f32[1,4,128,128]{3,2,1,0:T(8,128)S(1)}, f32[1,4,128,128]{3,2,1,0:T(8,128)}, u32[]{:S(2)}) copy-start(f32[1,4,128,128]{3,2,1,0:T(8,128)} %param.15) | copy-start | bytes 786436
  96.3 17.4 %copy-start.5 = (f32[1,1,192,192]{3,2,1,0:T(8,128)S(1)}, f32[1,1,192,192]{3,2,1,0:T(8,128)}, u32[]{:S(2)}) copy-start(f32[1,1,192,192]{3,2,1,0:T(8,128)} %param.14) | copy-start | bytes 442372
  96.3 17.4 %copy-start.7 = (s32[1,32]{1,0:T(1,128)S(1)}, s32[1,32]{1,0:T(1,128)}, u32[]{:S(2)}) copy-start(s32[1,32]{1,0:T(1,128)} %refs_0_.3) | copy-start | bytes 388
  96.3 22.4 %collective-permute-start.16 = (bf16[8,256,384]{2,1,0:T(8,128)(2,1)S(1)}, bf16[8,256,384]{2,1,0:T(8,128)(2,1)S(1)}, u32[]{:S(2)}, u32[]{:S(2)}) collective-permute-start(bf16[8,256,384]{2,1,0:T(8,128)(2,1)S(1)} %pad_maximum_fusion.1), channel_id=1, source_target_pairs={{0,2},{1,3},{2,0},{3,1},{4,6},{5,7},{6,4},{7,5},{8,10},{9,11},{10,... | collective-permute-start | bytes 4718600 | tf_op jit(solution)/shard_map/ppermute | solution.py:499
  99.2 14.5 %collective-permute-start.18 = (bf16[2,120,512]{2,1,0:T(8,128)(2,1)S(1)}, bf16[2,120,512]{2,1,0:T(8,128)(2,1)S(1)}, u32[]{:S(2)}, u32[]{:S(2)}) collective-permute-start(bf16[2,120,512]{2,1,0:T(8,128)(2,1)S(1)} %get-tuple-element.88), channel_id=1, source_target_pairs={{0,1},{1,0},{2,3},{3,2},{4,5},{5,4},{6,7},{7,6},{8,9},{9,8},{10,11... | collective-permute-start | bytes 737288 | tf_op jit(solution)/shard_map/ppermute | solution.py:499

commit v4 on v3

--- a/solution.py
+++ b/solution.py
@@ -456,7 +456,7 @@
     )(slots, keep, got, inv_in, inv_out)
 
 
-def passed_block(k_ref, resid_ref, pieces, i, ring):
+def passed_columns(i, ring):
     core, me = my_place()
     rels = [
         sum(bit(i, k) << d for k, d in enumerate(RINGS[c][0]))
@@ -465,34 +465,78 @@
     ]
     owner = me ^ jnp.where(core == 0, rels[0], rels[1])
     x, y = gray(owner >> 3), gray((owner >> 1) & 3)
-    cols = pl.ds(pl.multiple_of((x * NY + y) * PAIR, 128), PAIR)
-    branch = dot(k_ref[BLK:, : KO // 2], pieces[0][i]) + dot(k_ref[BLK:, KO // 2 :], pieces[1][i])
-    return cols, (resid_ref[:, cols].astype(jnp.float32) + branch).astype(jnp.bfloat16)
-
-
-def passed_kernel(held_a, held_b, third_a, third_b, last_a, last_b, k_ref, resid_ref, out_ref):
-    fourth_a, fourth_b, both_a, both_b = last_a.at[:4], last_b.at[:4], last_a.at[4:], last_b.at[4:]
-    groups = ((held_a, held_b), (third_a, fourth_b), (fourth_a, third_b), (both_a, both_b))
-    for ring, pieces in enumerate(groups):
-        for i in range(4):
-            cols, block = passed_block(k_ref, resid_ref, pieces, i, ring)
-            out_ref[:, cols] = block
-
-
-def passed_grad(*parts):
+    return pl.ds(pl.multiple_of((x * NY + y) * PAIR, 128), PAIR)
+
+
+def begin_kernel(held_a, held_b, third_a, third_b, k_ref, resid_ref, out_ref, part):
+    keys_a, keys_b = k_ref[BLK:, : KO // 2], k_ref[BLK:, KO // 2 :]
+    for i in range(4):
+        cols = passed_columns(i, 0)
+        branch = dot(keys_a, held_a[i]) + dot(keys_b, held_b[i])
+        out_ref[:, cols] = (resid_ref[:, cols].astype(jnp.float32) + branch).astype(jnp.bfloat16)
+        part[i] = dot(keys_a, third_a[i])
+        part[4 + i] = dot(keys_b, third_b[i])
+
+
+def passed_begun(*parts):
     vmem = pl.BlockSpec(memory_space=pltpu.VMEM)
     resid = parts[-1]
     return pl.pallas_call(
-        passed_kernel,
-        out_shape=jax.ShapeDtypeStruct(resid.shape, jnp.bfloat16),
-        in_specs=[vmem] * 8,
-        out_specs=vmem,
+        begin_kernel,
+        out_shape=(
+            jax.ShapeDtypeStruct(resid.shape, jnp.bfloat16),
+            jax.ShapeDtypeStruct((8, resid.shape[0], PAIR), jnp.float32),
+        ),
+        in_specs=[vmem] * 6,
+        out_specs=(vmem, vmem),
         compiler_params=pltpu.CompilerParams(vmem_limit_bytes=24 * 2**20),
         cost_estimate=pl.CostEstimate(
-            flops=2 * 256 * 6144 * 512, bytes_accessed=12 * 2**20, transcendentals=0
-        ),
-        name="passed_grad",
+            flops=256 * 6144 * 512, bytes_accessed=8 * 2**20, transcendentals=0
+        ),
+        name="passed_begun",
     )(*parts)
+
+
+def rest_kernel(last_a, last_b, k_ref, resid_ref, part, begun, out_ref, blocks, sems):
+    keys_a, keys_b = k_ref[BLK:, : KO // 2], k_ref[BLK:, KO // 2 :]
+    copies = []
+    for ring in (1, 2, 3):
+        for i in range(4):
+            if ring == 1:
+                branch = part[i] + dot(keys_b, last_b[i])
+            elif ring == 2:
+                branch = dot(keys_a, last_a[i]) + part[4 + i]
+            else:
+                branch = dot(keys_a, last_a[4 + i]) + dot(keys_b, last_b[4 + i])
+            cols = passed_columns(i, ring)
+            at = len(copies)
+            total = resid_ref[:, cols].astype(jnp.float32) + branch
+            blocks[at] = total.astype(jnp.bfloat16)
+            copies.append(pltpu.make_async_copy(blocks.at[at], out_ref.at[:, cols], sems.at[at]))
+            copies[at].start()
+    for copy in copies:
+        copy.wait()
+
+
+def passed_rest(last_a, last_b, key_pre, resid, part, begun):
+    vmem = pl.BlockSpec(memory_space=pltpu.VMEM)
+    hbm = pl.BlockSpec(memory_space=pl.ANY)
+    return pl.pallas_call(
+        rest_kernel,
+        out_shape=jax.ShapeDtypeStruct(resid.shape, jnp.bfloat16),
+        in_specs=[vmem] * 5 + [hbm],
+        out_specs=hbm,
+        input_output_aliases={5: 0},
+        scratch_shapes=[
+            pltpu.VMEM((12, resid.shape[0], PAIR), jnp.bfloat16),
+            pltpu.SemaphoreType.DMA((12,)),
+        ],
+        compiler_params=pltpu.CompilerParams(vmem_limit_bytes=24 * 2**20),
+        cost_estimate=pl.CostEstimate(
+            flops=256 * 6144 * 512, bytes_accessed=8 * 2**20, transcendentals=0
+        ),
+        name="passed_rest",
+    )(last_a, last_b, key_pre, resid, part, begun)
 
 
 def hop(block, route):
@@ -539,7 +583,9 @@
     fourth = [hop(more[s], step_route(WEIGHTS, s, 3)) for s in range(2)]
     keep, send, head_grams = last_sums(total, own, head, *ring)
     last = hop(send, flip_route(((Z,), (Z,))))
-    passed = passed_grad(*held, *third, *fourth, straight, resid)
+    begun, part = passed_begun(*held, *third, straight, resid)
+    last, part = tie(last, part)
+    passed = passed_rest(*fourth, straight, resid, part, begun)
     precond, gram = finished(total, slot_block, keep, last, inv_input[0], inv_head[0])
     return (passed[None], precond[None], gram[None, None], head_grams)
 

time: 124 us -> 122 us (0.984)
  waiting for transfers between devices: 52.7 us -> 49 us
    ppermute x19, waiting for transfers between devices: 52.7 us -> 49 us  [hop(): return lax.ppermute(block, AXES, route)]
    pallas_call x1 -> x2, Pallas kernels: 4.06 us -> 5.04 us  [the longest x1 2.84 us: passed_begun(): pl.pallas_call(begin_kernel, out_shape=(jax.ShapeDtypeStruct(resid.shape,...]
  transfers between devices with their start and end apart: 19 -> 19, of which waited for: 10 -> 10; matrix products, arithmetic and copies ran while one was open for 0% -> 0% of each run, Pallas kernels for 7% -> 10%
where the time goes in v4:
time: 122 us; the launch traced here: 120 us
  waiting for transfers between devices  49 us (40%)
  starting transfers between devices  44.6 us (37%)
  Pallas kernels  20 us (16%)
  local copies, waits for them, and re-layouts  5.08 us (4%)
    ppermute x19, waiting for transfers between devices, hop(): return lax.ppermute(block, AXES, route)  49 us
    ppermute x19, starting transfers between devices, hop(): return lax.ppermute(block, AXES, route)  44.6 us
    pallas_call x2, Pallas kernels, products(): pl.pallas_call(kernel, out_shape=out_shape, in_specs=[smem] + [vmem] * (l...  7.16 us
    unnamed x20, local copies, waits for them, and re-layouts  5.08 us
    pallas_call x1, Pallas kernels, finished(): pl.pallas_call(kernel, out_shape=(jax.ShapeDtypeStruct((1, BLK, KO), jnp....  3.6 us
    pallas_call x1, Pallas kernels, passed_begun(): pl.pallas_call(begin_kernel, out_shape=(jax.ShapeDtypeStruct(resid.shape,...  2.84 us
  transfers between devices with their start and end apart: 19, of which 10 were waited for; matrix products, arithmetic and copies ran while one was open for 0% of the time, Pallas kernels for 10%

profile of v4, /device:TPU:96, one launch (start us, length us, event | category | flops | bytes accessed | tf_op | source)
XLA Modules:
  0.0 120.0 jit_solution(491098495300822918)
XLA Ops:
  0.6 0.9 copy-done.1
  1.6 0.9 copy-done.3
  2.5 0.7 copy-done.6
  3.2 0.7 copy-done.8
  3.8 2.0 %keys.1 = (bf16[256,512]{1,0:T(8,128)(2,1)S(1)}, bf16[512,128]{1,0:T(8,128)(2,1)S(1)}, s32[2,32]{1,0:T(2,128)S(1)}, bf16[448,512]{1,0:T(8,128)(2,1)S(1)}) custom-call(s32[1,32]{1,0:T(1,128)S(1)} %copy-done.6, s32[1,2]{1,0:T(1,128)S(1)} %copy-done.8, bf16[1,256,512]{2,1,0:T(8,128)(2,1)S(1)} %copy-done.1, bf16[1,192,512]{2,1,0:T(8,128)(2,1)S(1)} %copy-done.3), custom_call_target="tpu_custom_call" | custom-call | tf_op jit(solution)/shard_map/keys/pallas_call | solution.py:171
  5.9 0.0 copy-start
  5.9 1.9 %copy-done = bf16[1,256,6144]{2,1,0:T(8,128)(2,1)S(1)} copy-done((bf16[1,256,6144]{2,1,0:T(8,128)(2,1)S(1)}, bf16[1,256,6144]{2,1,0:T(8,128)(2,1)}, u32[]{:S(2)}) %copy-start) | copy-done | bytes 3145752
  7.8 4.0 %sent_products.1 = (bf16[16,120,512]{2,1,0:T(8,128)(2,1)S(1)}, bf16[16,120,512]{2,1,0:T(8,128)(2,1)S(1)}, bf16[6144,256]{1,0:T(8,128)(2,1)S(1)}) custom-call(s32[2,32]{1,0:T(2,128)S(1)} %get-tuple-element.52.order_ref, bf16[1,256,6144]{2,1,0:T(8,128)(2,1)S(1)} %copy-done, bf16[256,512]{1,0:T(8,128)(2,1)S(1)} %get-tuple-element.53.key_ref), custom_call_target="tpu_custom_call" | custom-call | flops 1107296256 | bytes 10485760 | tf_op jit(solution)/shard_map/sent_products/pallas_call | solution.py:241
  11.8 1.6 %collective-permute-start.2 = (bf16[16,120,512]{2,1,0:T(8,128)(2,1)S(1)}, bf16[16,120,512]{2,1,0:T(8,128)(2,1)S(1)}, u32[]{:S(2)}, u32[]{:S(2)}) collective-permute-start(bf16[16,120,512]{2,1,0:T(8,128)(2,1)S(1)} %get-tuple-element.63), channel_id=1, source_target_pairs={{0,8},{1,9},{2,10},{3,11},{4,12},{5,13},{6,14},{7,15},{8,0},{9,1},... | collective-permute-start | bytes 5898248 | tf_op jit(solution)/shard_map/ppermute | solution.py:543
  13.4 2.1 %collective-permute-start.3 = (bf16[16,120,512]{2,1,0:T(8,128)(2,1)S(1)}, bf16[16,120,512]{2,1,0:T(8,128)(2,1)S(1)}, u32[]{:S(2)}, u32[]{:S(2)}) collective-permute-start(bf16[16,120,512]{2,1,0:T(8,128)(2,1)S(1)} %get-tuple-element.68), channel_id=1, source_target_pairs={{0,24},{1,25},{2,26},{3,27},{4,28},{5,29},{6,30},{7,31},{8,16},{9,... | collective-permute-start | bytes 5898248 | tf_op jit(solution)/shard_map/ppermute | solution.py:543
  15.5 1.9 %collective-permute-start.6 = (bf16[448,512]{1,0:T(8,128)(2,1)S(1)}, bf16[448,512]{1,0:T(8,128)(2,1)S(1)}, u32[]{:S(2)}, u32[]{:S(2)}) collective-permute-start(bf16[448,512]{1,0:T(8,128)(2,1)S(1)} %get-tuple-element.71), channel_id=1, source_target_pairs={{32,0},{33,1},{34,2},{35,3},{36,4},{37,5},{38,6},{39,7},{40,8},{41... | collective-permute-start | bytes 1376264 | tf_op jit(solution)/shard_map/ppermute | solution.py:543
  17.4 6.0 %collective-permute-start = (bf16[192,512]{1,0:T(8,128)(2,1)S(1)}, bf16[192,512]{1,0:T(8,128)(2,1)S(1)}, u32[]{:S(2)}, u32[]{:S(2)}) collective-permute-start(bf16[192,512]{1,0:T(8,128)(2,1)S(1)} %bitcast.8), channel_id=1, source_target_pairs={{32,1},{33,0},{34,3},{35,2},{36,5},{37,4},{38,7},{39,6},{40,9},{41... | collective-permute-start | bytes 589832 | tf_op jit(solution)/shard_map/ppermute | solution.py:543
  23.5 0.6 collective-permute-start.1
  24.1 3.1 %kept_products.1 = (f32[8,120,512]{2,1,0:T(8,128)S(1)}, f32[8,120,512]{2,1,0:T(8,128)S(1)}, f32[8,120,512]{2,1,0:T(8,128)S(1)}, f32[8,120,512]{2,1,0:T(8,128)S(1)}) custom-call(s32[2,32]{1,0:T(2,128)S(1)} %get-tuple-element.52.order_ref, bf16[1,256,6144]{2,1,0:T(8,128)(2,1)S(1)} %copy-done, bf16[256,512]{1,0:T(8,128)(2,1)S(1)} %get-tuple-element.53.key_ref, ...), custom_call_target="tpu_custom_call" | custom-call | flops 1107296256 | bytes 10485760 | tf_op jit(solution)/shard_map/kept_products/pallas_call | solution.py:241
  27.2 9.1 %collective-permute-done.1.other = bf16[512,128]{1,0:T(8,128)(2,1)S(1)} collective-permute-done((bf16[512,128]{1,0:T(8,128)(2,1)S(1)}, bf16[512,128]{1,0:T(8,128)(2,1)S(1)}, u32[]{:S(2)}, u32[]{:S(2)}) %collective-permute-start.1) | collective-permute-done | bytes 131104 | tf_op jit(solution)/shard_map/ppermute | solution.py:543
  36.3 4.4 %collective-permute-done.crossed = bf16[192,512]{1,0:T(8,128)(2,1)S(1)} collective-permute-done((bf16[192,512]{1,0:T(8,128)(2,1)S(1)}, bf16[192,512]{1,0:T(8,128)(2,1)S(1)}, u32[]{:S(2)}, u32[]{:S(2)}) %collective-permute-start) | collective-permute-done | bytes 196640 | tf_op jit(solution)/shard_map/ppermute | solution.py:543
  40.7 0.0 collective-permute-done.6.straight.k_ref
  40.7 0.2 weight_pair.1.own
  40.9 0.7 collective-permute-start.7
  41.5 1.1 collective-permute-start.8
  42.7 2.4 %collective-permute-start.9 = (bf16[512,512]{1,0:T(8,128)(2,1)S(1)}, bf16[512,512]{1,0:T(8,128)(2,1)S(1)}, u32[]{:S(2)}, u32[]{:S(2)}) collective-permute-start(bf16[512,512]{1,0:T(8,128)(2,1)S(1)} %weight_pair.1.own), channel_id=1, source_target_pairs={{0,16},{1,17},{2,18},{3,19},{4,20},{5,21},{6,22},{7,23},{8,24},{9,... | collective-permute-start | bytes 1572872 | tf_op jit(solution)/shard_map/ppermute | solution.py:543
  45.1 0.3 halved.1
  45.4 1.7 %collective-permute-start.4 = (bf16[8,120,512]{2,1,0:T(8,128)(2,1)S(1)}, bf16[8,120,512]{2,1,0:T(8,128)(2,1)S(1)}, u32[]{:S(2)}, u32[]{:S(2)}) collective-permute-start(bf16[8,120,512]{2,1,0:T(8,128)(2,1)S(1)} %get-tuple-element.69), channel_id=1, source_target_pairs={{0,24},{1,25},{2,26},{3,27},{4,28},{5,29},{6,30},{7,31},{8,16},{9,... | collective-permute-start | bytes 2949128 | tf_op jit(solution)/shard_map/ppermute | solution.py:543
  47.1 3.0 %collective-permute-done.7.near_a = bf16[512,512]{1,0:T(8,128)(2,1)S(1)} collective-permute-done((bf16[512,512]{1,0:T(8,128)(2,1)S(1)}, bf16[512,512]{1,0:T(8,128)(2,1)S(1)}, u32[]{:S(2)}, u32[]{:S(2)}) %collective-permute-start.7) | collective-permute-done | bytes 524320 | tf_op jit(solution)/shard_map/ppermute | solution.py:543
  50.1 7.4 %collective-permute-done.8.near_b = bf16[512,512]{1,0:T(8,128)(2,1)S(1)} collective-permute-done((bf16[512,512]{1,0:T(8,128)(2,1)S(1)}, bf16[512,512]{1,0:T(8,128)(2,1)S(1)}, u32[]{:S(2)}, u32[]{:S(2)}) %collective-permute-start.8) | collective-permute-done | bytes 524320 | tf_op jit(solution)/shard_map/ppermute | solution.py:543
  57.6 0.2 stacked.1
  57.8 3.5 %collective-permute-start.10 = (bf16[4,256,384]{2,1,0:T(8,128)(2,1)S(1)}, bf16[4,256,384]{2,1,0:T(8,128)(2,1)S(1)}, u32[]{:S(2)}, u32[]{:S(2)}) collective-permute-start(bf16[4,256,384]{2,1,0:T(8,128)(2,1)S(1)} %get-tuple-element.85.held_a), channel_id=1, source_target_pairs={{0,2},{1,3},{2,0},{3,1},{4,6},{5,7},{6,4},{7,5},{8,10},{9,11},{10,... | collective-permute-start | bytes 2359304 | tf_op jit(solution)/shard_map/ppermute | solution.py:543
  61.3 1.9 %collective-permute-start.17 = (bf16[256,6144]{1,0:T(8,128)(2,1)S(1)}, bf16[256,6144]{1,0:T(8,128)(2,1)S(1)}, u32[]{:S(2)}, u32[]{:S(2)}) collective-permute-start(bf16[256,6144]{1,0:T(8,128)(2,1)S(1)} %bitcast.11), channel_id=1, source_target_pairs={{32,0},{33,1},{34,2},{35,3},{36,4},{37,5},{38,6},{39,7},{40,8},{41... | collective-permute-start | bytes 9437192 | tf_op jit(solution)/shard_map/ppermute | solution.py:543
  63.2 4.1 %collective-permute-start.11 = (bf16[4,256,384]{2,1,0:T(8,128)(2,1)S(1)}, bf16[4,256,384]{2,1,0:T(8,128)(2,1)S(1)}, u32[]{:S(2)}, u32[]{:S(2)}) collective-permute-start(bf16[4,256,384]{2,1,0:T(8,128)(2,1)S(1)} %get-tuple-element.87.held_b), channel_id=1, source_target_pairs={{0,6},{1,7},{2,4},{3,5},{4,2},{5,3},{6,0},{7,1},{8,14},{9,15},{10,... | collective-permute-start | bytes 2359304 | tf_op jit(solution)/shard_map/ppermute | solution.py:543
  67.3 0.8 collective-permute-done.4.got_a
  68.1 0.6 ring_sums.1
  68.7 1.7 %collective-permute-start.12 = (bf16[608,512]{1,0:T(8,128)(2,1)S(1)}, bf16[608,512]{1,0:T(8,128)(2,1)S(1)}, u32[]{:S(2)}, u32[]{:S(2)}) collective-permute-start(bf16[608,512]{1,0:T(8,128)(2,1)S(1)} %get-tuple-element.82), channel_id=1, source_target_pairs={{0,2},{1,3},{2,0},{3,1},{4,6},{5,7},{6,4},{7,5},{8,10},{9,11},{10,... | collective-permute-start | bytes 1867784 | tf_op jit(solution)/shard_map/ppermute | solution.py:543
  70.4 2.2 %collective-permute-start.13 = (bf16[608,512]{1,0:T(8,128)(2,1)S(1)}, bf16[608,512]{1,0:T(8,128)(2,1)S(1)}, u32[]{:S(2)}, u32[]{:S(2)}) collective-permute-start(bf16[608,512]{1,0:T(8,128)(2,1)S(1)} %get-tuple-element.83), channel_id=1, source_target_pairs={{0,6},{1,7},{2,4},{3,5},{4,2},{5,3},{6,0},{7,1},{8,14},{9,15},{10,... | collective-permute-start | bytes 1867784 | tf_op jit(solution)/shard_map/ppermute | solution.py:543
  72.6 2.3 %collective-permute-start.14 = (bf16[608,512]{1,0:T(8,128)(2,1)S(1)}, bf16[608,512]{1,0:T(8,128)(2,1)S(1)}, u32[]{:S(2)}, u32[]{:S(2)}) collective-permute-start(bf16[608,512]{1,0:T(8,128)(2,1)S(1)} %get-tuple-element.84), channel_id=1, source_target_pairs={{0,4},{1,5},{2,6},{3,7},{4,0},{5,1},{6,2},{7,3},{8,12},{9,13},{10,... | collective-permute-start | bytes 1867784 | tf_op jit(solution)/shard_map/ppermute | solution.py:543
  74.8 3.4 %collective-permute-done.11.third_b = bf16[4,256,384]{2,1,0:T(8,128)(2,1)S(1)} collective-permute-done((bf16[4,256,384]{2,1,0:T(8,128)(2,1)S(1)}, bf16[4,256,384]{2,1,0:T(8,128)(2,1)S(1)}, u32[]{:S(2)}, u32[]{:S(2)}) %collective-permute-start.11) | collective-permute-done | bytes 786464 | tf_op jit(solution)/shard_map/ppermute | solution.py:543
  78.3 0.7 collective-permute-done.12.refs_2_
  79.0 12.6 %collective-permute-done.13.refs_3_ = bf16[608,512]{1,0:T(8,128)(2,1)S(1)} collective-permute-done((bf16[608,512]{1,0:T(8,128)(2,1)S(1)}, bf16[608,512]{1,0:T(8,128)(2,1)S(1)}, u32[]{:S(2)}, u32[]{:S(2)}) %collective-permute-start.13) | collective-permute-done | bytes 622624 | tf_op jit(solution)/shard_map/ppermute | solution.py:543
  91.6 0.2 pad_maximum_fusion.1
  91.8 2.1 %collective-permute-start.16 = (bf16[8,256,384]{2,1,0:T(8,128)(2,1)S(1)}, bf16[8,256,384]{2,1,0:T(8,128)(2,1)S(1)}, u32[]{:S(2)}, u32[]{:S(2)}) collective-permute-start(bf16[8,256,384]{2,1,0:T(8,128)(2,1)S(1)} %pad_maximum_fusion.1), channel_id=1, source_target_pairs={{0,2},{1,3},{2,0},{3,1},{4,6},{5,7},{6,4},{7,5},{8,10},{9,11},{10,... | collective-permute-start | bytes 4718600 | tf_op jit(solution)/shard_map/ppermute | solution.py:543
  93.9 0.2 pad_maximum_fusion
  94.1 4.1 %collective-permute-start.15 = (bf16[8,256,384]{2,1,0:T(8,128)(2,1)S(1)}, bf16[8,256,384]{2,1,0:T(8,128)(2,1)S(1)}, u32[]{:S(2)}, u32[]{:S(2)}) collective-permute-start(bf16[8,256,384]{2,1,0:T(8,128)(2,1)S(1)} %pad_maximum_fusion), channel_id=1, source_target_pairs={{0,6},{1,7},{2,4},{3,5},{4,2},{5,3},{6,0},{7,1},{8,14},{9,15},{10,... | collective-permute-start | bytes 4718600 | tf_op jit(solution)/shard_map/ppermute | solution.py:543
  98.3 0.8 last_sums.1
  99.1 4.6 %collective-permute-start.18 = (bf16[2,120,512]{2,1,0:T(8,128)(2,1)S(1)}, bf16[2,120,512]{2,1,0:T(8,128)(2,1)S(1)}, u32[]{:S(2)}, u32[]{:S(2)}) collective-permute-start(bf16[2,120,512]{2,1,0:T(8,128)(2,1)S(1)} %get-tuple-element.91), channel_id=1, source_target_pairs={{0,1},{1,0},{2,3},{3,2},{4,5},{5,4},{6,7},{7,6},{8,9},{9,8},{10,11... | collective-permute-start | bytes 737288 | tf_op jit(solution)/shard_map/ppermute | solution.py:543
  103.7 2.8 %passed_begun.1 = (bf16[256,6144]{1,0:T(8,128)(2,1)}, f32[8,256,384]{2,1,0:T(8,128)S(1)}) custom-call(bf16[4,256,384]{2,1,0:T(8,128)(2,1)S(1)} %get-tuple-element.85.held_a, bf16[4,256,384]{2,1,0:T(8,128)(2,1)S(1)} %get-tuple-element.87.held_b, bf16[4,256,384]{2,1,0:T(8,128)(2,1)S(1)} %collective-permute-done.10.third_a, ...), custom_call_target="tpu_custom_call" | custom-call | flops 805306368 | bytes 8388608 | tf_op jit(solution)/shard_map/passed_begun/pallas_call | solution.py:484
  106.5 7.2 %collective-permute-done.18.refs_2_ = bf16[2,120,512]{2,1,0:T(8,128)(2,1)S(1)} collective-permute-done((bf16[2,120,512]{2,1,0:T(8,128)(2,1)S(1)}, bf16[2,120,512]{2,1,0:T(8,128)(2,1)S(1)}, u32[]{:S(2)}, u32[]{:S(2)}) %collective-permute-start.18) | collective-permute-done | bytes 245792 | tf_op jit(solution)/shard_map/ppermute | solution.py:543
  113.7 3.6 %finish.1 = (f32[1,192,512]{2,1,0:T(8,128)}, f32[192,192]{1,0:T(8,128)}) custom-call(s32[1,32]{1,0:T(1,128)S(1)} %copy-done.7, f32[2,120,512]{2,1,0:T(8,128)S(1)} %get-tuple-element.95.refs_1_, bf16[2,120,512]{2,1,0:T(8,128)(2,1)S(1)} %collective-permute-done.18.refs_2_, f32[1,192,192]{2,1,0:T(8,128)S(1)} %bitcast.9, f32[4,128,128]{2,1,0:T(8,128)S(1)} %bitcast.7), custom_call_target="tpu_custom_call" | custom-call | tf_op jit(solution)/shard_map/finish/pallas_call | solution.py:446
  117.3 0.4 collective-permute-done.15.last_a
  117.6 2.2 %passed_rest.1 = bf16[256,6144]{1,0:T(8,128)(2,1)} custom-call(bf16[8,256,384]{2,1,0:T(8,128)(2,1)S(1)} %collective-permute-done.15.last_a, bf16[8,256,384]{2,1,0:T(8,128)(2,1)S(1)} %collective-permute-done.16.last_b, bf16[448,512]{1,0:T(8,128)(2,1)S(1)} %collective-permute-done.6.straight.k_ref, ...), custom_call_target="tpu_custom_call", output_to_operand_aliasing={{}: (5, {})} | custom-call | flops 805306368 | bytes 8388608 | tf_op jit(solution)/shard_map/passed_rest/pallas_call | solution.py:524
  (23 shorter events, 0.0 us)
Async XLA Ops:
  0.6 1.0 copy-start.1
  1.6 0.9 copy-start.3
  2.5 0.7 copy-start.6
  3.2 0.7 copy-start.8
  5.9 1.9 %copy-start = (bf16[1,256,6144]{2,1,0:T(8,128)(2,1)S(1)}, bf16[1,256,6144]{2,1,0:T(8,128)(2,1)}, u32[]{:S(2)}) copy-start(bf16[1,256,6144]{2,1,0:T(8,128)(2,1)} %x_ref.3) | copy-start | bytes 9437188
  7.8 9.6 %copy-start.4 = (bf16[1,192,512]{2,1,0:T(8,128)(2,1)S(1)}, bf16[1,192,512]{2,1,0:T(8,128)(2,1)}, u32[]{:S(2)}) copy-start(bf16[1,192,512]{2,1,0:T(8,128)(2,1)} %refs_3_.1) | copy-start | bytes 589828
  11.8 33.3 %collective-permute-start.2 = (bf16[16,120,512]{2,1,0:T(8,128)(2,1)S(1)}, bf16[16,120,512]{2,1,0:T(8,128)(2,1)S(1)}, u32[]{:S(2)}, u32[]{:S(2)}) collective-permute-start(bf16[16,120,512]{2,1,0:T(8,128)(2,1)S(1)} %get-tuple-element.63), channel_id=1, source_target_pairs={{0,8},{1,9},{2,10},{3,11},{4,12},{5,13},{6,14},{7,15},{8,0},{9,1},... | collective-permute-start | bytes 5898248 | tf_op jit(solution)/shard_map/ppermute | solution.py:543
  13.4 31.7 %collective-permute-start.3 = (bf16[16,120,512]{2,1,0:T(8,128)(2,1)S(1)}, bf16[16,120,512]{2,1,0:T(8,128)(2,1)S(1)}, u32[]{:S(2)}, u32[]{:S(2)}) collective-permute-start(bf16[16,120,512]{2,1,0:T(8,128)(2,1)S(1)} %get-tuple-element.68), channel_id=1, source_target_pairs={{0,24},{1,25},{2,26},{3,27},{4,28},{5,29},{6,30},{7,31},{8,16},{9,... | collective-permute-start | bytes 5898248 | tf_op jit(solution)/shard_map/ppermute | solution.py:543
  15.5 25.2 %collective-permute-start.6 = (bf16[448,512]{1,0:T(8,128)(2,1)S(1)}, bf16[448,512]{1,0:T(8,128)(2,1)S(1)}, u32[]{:S(2)}, u32[]{:S(2)}) collective-permute-start(bf16[448,512]{1,0:T(8,128)(2,1)S(1)} %get-tuple-element.71), channel_id=1, source_target_pairs={{32,0},{33,1},{34,2},{35,3},{36,4},{37,5},{38,6},{39,7},{40,8},{41... | collective-permute-start | bytes 1376264 | tf_op jit(solution)/shard_map/ppermute | solution.py:543
  17.4 23.3 %collective-permute-start = (bf16[192,512]{1,0:T(8,128)(2,1)S(1)}, bf16[192,512]{1,0:T(8,128)(2,1)S(1)}, u32[]{:S(2)}, u32[]{:S(2)}) collective-permute-start(bf16[192,512]{1,0:T(8,128)(2,1)S(1)} %bitcast.8), channel_id=1, source_target_pairs={{32,1},{33,0},{34,3},{35,2},{36,5},{37,4},{38,7},{39,6},{40,9},{41... | collective-permute-start | bytes 589832 | tf_op jit(solution)/shard_map/ppermute | solution.py:543
  23.5 12.8 %collective-permute-start.1 = (bf16[512,128]{1,0:T(8,128)(2,1)S(1)}, bf16[512,128]{1,0:T(8,128)(2,1)S(1)}, u32[]{:S(2)}, u32[]{:S(2)}) collective-permute-start(bf16[512,128]{1,0:T(8,128)(2,1)S(1)} %get-tuple-element.58.head), channel_id=1, source_target_pairs={{0,1},{1,0},{2,3},{3,2},{4,5},{5,4},{6,7},{7,6},{8,9},{9,8},{10,11... | collective-permute-start | bytes 393224 | tf_op jit(solution)/shard_map/ppermute | solution.py:543
  40.9 9.3 %collective-permute-start.7 = (bf16[512,512]{1,0:T(8,128)(2,1)S(1)}, bf16[512,512]{1,0:T(8,128)(2,1)S(1)}, u32[]{:S(2)}, u32[]{:S(2)}) collective-permute-start(bf16[512,512]{1,0:T(8,128)(2,1)S(1)} %weight_pair.1.own), channel_id=1, source_target_pairs={{0,8},{1,9},{2,10},{3,11},{4,12},{5,13},{6,14},{7,15},{8,0},{9,1},... | collective-permute-start | bytes 1572872 | tf_op jit(solution)/shard_map/ppermute | solution.py:543
  41.5 16.0 %collective-permute-start.8 = (bf16[512,512]{1,0:T(8,128)(2,1)S(1)}, bf16[512,512]{1,0:T(8,128)(2,1)S(1)}, u32[]{:S(2)}, u32[]{:S(2)}) collective-permute-start(bf16[512,512]{1,0:T(8,128)(2,1)S(1)} %weight_pair.1.own), channel_id=1, source_target_pairs={{0,24},{1,25},{2,26},{3,27},{4,28},{5,29},{6,30},{7,31},{8,16},{9,... | collective-permute-start | bytes 1572872 | tf_op jit(solution)/shard_map/ppermute | solution.py:543
  42.7 14.9 %collective-permute-start.9 = (bf16[512,512]{1,0:T(8,128)(2,1)S(1)}, bf16[512,512]{1,0:T(8,128)(2,1)S(1)}, u32[]{:S(2)}, u32[]{:S(2)}) collective-permute-start(bf16[512,512]{1,0:T(8,128)(2,1)S(1)} %weight_pair.1.own), channel_id=1, source_target_pairs={{0,16},{1,17},{2,18},{3,19},{4,20},{5,21},{6,22},{7,23},{8,24},{9,... | collective-permute-start | bytes 1572872 | tf_op jit(solution)/shard_map/ppermute | solution.py:543
  45.1 16.2 %copy-start.9 = (bf16[1,256,6144]{2,1,0:T(8,128)(2,1)S(1)}, bf16[1,256,6144]{2,1,0:T(8,128)(2,1)}, u32[]{:S(2)}) copy-start(bf16[1,256,6144]{2,1,0:T(8,128)(2,1)} %param.9) | copy-start | bytes 9437188
  45.4 22.7 %collective-permute-start.4 = (bf16[8,120,512]{2,1,0:T(8,128)(2,1)S(1)}, bf16[8,120,512]{2,1,0:T(8,128)(2,1)S(1)}, u32[]{:S(2)}, u32[]{:S(2)}) collective-permute-start(bf16[8,120,512]{2,1,0:T(8,128)(2,1)S(1)} %get-tuple-element.69), channel_id=1, source_target_pairs={{0,24},{1,25},{2,26},{3,27},{4,28},{5,29},{6,30},{7,31},{8,16},{9,... | collective-permute-start | bytes 2949128 | tf_op jit(solution)/shard_map/ppermute | solution.py:543
  47.1 21.0 %collective-permute-start.5 = (bf16[8,120,512]{2,1,0:T(8,128)(2,1)S(1)}, bf16[8,120,512]{2,1,0:T(8,128)(2,1)S(1)}, u32[]{:S(2)}, u32[]{:S(2)}) collective-permute-start(bf16[8,120,512]{2,1,0:T(8,128)(2,1)S(1)} %get-tuple-element.70), channel_id=1, source_target_pairs={{0,8},{1,9},{2,10},{3,11},{4,12},{5,13},{6,14},{7,15},{8,0},{9,1},... | collective-permute-start | bytes 2949128 | tf_op jit(solution)/shard_map/ppermute | solution.py:543
  57.8 14.8 %collective-permute-start.10 = (bf16[4,256,384]{2,1,0:T(8,128)(2,1)S(1)}, bf16[4,256,384]{2,1,0:T(8,128)(2,1)S(1)}, u32[]{:S(2)}, u32[]{:S(2)}) collective-permute-start(bf16[4,256,384]{2,1,0:T(8,128)(2,1)S(1)} %get-tuple-element.85.held_a), channel_id=1, source_target_pairs={{0,2},{1,3},{2,0},{3,1},{4,6},{5,7},{6,4},{7,5},{8,10},{9,11},{10,... | collective-permute-start | bytes 2359304 | tf_op jit(solution)/shard_map/ppermute | solution.py:543
  61.3 42.4 %collective-permute-start.17 = (bf16[256,6144]{1,0:T(8,128)(2,1)S(1)}, bf16[256,6144]{1,0:T(8,128)(2,1)S(1)}, u32[]{:S(2)}, u32[]{:S(2)}) collective-permute-start(bf16[256,6144]{1,0:T(8,128)(2,1)S(1)} %bitcast.11), channel_id=1, source_target_pairs={{32,0},{33,1},{34,2},{35,3},{36,4},{37,5},{38,6},{39,7},{40,8},{41... | collective-permute-start | bytes 9437192 | tf_op jit(solution)/shard_map/ppermute | solution.py:543
  63.2 15.1 %collective-permute-start.11 = (bf16[4,256,384]{2,1,0:T(8,128)(2,1)S(1)}, bf16[4,256,384]{2,1,0:T(8,128)(2,1)S(1)}, u32[]{:S(2)}, u32[]{:S(2)}) collective-permute-start(bf16[4,256,384]{2,1,0:T(8,128)(2,1)S(1)} %get-tuple-element.87.held_b), channel_id=1, source_target_pairs={{0,6},{1,7},{2,4},{3,5},{4,2},{5,3},{6,0},{7,1},{8,14},{9,15},{10,... | collective-permute-start | bytes 2359304 | tf_op jit(solution)/shard_map/ppermute | solution.py:543
  68.7 10.3 %collective-permute-start.12 = (bf16[608,512]{1,0:T(8,128)(2,1)S(1)}, bf16[608,512]{1,0:T(8,128)(2,1)S(1)}, u32[]{:S(2)}, u32[]{:S(2)}) collective-permute-start(bf16[608,512]{1,0:T(8,128)(2,1)S(1)} %get-tuple-element.82), channel_id=1, source_target_pairs={{0,2},{1,3},{2,0},{3,1},{4,6},{5,7},{6,4},{7,5},{8,10},{9,11},{10,... | collective-permute-start | bytes 1867784 | tf_op jit(solution)/shard_map/ppermute | solution.py:543
  70.4 21.2 %collective-permute-start.13 = (bf16[608,512]{1,0:T(8,128)(2,1)S(1)}, bf16[608,512]{1,0:T(8,128)(2,1)S(1)}, u32[]{:S(2)}, u32[]{:S(2)}) collective-permute-start(bf16[608,512]{1,0:T(8,128)(2,1)S(1)} %get-tuple-element.83), channel_id=1, source_target_pairs={{0,6},{1,7},{2,4},{3,5},{4,2},{5,3},{6,0},{7,1},{8,14},{9,15},{10,... | collective-permute-start | bytes 1867784 | tf_op jit(solution)/shard_map/ppermute | solution.py:543
  72.6 19.1 %collective-permute-start.14 = (bf16[608,512]{1,0:T(8,128)(2,1)S(1)}, bf16[608,512]{1,0:T(8,128)(2,1)S(1)}, u32[]{:S(2)}, u32[]{:S(2)}) collective-permute-start(bf16[608,512]{1,0:T(8,128)(2,1)S(1)} %get-tuple-element.84), channel_id=1, source_target_pairs={{0,4},{1,5},{2,6},{3,7},{4,0},{5,1},{6,2},{7,3},{8,12},{9,13},{10,... | collective-permute-start | bytes 1867784 | tf_op jit(solution)/shard_map/ppermute | solution.py:543
  91.8 25.4 %collective-permute-start.16 = (bf16[8,256,384]{2,1,0:T(8,128)(2,1)S(1)}, bf16[8,256,384]{2,1,0:T(8,128)(2,1)S(1)}, u32[]{:S(2)}, u32[]{:S(2)}) collective-permute-start(bf16[8,256,384]{2,1,0:T(8,128)(2,1)S(1)} %pad_maximum_fusion.1), channel_id=1, source_target_pairs={{0,2},{1,3},{2,0},{3,1},{4,6},{5,7},{6,4},{7,5},{8,10},{9,11},{10,... | collective-permute-start | bytes 4718600 | tf_op jit(solution)/shard_map/ppermute | solution.py:543
  94.1 23.5 %collective-permute-start.15 = (bf16[8,256,384]{2,1,0:T(8,128)(2,1)S(1)}, bf16[8,256,384]{2,1,0:T(8,128)(2,1)S(1)}, u32[]{:S(2)}, u32[]{:S(2)}) collective-permute-start(bf16[8,256,384]{2,1,0:T(8,128)(2,1)S(1)} %pad_maximum_fusion), channel_id=1, source_target_pairs={{0,6},{1,7},{2,4},{3,5},{4,2},{5,3},{6,0},{7,1},{8,14},{9,15},{10,... | collective-permute-start | bytes 4718600 | tf_op jit(solution)/shard_map/ppermute | solution.py:543
  99.1 14.6 %copy-start.2 = (f32[1,4,128,128]{3,2,1,0:T(8,128)S(1)}, f32[1,4,128,128]{3,2,1,0:T(8,128)}, u32[]{:S(2)}) copy-start(f32[1,4,128,128]{3,2,1,0:T(8,128)} %param.15) | copy-start | bytes 786436
  99.1 14.6 %copy-start.5 = (f32[1,1,192,192]{3,2,1,0:T(8,128)S(1)}, f32[1,1,192,192]{3,2,1,0:T(8,128)}, u32[]{:S(2)}) copy-start(f32[1,1,192,192]{3,2,1,0:T(8,128)} %param.14) | copy-start | bytes 442372
  99.1 14.6 %copy-start.7 = (s32[1,32]{1,0:T(1,128)S(1)}, s32[1,32]{1,0:T(1,128)}, u32[]{:S(2)}) copy-start(s32[1,32]{1,0:T(1,128)} %refs_0_.3) | copy-start | bytes 388
  99.1 14.6 %collective-permute-start.18 = (bf16[2,120,512]{2,1,0:T(8,128)(2,1)S(1)}, bf16[2,120,512]{2,1,0:T(8,128)(2,1)S(1)}, u32[]{:S(2)}, u32[]{:S(2)}) collective-permute-start(bf16[2,120,512]{2,1,0:T(8,128)(2,1)S(1)} %get-tuple-element.91), channel_id=1, source_target_pairs={{0,1},{1,0},{2,3},{3,2},{4,5},{5,4},{6,7},{7,6},{8,9},{9,8},{10,11... | collective-permute-start | bytes 737288 | tf_op jit(solution)/shard_map/ppermute | solution.py:543
